TPU v7x, 32 devices: a whole 2x2x4 slice. The times are simulated.
32 devices in a mesh: page: 8 (over z, y), seq: 4 (over x, core).
Axes of the slice: x: 2, y: 2, z: 4, core: 2. Of those that a mesh axis runs over, the one named last changes fastest.
Arguments:
- tokens: float32 [8, 512, 1024], P('page', 'seq'), may hold values from -6 to 6
- valid_len: int32 [8], P('page'), may hold values from 128 to 512, as said below
- query_weight: float32 [1024, 1024], P(('page', 'seq')), may hold values from -0.1875 to 0.1875
- query_bias: float32 [1024], P(('page', 'seq')), may hold values from -3 to 3
- key_weight: float32 [1024, 1024], P(('page', 'seq')), may hold values from -0.1875 to 0.1875
- value_weight: float32 [1024, 1024], P(('page', 'seq')), may hold values from -0.1875 to 0.1875
- value_bias: float32 [1024], P(('page', 'seq')), may hold values from -3 to 3
- output_weight: float32 [1024, 1024], P(('page', 'seq')), may hold values from -0.75 to 0.75
- output_bias: float32 [1024], P(('page', 'seq')), may hold values from -3 to 3
- attn_gain: float32 [1024], P(('page', 'seq')), may hold values from 0.25 to 1.75
- attn_shift: float32 [1024], P(('page', 'seq')), may hold values from -3 to 3
- inner_weight: float32 [1024, 4096], P(('page', 'seq')), may hold values from -0.1875 to 0.1875
- inner_bias: float32 [4096], P(('page', 'seq')), may hold values from -3 to 3
- outer_weight: float32 [4096, 1024], P(('page', 'seq')), may hold values from -0.09375 to 0.09375
- outer_bias: float32 [1024], P(('page', 'seq')), may hold values from -3 to 3
- final_gain: float32 [1024], P(('page', 'seq')), may hold values from 0.25 to 1.75
- final_shift: float32 [1024], P(('page', 'seq')), may hold values from -3 to 3
- out_grad: float32 [8, 512, 1024], P('page', 'seq'), may hold values from -6 to 6
Outputs:
- layer_out: float32 [8, 512, 1024], P('page', 'seq')
- input_grad: float32 [8, 512, 1024], P('page', 'seq')
- query_weight_grad: float32 [1024, 1024], P(('page', 'seq'))
- query_bias_grad: float32 [1024], P(('page', 'seq'))
- key_weight_grad: float32 [1024, 1024], P(('page', 'seq'))
- value_weight_grad: float32 [1024, 1024], P(('page', 'seq'))
- value_bias_grad: float32 [1024], P(('page', 'seq'))
- output_weight_grad: float32 [1024, 1024], P(('page', 'seq'))
- output_bias_grad: float32 [1024], P(('page', 'seq'))
- attn_gain_grad: float32 [1024], P(('page', 'seq'))
- attn_shift_grad: float32 [1024], P(('page', 'seq'))
- inner_weight_grad: float32 [1024, 4096], P(('page', 'seq'))
- inner_bias_grad: float32 [4096], P(('page', 'seq'))
- outer_weight_grad: float32 [4096, 1024], P(('page', 'seq'))
- outer_bias_grad: float32 [1024], P(('page', 'seq'))
- final_gain_grad: float32 [1024], P(('page', 'seq'))
- final_shift_grad: float32 [1024], P(('page', 'seq'))
Inputs may be any that keep to these rules, and one draw needn't show every extreme that they name: `valid_len`: keys at or beyond a page's valid length are padding; some page is full and some page has only 128 valid tokens.
All inputs are finite; a program needn't handle non-finite values.
Results may differ from a plain program's by a relative error of at most 0.015.
The roundings to bfloat16 on the way count: a program that leaves them out, or rounds other values in their place, can miss the bound.
Values may be sent and summed in bfloat16 or wider, within the bound.
A program may use at most 192 MiB of HBM per device.

v0:
```python
import math

import jax
import jax.numpy as jnp
from jax import lax
from jax.sharding import PartitionSpec as P

HEAD_DIM = 64


EPSILON = 1e-05
INV_ROOT_TWO = 1.0 / math.sqrt(2.0)
INV_ROOT_TWO_PI = 1.0 / math.sqrt(2.0 * math.pi)


def product(left, right):
    return jnp.dot(left, right, preferred_element_type=jnp.float32)


def product_tn(left, right):
    return lax.dot_general(
        left, right, (((0,), (0,)), ((), ())), preferred_element_type=jnp.float32
    )


def product_nt(left, right):
    return lax.dot_general(
        left, right, (((1,), (1,)), ((), ())), preferred_element_type=jnp.float32
    )


def norm_parts(values):
    center = values - jnp.mean(values, axis=-1, keepdims=True)
    inverse = lax.rsqrt(jnp.mean(center * center, axis=-1, keepdims=True) + EPSILON)
    return (center * inverse, inverse)


def norm_backward(grad_out, normed, inverse, gain):
    scaled = grad_out * gain
    return inverse * (
        scaled
        - jnp.mean(scaled, axis=-1, keepdims=True)
        - normed * jnp.mean(scaled * normed, axis=-1, keepdims=True)
    )


def gelu_parts(values):
    cumulative = 0.5 * (1.0 + lax.erf(values * INV_ROOT_TWO))
    return (
        values * cumulative,
        cumulative + values * jnp.exp(-0.5 * values * values) * INV_ROOT_TWO_PI,
    )


def sequence_layer(tokens, valid_len, lowered, out_grad):
    fetched = (
        lax.all_gather(lowered[0], ("page", "seq"), axis=0, tiled=True),
        lax.all_gather(lowered[1], ("page", "seq"), axis=0, tiled=True),
        lax.all_gather(lowered[2], ("page", "seq"), axis=0, tiled=True),
        lax.all_gather(lowered[3], ("page", "seq"), axis=0, tiled=True),
        lax.all_gather(lowered[4], ("page", "seq"), axis=0, tiled=True),
        lax.all_gather(lowered[5], ("page", "seq"), axis=0, tiled=True),
        lax.all_gather(lowered[6], ("page", "seq"), axis=0, tiled=True),
        lax.all_gather(lowered[7], ("page", "seq"), axis=0, tiled=True),
        lax.all_gather(lowered[8], ("page", "seq"), axis=0, tiled=True),
        lax.all_gather(lowered[9], ("page", "seq"), axis=0, tiled=True),
        lax.all_gather(lowered[10], ("page", "seq"), axis=0, tiled=True),
        lax.all_gather(lowered[11], ("page", "seq"), axis=0, tiled=True),
        lax.all_gather(lowered[12], ("page", "seq"), axis=0, tiled=True),
        lax.all_gather(lowered[13], ("page", "seq"), axis=0, tiled=True),
        lax.all_gather(lowered[14], ("page", "seq"), axis=0, tiled=True),
    )
    (
        w_query,
        b_query,
        w_key,
        w_value,
        b_value,
        w_out,
        b_out,
        g_attn,
        s_attn,
        w_inner,
        b_inner,
        w_outer,
        b_outer,
        g_final,
        s_final,
    ) = fetched
    f32 = jnp.float32
    bf16 = jnp.bfloat16
    scale = HEAD_DIM ** (-0.5)
    page_count, span_len, width = tokens.shape
    heads = width // HEAD_DIM
    row_count = page_count * span_len
    tok_rows = tokens.reshape(row_count, width)
    tok_low = tok_rows.astype(bf16)
    q_low = (product(tok_low, w_query) + b_query.astype(f32)).astype(bf16)
    k_low = product(tok_low, w_key).astype(bf16)
    v_low = (product(tok_low, w_value) + b_value.astype(f32)).astype(bf16)
    k_full, v_full = (
        lax.all_gather(k_low.reshape(page_count, span_len, width), "seq", axis=1, tiled=True),
        lax.all_gather(v_low.reshape(page_count, span_len, width), "seq", axis=1, tiled=True),
    )
    seq_len = k_full.shape[1]
    q_heads = q_low.reshape(page_count, span_len, heads, HEAD_DIM)
    k_heads = k_full.reshape(page_count, seq_len, heads, HEAD_DIM)
    v_heads = v_full.reshape(page_count, seq_len, heads, HEAD_DIM)
    key_mask = (lax.broadcasted_iota(jnp.int32, (page_count, seq_len), 1) < valid_len[:, None])[
        :, None, None, :
    ]

    def masked_scores():
        raw = jnp.einsum("pqhe,pkhe->phqk", q_heads, k_heads, preferred_element_type=f32) * scale
        return jnp.where(key_mask, raw, -1000000000.0)

    scores = masked_scores()
    top_score = jnp.max(scores, axis=-1, keepdims=True)
    log_total = top_score + jnp.log(jnp.sum(jnp.exp(scores - top_score), axis=-1, keepdims=True))
    probs_low = jnp.exp(scores - log_total).astype(bf16)
    context = jnp.einsum("phqk,pkhe->pqhe", probs_low, v_heads, preferred_element_type=f32)
    ctx_low = context.reshape(row_count, width).astype(bf16)
    attended = product(ctx_low, w_out) + b_out.astype(f32)
    norm_one, inv_one = norm_parts(tok_rows + attended)
    hidden = norm_one * g_attn.astype(f32) + s_attn.astype(f32)
    hid_low = hidden.astype(bf16)
    inner = product(hid_low, w_inner) + b_inner.astype(f32)
    active, slope = gelu_parts(inner)
    act_low = active.astype(bf16)
    outer = product(act_low, w_outer) + b_outer.astype(f32)
    norm_two, inv_two = norm_parts(hidden + outer)
    result = norm_two * g_final.astype(f32) + s_final.astype(f32)
    (
        w_query,
        b_query,
        w_key,
        w_value,
        b_value,
        w_out,
        b_out,
        g_attn,
        s_attn,
        w_inner,
        b_inner,
        w_outer,
        b_outer,
        g_final,
        s_final,
    ) = (
        lax.all_gather(lowered[0], ("page", "seq"), axis=0, tiled=True),
        lax.all_gather(lowered[1], ("page", "seq"), axis=0, tiled=True),
        lax.all_gather(lowered[2], ("page", "seq"), axis=0, tiled=True),
        lax.all_gather(lowered[3], ("page", "seq"), axis=0, tiled=True),
        lax.all_gather(lowered[4], ("page", "seq"), axis=0, tiled=True),
        lax.all_gather(lowered[5], ("page", "seq"), axis=0, tiled=True),
        lax.all_gather(lowered[6], ("page", "seq"), axis=0, tiled=True),
        lax.all_gather(lowered[7], ("page", "seq"), axis=0, tiled=True),
        lax.all_gather(lowered[8], ("page", "seq"), axis=0, tiled=True),
        lax.all_gather(lowered[9], ("page", "seq"), axis=0, tiled=True),
        lax.all_gather(lowered[10], ("page", "seq"), axis=0, tiled=True),
        lax.all_gather(lowered[11], ("page", "seq"), axis=0, tiled=True),
        lax.all_gather(lowered[12], ("page", "seq"), axis=0, tiled=True),
        lax.all_gather(lowered[13], ("page", "seq"), axis=0, tiled=True),
        lax.all_gather(lowered[14], ("page", "seq"), axis=0, tiled=True),
    )
    grad_rows = out_grad.reshape(row_count, width)
    grad_gfinal = jnp.sum(grad_rows * norm_two, axis=0)
    grad_sfinal = jnp.sum(grad_rows, axis=0)
    grad_sum = norm_backward(grad_rows, norm_two, inv_two, g_final.astype(f32))
    grad_f_low = grad_sum.astype(bf16)
    grad_bouter = jnp.sum(grad_f_low.astype(f32), axis=0)
    grad_wouter = product_tn(act_low, grad_f_low)
    grad_active = product_nt(grad_f_low, w_outer)
    grad_in_low = (grad_active * slope).astype(bf16)
    grad_binner = jnp.sum(grad_in_low.astype(f32), axis=0)
    grad_winner = product_tn(hid_low, grad_in_low)
    grad_hidden = grad_sum + product_nt(grad_in_low, w_inner)
    grad_gattn = jnp.sum(grad_hidden * norm_one, axis=0)
    grad_sattn = jnp.sum(grad_hidden, axis=0)
    grad_mixed = norm_backward(grad_hidden, norm_one, inv_one, g_attn.astype(f32))
    grad_att_low = grad_mixed.astype(bf16)
    grad_bout = jnp.sum(grad_att_low.astype(f32), axis=0)
    grad_wout = product_tn(ctx_low, grad_att_low)
    grad_ctx = (
        product_nt(grad_att_low, w_out).astype(bf16).reshape(page_count, span_len, heads, HEAD_DIM)
    )
    probs = jnp.exp(masked_scores() - log_total)
    probs_low = probs.astype(bf16)
    grad_probs = jnp.einsum("pqhe,pkhe->phqk", grad_ctx, v_heads, preferred_element_type=f32)
    grad_vfull = jnp.einsum("phqk,pqhe->pkhe", probs_low, grad_ctx, preferred_element_type=f32)
    grad_scores = (
        probs * (grad_probs - jnp.sum(grad_probs * probs, axis=-1, keepdims=True))
    ).astype(bf16)
    grad_q_low = (
        (jnp.einsum("phqk,pkhe->pqhe", grad_scores, k_heads, preferred_element_type=f32) * scale)
        .astype(bf16)
        .reshape(row_count, width)
    )
    grad_kfull = (
        jnp.einsum("phqk,pqhe->pkhe", grad_scores, q_heads, preferred_element_type=f32) * scale
    )
    grad_keys, grad_values = (
        lax.psum_scatter(
            grad_kfull.reshape(page_count, seq_len, width).astype(jnp.bfloat16),
            "seq",
            scatter_dimension=1,
            tiled=True,
        ).astype(jnp.float32),
        lax.psum_scatter(
            grad_vfull.reshape(page_count, seq_len, width).astype(jnp.bfloat16),
            "seq",
            scatter_dimension=1,
            tiled=True,
        ).astype(jnp.float32),
    )
    grad_k_low = grad_keys.reshape(row_count, width).astype(bf16)
    grad_v_low = grad_values.reshape(row_count, width).astype(bf16)
    grad_tokens = (
        grad_mixed
        + product_nt(grad_q_low, w_query)
        + product_nt(grad_k_low, w_key)
        + product_nt(grad_v_low, w_value)
    )
    grad_wquery = product_tn(tok_low, grad_q_low)
    grad_bquery = jnp.sum(grad_q_low.astype(f32), axis=0)
    grad_wkey = product_tn(tok_low, grad_k_low)
    grad_wvalue = product_tn(tok_low, grad_v_low)
    grad_bvalue = jnp.sum(grad_v_low.astype(f32), axis=0)
    owned = (
        lax.psum_scatter(grad_wquery, ("page", "seq"), scatter_dimension=0, tiled=True),
        lax.psum_scatter(grad_bquery, ("page", "seq"), scatter_dimension=0, tiled=True),
        lax.psum_scatter(grad_wkey, ("page", "seq"), scatter_dimension=0, tiled=True),
        lax.psum_scatter(grad_wvalue, ("page", "seq"), scatter_dimension=0, tiled=True),
        lax.psum_scatter(grad_bvalue, ("page", "seq"), scatter_dimension=0, tiled=True),
        lax.psum_scatter(grad_wout, ("page", "seq"), scatter_dimension=0, tiled=True),
        lax.psum_scatter(grad_bout, ("page", "seq"), scatter_dimension=0, tiled=True),
        lax.psum_scatter(grad_gattn, ("page", "seq"), scatter_dimension=0, tiled=True),
        lax.psum_scatter(grad_sattn, ("page", "seq"), scatter_dimension=0, tiled=True),
        lax.psum_scatter(grad_winner, ("page", "seq"), scatter_dimension=0, tiled=True),
        lax.psum_scatter(grad_binner, ("page", "seq"), scatter_dimension=0, tiled=True),
        lax.psum_scatter(grad_wouter, ("page", "seq"), scatter_dimension=0, tiled=True),
        lax.psum_scatter(grad_bouter, ("page", "seq"), scatter_dimension=0, tiled=True),
        lax.psum_scatter(grad_gfinal, ("page", "seq"), scatter_dimension=0, tiled=True),
        lax.psum_scatter(grad_sfinal, ("page", "seq"), scatter_dimension=0, tiled=True),
    )
    return (
        result.reshape(tokens.shape),
        grad_tokens.reshape(tokens.shape),
        owned[0],
        owned[1],
        owned[2],
        owned[3],
        owned[4],
        owned[5],
        owned[6],
        owned[7],
        owned[8],
        owned[9],
        owned[10],
        owned[11],
        owned[12],
        owned[13],
        owned[14],
    )


def body(
    tokens,
    valid_len,
    query_weight,
    query_bias,
    key_weight,
    value_weight,
    value_bias,
    output_weight,
    output_bias,
    attn_gain,
    attn_shift,
    inner_weight,
    inner_bias,
    outer_weight,
    outer_bias,
    final_gain,
    final_shift,
    out_grad,
):
    lowered = [
        piece.astype(jnp.bfloat16)
        for piece in (
            query_weight,
            query_bias,
            key_weight,
            value_weight,
            value_bias,
            output_weight,
            output_bias,
            attn_gain,
            attn_shift,
            inner_weight,
            inner_bias,
            outer_weight,
            outer_bias,
            final_gain,
            final_shift,
        )
    ]
    outputs = sequence_layer(tokens, valid_len, lowered, out_grad)
    return outputs


def solution(mesh):
    in_specs = (
        P("page", "seq", None),
        P("page"),
        P(("page", "seq"), None),
        P(("page", "seq")),
        P(("page", "seq"), None),
        P(("page", "seq"), None),
        P(("page", "seq")),
        P(("page", "seq"), None),
        P(("page", "seq")),
        P(("page", "seq")),
        P(("page", "seq")),
        P(("page", "seq"), None),
        P(("page", "seq")),
        P(("page", "seq"), None),
        P(("page", "seq")),
        P(("page", "seq")),
        P(("page", "seq")),
        P("page", "seq", None),
    )
    out_specs = (
        P("page", "seq", None),
        P("page", "seq", None),
        P(("page", "seq"), None),
        P(("page", "seq")),
        P(("page", "seq"), None),
        P(("page", "seq"), None),
        P(("page", "seq")),
        P(("page", "seq"), None),
        P(("page", "seq")),
        P(("page", "seq")),
        P(("page", "seq")),
        P(("page", "seq"), None),
        P(("page", "seq")),
        P(("page", "seq"), None),
        P(("page", "seq")),
        P(("page", "seq")),
        P(("page", "seq")),
    )
    return jax.shard_map(body, mesh=mesh, in_specs=in_specs, out_specs=out_specs, check_vma=False)
```

profile of v0, /device:TPU:0, one launch (start us, length us, event | category | flops | bytes accessed | tf_op | source)
XLA Modules:
  0.0 1467.9 jit_solution(7415610204795494744)
XLA Ops:
  19.0 42.4 %all-reduce.18 = (bf16[1024]{0:T(1024)(128)(2,1)S(1)}, bf16[1024]{0:T(1024)(128)(2,1)S(1)}, bf16[1024]{0:T(1024)(128)(2,1)S(1)}, bf16[1024]{0:T(1024)(128)(2,1)S...) all-reduce(bf16[1024]{0:T(1024)(128)(2,1)S(1)} %dynamic-update-slic, ...), channel_id=1, replica_groups=mesh['page'=8,'seq'=4] {'page','seq'}, use_global_device_ids=true, to_apply=%add | all-reduce | flops 8192 | bytes 32768
  61.5 9.5 all-gather.12.cloned.1.call-done
  74.0 55.8 %all-gather.16.cloned.1.call-done = bf16[1024,1024]{1,0:T(8,128)(2,1)} async-done(((bf16[32,1024]{1,0:T(8,128)(2,1)}), bf16[1024,1024]{1,0:T(8,128)(2,1)}) %all-gather.16.cloned.1.call-update) | async-done | bytes 2097168 | tf_op jit(solution)/shard_map/all_gather | solution.py:59
  134.9 39.5 %all-gather.2 = bf16[32,1,128]{2,1,0:T(2,128)(2,1)S(1)} all-gather(bf16[1,1,128]{2,1,0:T(2,128)(2,1)S(1)} %convert_bitcast_fusion), channel_id=1, replica_groups=mesh['page'=8,'seq'=4] {'page','seq'}, dimensions={0}, use_global_device_ids=true | all-gather | bytes 8448 | tf_op jit(solution)/shard_map/all_gather | solution.py:67
  175.1 13.3 all-gather.14.cloned.1.call-done
  190.7 15.4 %all-gather.24.cloned.1.call-done = bf16[512,1024]{1,0:T(8,128)(2,1)} async-done(((bf16[128,1024]{1,0:T(8,128)(2,1)}), bf16[512,1024]{1,0:T(8,128)(2,1)}) %all-gather.24.cloned.1.call-update) | async-done | bytes 1048592 | tf_op jit(solution)/shard_map/all_gather | solution.py:103
  207.6 17.2 %all-gather.26.cloned.1.call-done = bf16[512,1024]{1,0:T(8,128)(2,1)} async-done(((bf16[128,1024]{1,0:T(8,128)(2,1)}), bf16[512,1024]{1,0:T(8,128)(2,1)}) %all-gather.26.cloned.1.call-update) | async-done | bytes 1048592 | tf_op jit(solution)/shard_map/all_gather | solution.py:102
  230.4 54.1 %all-gather.18.cloned.1.call-done = bf16[1024,1024]{1,0:T(8,128)(2,1)} async-done(((bf16[32,1024]{1,0:T(8,128)(2,1)}), bf16[1024,1024]{1,0:T(8,128)(2,1)}) %all-gather.18.cloned.1.call-update) | async-done | bytes 2097168 | tf_op jit(solution)/shard_map/all_gather | solution.py:62
  286.9 77.4 %all-gather.20.cloned.1.call-done = bf16[1024,4096]{1,0:T(8,128)(2,1)} async-done(((bf16[32,4096]{1,0:T(8,128)(2,1)}), bf16[1024,4096]{1,0:T(8,128)(2,1)}) %all-gather.20.cloned.1.call-update) | async-done | bytes 8388624 | tf_op jit(solution)/shard_map/all_gather | solution.py:66
  364.3 4.7 convolution_add_fusion
  369.0 74.8 %all-gather.22.cloned.1.call-done = bf16[4096,1024]{1,0:T(8,128)(2,1)} async-done(((bf16[128,1024]{1,0:T(8,128)(2,1)}), bf16[4096,1024]{1,0:T(8,128)(2,1)}) %all-gather.22.cloned.1.call-update) | async-done | bytes 8388624 | tf_op jit(solution)/shard_map/all_gather | solution.py:68
  443.8 5.0 fusion.45
  450.4 3.5 convert_reduce_fusion
  454.0 3.0 multiply_reduce_fusion.1
  461.4 4.4 multiply_reduce_fusion
  469.7 6.0 copy.60
  478.8 4.3 convolution_convert_fusion
  483.1 6.0 copy.62
  498.5 5.4 copy.64
  504.8 3.7 fusion.28
  514.5 5.3 copy.66
  519.9 9.9 reduce-scatter.27.cloned.1.call-done
  535.8 5.4 copy.68
  541.2 9.4 fusion.38
  551.7 8.1 fusion.31
  564.3 40.5 %all-reduce.17 = (f32[1024]{0:T(1024)S(1)}, f32[1024]{0:T(1024)S(1)}, f32[1024]{0:T(1024)S(1)}, f32[1024]{0:T(1024)S(1)}, f32[1024]{0:T(1024)S(1)}, /*index=5*/f...) all-reduce(f32[1024]{0:T(1024)S(1)} %reduce_sum.184, ...), channel_id=7, replica_groups=mesh['page'=8,'seq'=4] {'page','seq'}, use_global_device_ids=true, to_apply=%region_15.16.clone | all-reduce | flops 12288 | bytes 98304
  614.2 59.7 %reduce-scatter.29.cloned.1.call-done = f32[32,1024]{1,0:T(8,128)} async-done(((f32[1024,1024]{1,0:T(8,128)}), f32[32,1024]{1,0:T(8,128)}) %reduce-scatter.29.cloned.1.call-update) | async-done | bytes 131088
  674.0 139.6 %reduce-scatter.19.cloned.1.call-done = f32[32,1024]{1,0:T(8,128)} async-done(((f32[1024,1024]{1,0:T(8,128)}), f32[32,1024]{1,0:T(8,128)}) %reduce-scatter.19.cloned.1.call-update) | async-done | bytes 131088 | tf_op jit(solution)/shard_map/reduce_scatter | solution.py:235
  813.6 139.7 %reduce-scatter.31.cloned.1.call-done = f32[32,1024]{1,0:T(8,128)} async-done(((f32[1024,1024]{1,0:T(8,128)}), f32[32,1024]{1,0:T(8,128)}) %reduce-scatter.31.cloned.1.call-update) | async-done | bytes 131088
  953.2 139.4 %reduce-scatter.33.cloned.1.call-done = f32[32,1024]{1,0:T(8,128)} async-done(((f32[1024,1024]{1,0:T(8,128)}), f32[32,1024]{1,0:T(8,128)}) %reduce-scatter.33.cloned.1.call-update) | async-done | bytes 131088
  1092.6 181.4 %reduce-scatter.21.cloned.1.call-done = f32[32,4096]{1,0:T(8,128)} async-done(((f32[1024,4096]{1,0:T(8,128)}), f32[32,4096]{1,0:T(8,128)}) %reduce-scatter.21.cloned.1.call-update) | async-done | bytes 524304 | tf_op jit(solution)/shard_map/reduce_scatter | solution.py:239
  1274.1 187.4 %reduce-scatter.23.cloned.1.call-done = f32[128,1024]{1,0:T(8,128)} async-done(((f32[4096,1024]{1,0:T(8,128)}), f32[128,1024]{1,0:T(8,128)}) %reduce-scatter.23.cloned.1.call-update) | async-done | bytes 524304 | tf_op jit(solution)/shard_map/reduce_scatter | solution.py:241
  (185 shorter events, 81.6 us)
Async XLA Ops:
  7.2 122.5 %copy-start.3 = (f32[1,128,1024]{2,1,0:T(8,128)S(1)}, f32[1,128,1024]{2,1,0:T(8,128)}, u32[]{:S(2)}) copy-start(f32[1,128,1024]{2,1,0:T(8,128)} %param.18) | copy-start | bytes 1572868
  7.2 63.7 %all-gather.12.cloned.1.call-start = ((), (), s32[]{:S(2)}) async-start(), calls=%async_computation.8 | async-start | bytes 2162688 | tf_op jit(solution)/shard_map/all_gather | solution.py:60
  8.9 120.9 %all-gather.16.cloned.1.call-start = ((), (), s32[]{:S(2)}) async-start(), calls=%async_computation.10 | async-start | bytes 2162688 | tf_op jit(solution)/shard_map/all_gather | solution.py:59
  10.5 178.0 %all-gather.14.cloned.1.call-start = ((), (), s32[]{:S(2)}) async-start(), calls=%async_computation.9 | async-start | bytes 2162688 | tf_op jit(solution)/shard_map/all_gather | solution.py:57
  12.1 194.0 %all-gather.24.cloned.1.call-start = ((), (), s32[]{:S(2)}) async-start(), calls=%async_computation.17 | async-start | bytes 1310720 | tf_op jit(solution)/shard_map/all_gather | solution.py:103
  73.9 58.7 %copy-start.25 = (f32[32,1024]{1,0:T(8,128)S(1)}, f32[32,1024]{1,0:T(8,128)}, u32[]{:S(2)}) copy-start(f32[32,1024]{1,0:T(8,128)} %param.25) | copy-start | bytes 393220
  73.9 59.4 %copy-start.23 = (f32[32,4096]{1,0:T(8,128)S(1)}, f32[32,4096]{1,0:T(8,128)}, u32[]{:S(2)}) copy-start(f32[32,4096]{1,0:T(8,128)} %param.29) | copy-start | bytes 1572868
  73.9 60.2 %copy-start.24 = (f32[128,1024]{1,0:T(8,128)S(1)}, f32[128,1024]{1,0:T(8,128)}, u32[]{:S(2)}) copy-start(f32[128,1024]{1,0:T(8,128)} %param.31) | copy-start | bytes 1572868
  73.9 61.0 %copy-start.26 = (f32[128]{0:T(128)S(1)}, f32[128]{0:T(128)}, u32[]{:S(2)}) copy-start(f32[128]{0:T(128)} %param.30) | copy-start | bytes 1540
  73.9 150.9 %all-gather.26.cloned.1.call-start = ((), (), s32[]{:S(2)}) async-start(), calls=%async_computation.18 | async-start | bytes 1310720 | tf_op jit(solution)/shard_map/all_gather | solution.py:102
  132.5 152.0 %all-gather.18.cloned.1.call-start = ((), (), s32[]{:S(2)}) async-start(), calls=%async_computation.11 | async-start | bytes 2162688 | tf_op jit(solution)/shard_map/all_gather | solution.py:62
  133.2 231.1 %all-gather.20.cloned.1.call-start = ((), (), s32[]{:S(2)}) async-start(), calls=%async_computation.12 | async-start | bytes 8650752 | tf_op jit(solution)/shard_map/all_gather | solution.py:66
  134.0 309.8 %all-gather.22.cloned.1.call-start = ((), (), s32[]{:S(2)}) async-start(), calls=%async_computation.13 | async-start | bytes 8650752 | tf_op jit(solution)/shard_map/all_gather | solution.py:68
  134.9 373.7 %reduce-scatter.25.cloned.1.call-start = ((), (), s32[]{:S(2)}) async-start(), calls=%async_computation.19 | async-start | bytes 1310720
  207.6 21.0 %copy-start.16 = (bf16[512,1024]{0,1:T(8,128)(2,1)}, bf16[512,1024]{0,1:T(8,128)(2,1)S(1)}, u32[]{:S(2)}) copy-start(bf16[512,1024]{0,1:T(8,128)(2,1)S(1)} %copy.53) | copy-start | bytes 3145732
  230.4 133.9 %copy-start.20 = (bf16[16,64,128]{2,1,0:T(8,128)(2,1)}, bf16[16,64,128]{2,1,0:T(8,128)(2,1)S(1)}, u32[]{:S(2)}) copy-start(bf16[16,64,128]{2,1,0:T(8,128)(2,1)S(1)} %convolution_convert_fusion.2) | copy-start | bytes 786436
  443.8 5.3 copy-start.13
  443.8 6.6 copy-start.2
  449.3 4.6 slice-start
  450.4 3.5 copy-start.11
  450.4 3.5 slice-start.1
  453.9 4.1 copy-start.8
  461.4 4.4 copy-start.1
  478.7 51.1 %reduce-scatter.27.cloned.1.call-start = ((), (), s32[]{:S(2)}) async-start(), calls=%async_computation.20 | async-start | bytes 1310720
  492.1 181.9 %reduce-scatter.29.cloned.1.call-start = ((), (), s32[]{:S(2)}) async-start(), calls=%async_computation.21 | async-start | bytes 4325376
  503.9 309.7 %reduce-scatter.19.cloned.1.call-start = ((), (), s32[]{:S(2)}) async-start(), calls=%async_computation.14 | async-start | bytes 4325376 | tf_op jit(solution)/shard_map/reduce_scatter | solution.py:235
  508.5 444.7 %reduce-scatter.31.cloned.1.call-start = ((), (), s32[]{:S(2)}) async-start(), calls=%async_computation.22 | async-start | bytes 4325376
  519.9 572.7 %reduce-scatter.33.cloned.1.call-start = ((), (), s32[]{:S(2)}) async-start(), calls=%async_computation.23 | async-start | bytes 4325376
  541.2 732.9 %reduce-scatter.21.cloned.1.call-start = ((), (), s32[]{:S(2)}) async-start(), calls=%async_computation.15 | async-start | bytes 17301504 | tf_op jit(solution)/shard_map/reduce_scatter | solution.py:239
  550.7 910.7 %reduce-scatter.23.cloned.1.call-start = ((), (), s32[]{:S(2)}) async-start(), calls=%async_computation.16 | async-start | bytes 17301504 | tf_op jit(solution)/shard_map/reduce_scatter | solution.py:241
  560.9 49.2 %copy-start.18 = (bf16[1,128,1024]{1,2,0:T(8,128)(2,1)S(1)}, bf16[1,128,1024]{1,2,0:T(8,128)(2,1)}, u32[]{:S(2)}) copy-start(bf16[1,128,1024]{1,2,0:T(8,128)(2,1)} %copy-done.17) | copy-start | bytes 786436
  564.2 48.4 %copy-start.6 = (bf16[1024,1024]{1,0:T(8,128)(2,1)S(1)}, bf16[1024,1024]{1,0:T(8,128)(2,1)}, u32[]{:S(2)}) copy-start(bf16[1024,1024]{1,0:T(8,128)(2,1)} %all-gather.12.cloned.1.call-done) | copy-start | bytes 6291460
  (13 other events, 21.2 us)
Sparse Core Ops, SparseCore 0:
  11.5 59.4 all-gather.11
  74.4 55.3 all-gather.15
  133.2 55.2 all-gather.13
  190.5 15.5 all-gather.23
  208.0 16.7 all-gather.25
  228.1 56.3 all-gather.17
  287.9 76.2 all-gather.19
  367.7 76.0 all-gather.21
  478.9 23.4 reduce-scatter.24
  504.9 24.8 reduce-scatter.26
  532.7 141.2 reduce-scatter.28
  676.7 136.8 reduce-scatter.18
  816.4 136.7 reduce-scatter.30
  955.9 136.6 reduce-scatter.32
  1095.3 178.6 reduce-scatter.20
  1276.8 184.5 reduce-scatter.22
where the time goes:
time: 1470 us
  waiting for transfers between devices  1170 us (80%)
  blocking collectives  122 us (8%)
  matrix products  78.5 us (5%)
  local copies, waits for them, and re-layouts  59.8 us (4%)
  other arithmetic  16.7 us (1%)
  between operations  15.2 us (1%)
    unnamed x21, waiting for transfers between devices  349 us
    reduce_scatter x1, waiting for transfers between devices, sequence_layer(): lax.psum_scatter(grad_wouter, ('page', 'seq'), scatter_dimension=0, tiled...  187 us
    reduce_scatter x1, waiting for transfers between devices, sequence_layer(): lax.psum_scatter(grad_winner, ('page', 'seq'), scatter_dimension=0, tiled...  181 us
    reduce_scatter x1, waiting for transfers between devices, sequence_layer(): lax.psum_scatter(grad_wout, ('page', 'seq'), scatter_dimension=0, tiled=T...  140 us
    unnamed x2, blocking collectives  82.9 us
    all_gather x1, waiting for transfers between devices, sequence_layer(): lax.all_gather(lowered[9], ('page', 'seq'), axis=0, tiled=True)  77.4 us
    all_gather x1, waiting for transfers between devices, sequence_layer(): lax.all_gather(lowered[11], ('page', 'seq'), axis=0, tiled=True)  74.8 us
    all_gather x1, waiting for transfers between devices, sequence_layer(): lax.all_gather(lowered[2], ('page', 'seq'), axis=0, tiled=True)  55.8 us
  transfers between devices with their start and end apart: 16, of which 15 were waited for; matrix products, arithmetic and copies ran while one was open for 8% of the time, Pallas kernels for 0%

commit v1 on v0

--- a/solution.py
+++ b/solution.py
@@ -1,8 +1,12 @@
+import functools
 import math
+import types
 
 import jax
 import jax.numpy as jnp
 from jax import lax
+from jax.experimental import pallas as pl
+from jax.experimental.pallas import tpu as pltpu
 from jax.sharding import PartitionSpec as P
 
 HEAD_DIM = 64
@@ -264,6 +268,885 @@
     )
 
 
+MESH = pl.DeviceIdType.MESH
+BF16 = jnp.bfloat16
+F32 = jnp.float32
+VECTORS = 8
+SLAB = 16
+NEGATIVE = -1000000000.0
+
+
+def dot_nn(left, right):
+    return lax.dot_general(left, right, (((1,), (0,)), ((), ())), preferred_element_type=F32)
+
+
+def dot_nt(left, right):
+    return lax.dot_general(left, right, (((1,), (1,)), ((), ())), preferred_element_type=F32)
+
+
+def dot_tn(left, right):
+    return lax.dot_general(left, right, (((0,), (0,)), ((), ())), preferred_element_type=F32)
+
+
+class Sizes:
+    def __init__(self, mesh, width, units, span):
+        self.pages = mesh.shape["page"]
+        self.parts = mesh.shape["seq"]
+        self.half = self.pages // 2
+        self.width = width
+        self.units = units
+        self.span = span
+        self.length = span * self.parts
+        self.row = width // (self.pages * self.parts)
+        self.rows = self.row * self.parts
+        self.unit = units // (self.pages * self.parts)
+        self.mine = self.unit * self.pages
+        self.cols = width // self.parts
+        self.heads = self.cols // HEAD_DIM
+
+
+def supported(mesh, token_shape, width, units):
+    pages, parts = mesh.shape["page"], mesh.shape["seq"]
+    return (
+        parts == 4
+        and pages % 2 == 0
+        and pages >= 4
+        and token_shape[0] == pages
+        and token_shape[1] % (parts * 128) == 0
+        and width % (pages * parts * 32) == 0
+        and width // pages == 128
+        and units % (pages * parts * 128) == 0
+        and (width // parts) % 128 == 0
+    )
+
+
+def layer_kernel(z, names, *refs):
+    r = types.SimpleNamespace(**dict(zip(names, refs)))
+    send_sem, recv_sem = r.send_sem, r.recv_sem
+    page = lax.axis_index("page")
+    part = lax.axis_index("seq")
+    counter = [0]
+    sent = []
+
+    def slots(count):
+        first = counter[0]
+        counter[0] += count
+        return first
+
+    odd = page % 2
+    place = odd * (z.pages - 1 - page // 2) + (1 - odd) * (page // 2)
+
+    def page_at(index):
+        index = (index + 2 * z.pages) % z.pages
+        late = index // z.half
+        return (1 - late) * (2 * index) + late * (2 * z.pages - 1 - 2 * index)
+
+    def peer(j):
+        return ((part // 2 + j // 2) % 2) * 2 + (part % 2 + j % 2) % 2
+
+    rank = page * z.parts + part
+    hold_page, hold_part = rank % z.pages, rank // z.pages
+    flat = part * z.pages + page
+    own_page, own_part = flat // z.parts, flat % z.parts
+    moves = 1 - (1 - jnp.minimum(1, (hold_page - page) * (hold_page - page))) * (
+        1 - jnp.minimum(1, (hold_part - part) * (hold_part - part))
+    )
+
+    def copy(src, dst, index, device):
+        return pltpu.make_async_remote_copy(
+            src_ref=src,
+            dst_ref=dst,
+            send_sem=send_sem.at[index],
+            recv_sem=recv_sem.at[index],
+            device_id=device,
+            device_id_type=MESH,
+        )
+
+    def block(ref, index, size):
+        return ref.at[pl.ds(pl.multiple_of(index * size, size), size)]
+
+    barrier = pltpu.get_barrier_semaphore()
+
+    def greet(device):
+        pl.semaphore_signal(barrier, inc=1, device_id=device, device_id_type=MESH)
+
+    for j in (1, 2, 3):
+        greet((page, peer(j)))
+    greet((page_at(place + 1), part))
+    greet((page_at(place - 1), part))
+
+    @pl.when(moves == 1)
+    def _():
+        greet((hold_page, hold_part))
+        greet((own_page, own_part))
+
+    class Share:
+        def __init__(self, ref, size):
+            self.ref, self.size, self.first = ref, size, slots(4)
+
+        def copy(self, j, owner):
+            piece = block(self.ref, owner, self.size)
+            return copy(piece, piece, self.first + j, (page, peer(j)))
+
+        def start(self):
+            for j in (2, 3, 1):
+                self.copy(j, part).start()
+            sent.append(lambda: [self.copy(j, part).wait_send() for j in (1, 2, 3)])
+
+        def wait(self, j):
+            self.copy(j, peer(j)).wait_recv()
+
+        def wait_all(self):
+            for j in (1, 2, 3):
+                self.wait(j)
+
+    class Spread:
+        def __init__(self, src, dst, size):
+            self.src, self.dst, self.size, self.first = src, dst, size, slots(4)
+
+        def copy(self, j):
+            return copy(
+                block(self.src, peer(j), self.size),
+                self.dst.at[j],
+                self.first + j,
+                (page, peer(j)),
+            )
+
+        def start(self, j):
+            self.copy(j).start()
+
+        def start_all(self):
+            for j in (2, 3, 1):
+                self.start(j)
+
+        def finish(self):
+            sent.append(lambda: [self.copy(j).wait_send() for j in (1, 2, 3)])
+
+        def wait(self, j):
+            self.copy(j).wait_recv()
+
+    class Place:
+        def __init__(self, src, dst, size, base):
+            self.src, self.dst, self.size, self.base, self.first = src, dst, size, base, slots(4)
+
+        def copy(self, j, owner):
+            return copy(
+                block(self.src, peer(j), self.size),
+                block(self.dst, self.base + owner, self.size),
+                self.first + j,
+                (page, peer(j)),
+            )
+
+        def start(self):
+            for j in (2, 3, 1):
+                self.copy(j, part).start()
+            sent.append(lambda: [self.copy(j, part).wait_send() for j in (1, 2, 3)])
+
+        def wait(self):
+            for j in (1, 2, 3):
+                self.copy(j, peer(j)).wait_recv()
+
+    class Gather:
+        def __init__(self, ref, size):
+            self.ref, self.size = ref, size
+            self.first = slots(2 * z.half)
+
+        def copy(self, t, d, index):
+            piece = block(self.ref, page_at(index), self.size)
+            if t == z.half - 1:
+                h = self.size // 2
+                piece = piece.at[pl.ds(d * h, h)]
+            return copy(
+                piece, piece, self.first + 2 * t + d, (page_at(place + 1 - 2 * d), part)
+            )
+
+        def wait(self, t):
+            for d in (0, 1):
+                self.copy(t, d, place - (1 - 2 * d) * (1 + t)).wait_recv()
+
+        def step(self, t):
+            if t > 0:
+                self.wait(t - 1)
+            for d in (0, 1):
+                self.copy(t, d, place - (1 - 2 * d) * t).start()
+                sent.append(
+                    functools.partial(
+                        lambda t, d: self.copy(t, d, place - (1 - 2 * d) * t).wait_send(), t, d
+                    )
+                )
+
+        def done(self):
+            self.wait(z.half - 1)
+
+    class Reduce:
+        def __init__(self, slot, stage, local, shape, kind):
+            self.slot, self.stage, self.local = slot, stage, local
+            self.size, self.kind = shape[0], kind
+            self.first = slots(2 * z.half)
+
+        def copy(self, t, d):
+            h = self.size // 2
+            if t == 0:
+                src = self.stage.at[pl.ds(d * h, h)]
+                dst = self.slot.at[d, 0, pl.ds(d * h, h)]
+            else:
+                src = self.slot.at[d, t - 1]
+                dst = self.slot.at[d, t]
+            return copy(src, dst, self.first + 2 * t + d, (page_at(place + 1 - 2 * d), part))
+
+        def step(self, t):
+            h = self.size // 2
+            if t == 0:
+                self.stage[...] = self.local(page_at(place + z.half)).astype(self.kind)
+                for d in (0, 1):
+                    self.copy(0, d).start()
+            else:
+                for d in (0, 1):
+                    term = self.local(page_at(place + (1 - 2 * d) * (z.half - t)))
+                    self.copy(t - 1, d).wait_recv()
+                    held = self.slot.at[d, t - 1]
+                    if t == 1:
+                        near, far = pl.ds(d * h, h), pl.ds((1 - d) * h, h)
+                        part_near = term[d * h : (d + 1) * h]
+                        part_far = term[(1 - d) * h : (2 - d) * h]
+                        held[near] = (held[near].astype(F32) + part_near).astype(self.kind)
+                        held[far] = part_far.astype(self.kind)
+                    else:
+                        held[...] = (held[...].astype(F32) + term).astype(self.kind)
+                    self.copy(t, d).start()
+            for d in (0, 1):
+                sent.append(functools.partial(lambda t, d: self.copy(t, d).wait_send(), t, d))
+
+        def total(self):
+            term = self.local(page)
+            for d in (0, 1):
+                self.copy(z.half - 1, d).wait_recv()
+            last = z.half - 1
+            return term + self.slot[0, last].astype(F32) + self.slot[1, last].astype(F32)
+
+    c, w, n = z.cols, z.width, z.span
+    for q in range(z.parts):
+        rows = pl.ds(q * z.row, z.row)
+        for i, weight in enumerate((r.w_query, r.w_key, r.w_value)):
+            r.cut_qkv[rows, i * c : (i + 1) * c] = weight[:, q * c : (q + 1) * c].astype(BF16)
+        for g in range(z.pages):
+            at = (z.parts * g + q) * z.unit
+            r.cut_inner[rows, g * z.unit : (g + 1) * z.unit] = r.w_inner[
+                :, at : at + z.unit
+            ].astype(BF16)
+    r.own_out[...] = r.w_out[...].astype(BF16)
+    r.tok_all[pl.ds(pl.multiple_of(part * n, n), n), :] = r.tokens[...].astype(BF16)
+    base = pl.multiple_of(rank * SLAB, SLAB)
+    for i, small in enumerate(
+        (r.b_query, r.b_value, r.b_out, r.g_attn, r.s_attn, r.b_outer, r.g_final, r.s_final)
+    ):
+        r.vec_all[pl.ds(base + i, 1), 0 : z.row] = small[...]
+    r.vec_all[pl.ds(base + VECTORS, 1), :] = r.b_inner[...]
+
+    cut_qkv = Place(r.cut_qkv, r.qkv_w, z.row, page * z.parts)
+    cut_inner = Place(r.cut_inner, r.inner_w, z.row, page * z.parts)
+    share_tok = Share(r.tok_all, n)
+
+    class ShareVec:
+        first = slots(4)
+
+        def copy(self, j, owner):
+            piece = block(r.vec_all, page * z.parts + owner, SLAB)
+            return copy(piece, piece, self.first + j, (page, peer(j)))
+
+    vec_share = ShareVec()
+    hold = slots(1)
+
+    def hold_copy():
+        return copy(
+            r.own_out, block(r.out_w, own_slot_page, z.row), hold, (hold_page, hold_part)
+        )
+
+    own_slot_page = hold_page
+    pl.semaphore_wait(barrier, 5 + 2 * moves)
+    cut_qkv.start()
+    for j in (2, 3, 1):
+        vec_share.copy(j, part).start()
+    sent.append(lambda: [vec_share.copy(j, part).wait_send() for j in (1, 2, 3)])
+    share_tok.start()
+
+    @pl.when(moves == 1)
+    def _():
+        hold_copy().start()
+
+    @pl.when(moves == 0)
+    def _():
+        r.out_w[pl.ds(pl.multiple_of(page * z.row, z.row), z.row), :] = r.own_out[...]
+
+    cut_inner.start()
+    own_rows = pl.ds(pl.multiple_of(rank * z.row, z.row), z.row)
+    cut_rows = pl.ds(pl.multiple_of(part * z.row, z.row), z.row)
+    r.qkv_w[own_rows, :] = r.cut_qkv[cut_rows, :]
+    r.inner_w[own_rows, :] = r.cut_inner[cut_rows, :]
+    r.outer_w[pl.ds(pl.multiple_of(page * z.unit, z.unit), z.unit), :] = r.w_outer[
+        ...
+    ].astype(BF16)
+
+    ring_qkv = Gather(r.qkv_w, z.rows)
+    ring_vec = Gather(r.vec_all, z.parts * SLAB)
+    ring_inner = Gather(r.inner_w, z.rows)
+    ring_out = Gather(r.out_w, z.row)
+    ring_outer = Gather(r.outer_w, z.unit)
+
+    cut_qkv.wait()
+    ring_qkv.step(0)
+    for j in (1, 2, 3):
+        vec_share.copy(j, peer(j)).wait_recv()
+    ring_vec.step(0)
+    for t in range(1, z.half):
+        ring_qkv.step(t)
+        ring_vec.step(t)
+
+    @pl.when(moves == 1)
+    def _():
+        copy(
+            r.own_out, block(r.out_w, page, z.row), hold, (hold_page, hold_part)
+        ).wait_recv()
+
+    ring_out.step(0)
+    cut_inner.wait()
+    ring_inner.step(0)
+    ring_qkv.done()
+    ring_vec.done()
+
+    lane = lax.broadcasted_iota(jnp.int32, (VECTORS, 128), 1)
+    for g in range(z.pages):
+        total = jnp.zeros((VECTORS, 128), F32)
+        for q in range(z.parts):
+            tile = r.vec_all[pl.ds((g * z.parts + q) * SLAB, VECTORS), :]
+            if q:
+                tile = pltpu.roll(tile, q * z.row, 1)
+            total = total + jnp.where(lane // z.row == q, tile, 0.0)
+        r.vecs[:, g * 128 : (g + 1) * 128] = total.astype(BF16).astype(F32)
+        at = pl.multiple_of((g * z.parts + part) * SLAB + VECTORS, VECTORS)
+        tile = r.vec_all[pl.ds(at, 8), :]
+        r.b_mine[:, g * z.unit : (g + 1) * z.unit] = tile[0:1].astype(BF16).astype(F32)
+
+    def vector(i):
+        return r.vecs[i : i + 1, :]
+
+    my_cols = pl.ds(pl.multiple_of(part * c, c), c)
+
+    share_tok.wait_all()
+
+    def make_qkv(b, carry):
+        rows = pl.ds(pl.multiple_of(b * n, n), n)
+        out = dot_nn(r.tok_all[rows, :], r.qkv_w[...])
+        r.qkv[rows, 0:c] = (out[:, 0:c] + r.vecs[0:1, my_cols]).astype(BF16)
+        r.qkv[rows, c : 2 * c] = out[:, c : 2 * c].astype(BF16)
+        r.qkv[rows, 2 * c :] = (out[:, 2 * c :] + r.vecs[1:2, my_cols]).astype(BF16)
+        return carry
+
+    lax.fori_loop(0, z.parts, make_qkv, 0)
+    ring_out.step(1)
+    ring_inner.step(1)
+
+    scale = HEAD_DIM ** (-0.5)
+    first_head = lax.broadcasted_iota(jnp.int32, (n, 128), 1) < HEAD_DIM
+    key_place = lax.broadcasted_iota(jnp.int32, (n, z.length), 1)
+    valid = r.valid[0]
+
+    def pair_cols(kind, pair):
+        return pl.ds(kind * c + pair * 128, 128)
+
+    def attend(pair):
+        def body(b, carry):
+            rows = pl.ds(pl.multiple_of(b * n, n), n)
+            queries = r.qkv[rows, pair_cols(0, pair)]
+            keys = r.qkv[:, pair_cols(1, pair)]
+            values = r.qkv[:, pair_cols(2, pair)]
+            outs = []
+            for h in range(2):
+                mine = first_head if h == 0 else ~first_head
+                scores = dot_nt(jnp.where(mine, queries, jnp.zeros_like(queries)), keys) * scale
+                scores = jnp.where(key_place < valid, scores, NEGATIVE)
+                top = jnp.max(scores, axis=-1, keepdims=True)
+                weight = jnp.exp(scores - top)
+                probs = weight * (1.0 / jnp.sum(weight, axis=-1, keepdims=True))
+                r.probs[2 * pair + h, rows, :] = probs
+                outs.append(dot_nn(probs.astype(BF16), values))
+            r.ctx[rows, pl.ds(pair * 128, 128)] = jnp.where(first_head, outs[0], outs[1]).astype(
+                BF16
+            )
+            return carry
+
+        lax.fori_loop(0, z.parts, body, 0)
+
+    attend(0)
+    ring_out.step(2)
+    ring_inner.step(2)
+    ring_outer.step(0)
+    attend(1)
+    ring_out.step(3)
+    ring_inner.step(3)
+    ring_outer.step(1)
+    ring_out.done()
+
+    def partial_rows(phase, make):
+        spread = Spread(r.part_out.at[phase], r.part_in.at[phase], n)
+
+        def body(i, carry):
+            j = (i + 1) % 4
+            b = peer(j)
+            rows = pl.ds(pl.multiple_of(b * n, n), n)
+            term = make(rows, j)
+
+            @pl.when(j > 0)
+            def _():
+                r.part_out[phase, rows, :] = term.astype(BF16)
+                spread.start(j)
+
+            @pl.when(j == 0)
+            def _():
+                r.part_own[...] = term
+
+            return carry
+
+        lax.fori_loop(0, z.parts, body, 0)
+        spread.finish()
+        return spread
+
+    def row_sum(phase, rows):
+        total = r.part_own[rows, :]
+        for j in (1, 2, 3):
+            total = total + r.part_in[phase, j, rows, :].astype(F32)
+        return total
+
+    def by_rows(fn):
+        size = 32
+
+        def body(i, carry):
+            fn(pl.ds(pl.multiple_of(i * size, size), size), pl.multiple_of(i * size, size))
+            return carry
+
+        lax.fori_loop(0, n // size, body, 0)
+
+    def add_column_sum(i, values):
+        r.sums[i : i + 1, :] += jnp.sum(values, axis=0, keepdims=True)
+
+    r.sums[...] = jnp.zeros_like(r.sums)
+
+    spread = partial_rows(0, lambda rows, j: dot_nn(r.ctx[rows, :], r.out_w[...]))
+    ring_outer.step(2)
+    for j in (1, 2, 3):
+        spread.wait(j)
+
+    share_hid = Share(r.hid_all, n)
+
+    def first_norm(rows, at):
+        mixed = r.tokens[rows, :] + (row_sum(0, rows) + vector(2))
+        normed, inverse = norm_parts(mixed)
+        hidden = normed * vector(3) + vector(4)
+        r.norm_one[rows, :] = normed
+        r.inv_one[rows, :] = inverse
+        r.hidden[rows, :] = hidden
+        r.hid_all[pl.ds(pl.multiple_of(part * n + at, 32), 32), :] = hidden.astype(BF16)
+
+    by_rows(first_norm)
+    share_hid.start()
+    ring_outer.step(3)
+    ring_inner.done()
+
+    def make_inner(j, carry):
+        @pl.when(j > 0)
+        def _():
+            share_hid.copy(j, peer(j)).wait_recv()
+
+        rows = pl.ds(pl.multiple_of(peer(j) * n, n), n)
+        tile = 256
+
+        def columns(i, carry):
+            cols = pl.ds(pl.multiple_of(i * tile, tile), tile)
+            inner = dot_nn(r.hid_all[rows, :], r.inner_w[:, cols]) + r.b_mine[:, cols]
+            active, slope = gelu_parts(inner)
+            r.active[rows, cols] = active.astype(BF16)
+            r.slope[rows, cols] = slope
+            return carry
+
+        return lax.fori_loop(0, z.mine // tile, columns, carry)
+
+    lax.fori_loop(0, z.parts, make_inner, 0)
+    ring_outer.done()
+    spread = partial_rows(1, lambda rows, j: dot_nn(r.active[rows, :], r.outer_w[...]))
+    for j in (1, 2, 3):
+        spread.wait(j)
+
+    share_gf = Share(r.gf_all, n)
+
+    def second_norm(rows, at):
+        outer = row_sum(1, rows) + vector(5)
+        normed, inverse = norm_parts(r.hidden[rows, :] + outer)
+        r.o_out[rows, :] = normed * vector(6) + vector(7)
+        grad = r.out_grad[rows, :]
+        add_column_sum(6, grad * normed)
+        add_column_sum(7, grad)
+        grad_sum = norm_backward(grad, normed, inverse, vector(6))
+        low = grad_sum.astype(BF16)
+        add_column_sum(5, low.astype(F32))
+        r.grad_sum[rows, :] = grad_sum
+        r.gf_all[pl.ds(pl.multiple_of(part * n + at, 32), 32), :] = low
+
+    by_rows(second_norm)
+    share_gf.start()
+
+    def chunk_term(left, right, size):
+        def local(g):
+            cols = pl.ds(pl.multiple_of(g * size, size), size)
+            return dot_tn(left[:, cols], right[...])
+
+        return local
+
+    reduce_outer = Reduce(
+        r.slot_outer, r.stage_outer, chunk_term(r.active, r.gf_all, z.unit), (z.unit, w), BF16
+    )
+    reduce_inner = Reduce(
+        r.slot_inner, r.stage_inner, chunk_term(r.hid_all, r.grad_inner, z.rows),
+        (z.rows, z.mine), BF16,
+    )
+    reduce_qkv = Reduce(
+        r.slot_qkv, r.stage_qkv, chunk_term(r.tok_all, r.grad_qkv, z.rows),
+        (z.rows, 3 * c), BF16,
+    )
+    reduce_out = Reduce(
+        r.slot_out, r.stage_out,
+        lambda g: r.term_out[pl.ds(pl.multiple_of(g * z.row, z.row), z.row), :], (z.row, w), BF16,
+    )
+    reduce_vec = Reduce(
+        r.slot_vec, r.stage_vec,
+        lambda g: r.term_vec[pl.ds(pl.multiple_of(g * SLAB, SLAB), SLAB), :], (SLAB, 128), F32,
+    )
+
+    r.b_sum[...] = jnp.zeros_like(r.b_sum)
+
+    def make_grad_inner(rows, j):
+        @pl.when(j > 0)
+        def _():
+            share_gf.copy(j, peer(j)).wait_recv()
+
+        tile = 256
+
+        def columns(i, carry):
+            cols = pl.ds(pl.multiple_of(i * tile, tile), tile)
+            grad = dot_nt(r.gf_all[rows, :], r.outer_w[cols, :]) * r.slope[rows, cols]
+            low = grad.astype(BF16)
+            r.grad_inner[rows, cols] = low
+            r.b_sum[:, cols] += jnp.sum(low.astype(F32), axis=0, keepdims=True)
+            return carry
+
+        lax.fori_loop(0, z.mine // tile, columns, 0)
+        return dot_nt(r.grad_inner[rows, :], r.inner_w[...])
+
+    spread = partial_rows(2, make_grad_inner)
+    reduce_outer.step(0)
+    reduce_inner.step(0)
+    for j in (1, 2, 3):
+        spread.wait(j)
+
+    share_ga = Share(r.ga_all, n)
+
+    def first_norm_back(rows, at):
+        grad = r.grad_sum[rows, :] + row_sum(2, rows)
+        normed = r.norm_one[rows, :]
+        add_column_sum(3, grad * normed)
+        add_column_sum(4, grad)
+        mixed = norm_backward(grad, normed, r.inv_one[rows, :], vector(3))
+        low = mixed.astype(BF16)
+        add_column_sum(2, low.astype(F32))
+        r.grad_mixed[rows, :] = mixed
+        r.ga_all[pl.ds(pl.multiple_of(part * n + at, 32), 32), :] = low
+
+    by_rows(first_norm_back)
+    share_ga.start()
+    reduce_outer.step(1)
+    reduce_inner.step(1)
+
+    def make_grad_ctx(j, carry):
+        @pl.when(j > 0)
+        def _():
+            share_ga.copy(j, peer(j)).wait_recv()
+
+        rows = pl.ds(pl.multiple_of(peer(j) * n, n), n)
+        r.grad_ctx[rows, :] = dot_nt(r.ga_all[rows, :], r.out_w[...]).astype(BF16)
+        return carry
+
+    lax.fori_loop(0, z.parts, make_grad_ctx, 0)
+    r.term_out[...] = dot_tn(r.ctx[...], r.ga_all[...])
+    reduce_out.step(0)
+
+    def attend_back(pair):
+        r.grad_kv[...] = jnp.zeros_like(r.grad_kv)
+
+        def body(b, carry):
+            rows = pl.ds(pl.multiple_of(b * n, n), n)
+            queries = r.qkv[rows, pair_cols(0, pair)]
+            keys = r.qkv[:, pair_cols(1, pair)]
+            values = r.qkv[:, pair_cols(2, pair)]
+            grad = r.grad_ctx[rows, pl.ds(pair * 128, 128)]
+            outs = []
+            for h in range(2):
+                mine = first_head if h == 0 else ~first_head
+                grad_mine = jnp.where(mine, grad, jnp.zeros_like(grad))
+                query_mine = jnp.where(mine, queries, jnp.zeros_like(queries))
+                probs = r.probs[2 * pair + h, rows, :]
+                grad_probs = dot_nt(grad_mine, values)
+                r.grad_kv[1] += dot_tn(probs.astype(BF16), grad_mine)
+                inside = jnp.sum(grad_probs * probs, axis=-1, keepdims=True)
+                grad_scores = (probs * (grad_probs - inside)).astype(BF16)
+                outs.append(dot_nn(grad_scores, keys))
+                r.grad_kv[0] += dot_tn(grad_scores, query_mine)
+            r.grad_qkv[rows, pair_cols(0, pair)] = (
+                jnp.where(first_head, outs[0], outs[1]) * scale
+            ).astype(BF16)
+            return carry
+
+        lax.fori_loop(0, z.parts, body, 0)
+        r.grad_qkv[:, pair_cols(1, pair)] = (r.grad_kv[0] * scale).astype(BF16)
+        r.grad_qkv[:, pair_cols(2, pair)] = r.grad_kv[1].astype(BF16)
+
+    attend_back(0)
+    reduce_outer.step(2)
+    reduce_inner.step(2)
+    reduce_out.step(1)
+    attend_back(1)
+    reduce_outer.step(3)
+    reduce_inner.step(3)
+    reduce_out.step(2)
+    reduce_qkv.step(0)
+
+    r.sums[0:1, my_cols] = jnp.sum(r.grad_qkv[:, 0:c].astype(F32), axis=0, keepdims=True)
+    r.sums[1:2, my_cols] = jnp.sum(r.grad_qkv[:, 2 * c :].astype(F32), axis=0, keepdims=True)
+    r.term_vec[...] = jnp.zeros_like(r.term_vec)
+    for g in range(z.pages):
+        r.term_vec[g * SLAB : g * SLAB + VECTORS, :] = r.sums[:, g * 128 : (g + 1) * 128]
+        r.term_vec[g * SLAB + VECTORS : g * SLAB + VECTORS + 1, :] = r.b_sum[
+            :, g * z.unit : (g + 1) * z.unit
+        ]
+    reduce_vec.step(0)
+
+    spread = partial_rows(3, lambda rows, j: dot_nt(r.grad_qkv[rows, :], r.qkv_w[...]))
+    reduce_out.step(3)
+    reduce_qkv.step(1)
+    reduce_vec.step(1)
+
+    r.o_outer[...] = reduce_outer.total()
+    r.fin_inner[...] = reduce_inner.total().astype(BF16)
+    fin_inner = Spread(r.fin_inner, r.got_inner, z.row)
+    fin_inner.start_all()
+    fin_inner.finish()
+    reduce_qkv.step(2)
+    reduce_vec.step(2)
+    for j in (1, 2, 3):
+        spread.wait(j)
+
+    def input_rows(rows, at):
+        r.o_grad[rows, :] = r.grad_mixed[rows, :] + row_sum(3, rows)
+
+    by_rows(input_rows)
+    r.fin_out[...] = reduce_out.total().astype(BF16)
+    home = slots(1)
+
+    def home_copy():
+        return copy(r.fin_out, r.got_out, home, (own_page, own_part))
+
+    @pl.when(moves == 1)
+    def _():
+        home_copy().start()
+
+    @pl.when(moves == 0)
+    def _():
+        r.got_out[...] = r.fin_out[...]
+
+    reduce_qkv.step(3)
+    reduce_vec.step(3)
+    r.fin_vec[...] = reduce_vec.total()
+
+    class VecAll:
+        first = slots(4)
+
+        def copy(self, j):
+            return copy(r.fin_vec, r.got_vec.at[j], self.first + j, (page, peer(j)))
+
+    fin_vec = VecAll()
+    for j in (2, 3, 1):
+        fin_vec.copy(j).start()
+    sent.append(lambda: [fin_vec.copy(j).wait_send() for j in (1, 2, 3)])
+    r.fin_qkv[...] = reduce_qkv.total().astype(BF16)
+    fin_qkv = Spread(r.fin_qkv, r.got_qkv, z.row)
+    fin_qkv.start_all()
+    fin_qkv.finish()
+
+    my_rows = pl.ds(pl.multiple_of(part * z.row, z.row), z.row)
+
+    def deliver(spread, mine, got, out):
+        for j in range(4):
+            if j:
+                spread.wait(j)
+            value = got[j] if j else mine[my_rows, :]
+            out[peer(j)] = value
+
+    deliver(fin_inner, r.fin_inner, r.got_inner, r.o_inner)
+
+    @pl.when(moves == 1)
+    def _():
+        home_copy().wait_recv()
+
+    r.o_wout[...] = r.got_out[...]
+    summed = r.fin_vec[0:VECTORS, :]
+    for j in (1, 2, 3):
+        fin_vec.copy(j).wait_recv()
+        summed = summed + r.got_vec[j, 0:VECTORS, :]
+    r.o_vec[0:VECTORS, :] = pltpu.roll(summed, (128 - part * z.row) % 128, 1)
+    r.o_vec[VECTORS:, :] = r.fin_vec[VECTORS:, :]
+    deliver(fin_qkv, r.fin_qkv, r.got_qkv, r.o_qkv)
+
+    for wait in sent:
+        wait()
+
+    @pl.when(moves == 1)
+    def _():
+        hold_copy().wait_send()
+        home_copy().wait_send()
+
+    assert counter[0] <= z.sems, counter[0]
+
+
+def finish_kernel(z, out, grad, outer, inner, qkv, wout, vec, *outs):
+    (o_out, o_grad, o_wq, o_bq, o_wk, o_wv, o_bv, o_wo, o_bo, o_ga, o_sa, o_wi, o_bi, o_wu, o_bu, o_gf, o_sf) = outs
+    o_out[...] = out[...]
+    o_grad[...] = grad[...]
+    o_wu[...] = outer[...]
+    o_wo[...] = wout[...].astype(F32)
+    c = z.cols
+    for q in range(z.parts):
+        for i, ref in enumerate((o_wq, o_wk, o_wv)):
+            ref[:, q * c : (q + 1) * c] = qkv[q, :, i * c : (i + 1) * c].astype(F32)
+        for g in range(z.pages):
+            at = (z.parts * g + q) * z.unit
+            o_wi[:, at : at + z.unit] = inner[q, :, g * z.unit : (g + 1) * z.unit].astype(F32)
+    for i, ref in enumerate((o_bq, o_bv, o_bo, o_ga, o_sa, o_bu, o_gf, o_sf)):
+        ref[...] = vec[i : i + 1, 0 : z.row]
+    o_bi[...] = vec[VECTORS : VECTORS + 1, :]
+
+
+def paged_layer(z, tokens, valid_len, params, out_grad):
+    (
+        w_query, b_query, w_key, w_value, b_value, w_out, b_out, g_attn, s_attn,
+        w_inner, b_inner, w_outer, b_outer, g_final, s_final,
+    ) = params
+    flat = lambda v: v.reshape(1, v.shape[0])
+    c, w, n, ln, half = z.cols, z.width, z.span, z.length, z.half
+    ins = dict(
+        valid=valid_len,
+        tokens=tokens.reshape(n, w),
+        out_grad=out_grad.reshape(n, w),
+        w_query=w_query, w_key=w_key, w_value=w_value, w_out=w_out,
+        w_inner=w_inner, w_outer=w_outer,
+        b_query=flat(b_query), b_value=flat(b_value), b_out=flat(b_out),
+        g_attn=flat(g_attn), s_attn=flat(s_attn), b_inner=flat(b_inner),
+        b_outer=flat(b_outer), g_final=flat(g_final), s_final=flat(s_final),
+    )
+    outs = dict(
+        o_out=((n, w), F32),
+        o_grad=((n, w), F32),
+        o_outer=((z.unit, w), F32),
+        o_inner=((z.parts, z.row, z.mine), BF16),
+        o_qkv=((z.parts, z.row, 3 * c), BF16),
+        o_wout=((z.row, w), BF16),
+        o_vec=((SLAB, 128), F32),
+    )
+    scratch = dict(
+        qkv_w=((w, 3 * c), BF16),
+        inner_w=((w, z.mine), BF16),
+        out_w=((c, w), BF16),
+        outer_w=((z.mine, w), BF16),
+        vec_all=((z.pages * z.parts * SLAB, 128), F32),
+        cut_qkv=((z.rows, 3 * c), BF16),
+        cut_inner=((z.rows, z.mine), BF16),
+        own_out=((z.row, w), BF16),
+        vecs=((VECTORS, w), F32),
+        b_mine=((1, z.mine), F32),
+        tok_all=((ln, w), BF16),
+        hid_all=((ln, w), BF16),
+        gf_all=((ln, w), BF16),
+        ga_all=((ln, w), BF16),
+        qkv=((ln, 3 * c), BF16),
+        grad_qkv=((ln, 3 * c), BF16),
+        probs=((z.heads, ln, ln), F32),
+        ctx=((ln, c), BF16),
+        grad_ctx=((ln, c), BF16),
+        grad_kv=((2, ln, 128), F32),
+        part_out=((4, ln, w), BF16),
+        part_in=((4, 4, n, w), BF16),
+        part_own=((n, w), F32),
+        norm_one=((n, w), F32),
+        inv_one=((n, 1), F32),
+        hidden=((n, w), F32),
+        grad_sum=((n, w), F32),
+        grad_mixed=((n, w), F32),
+        active=((ln, z.mine), BF16),
+        slope=((ln, z.mine), F32),
+        grad_inner=((ln, z.mine), BF16),
+        sums=((VECTORS, w), F32),
+        b_sum=((1, z.mine), F32),
+        term_out=((c, w), F32),
+        term_vec=((z.pages * SLAB, 128), F32),
+        slot_outer=((2, half, z.unit, w), BF16), stage_outer=((z.unit, w), BF16),
+        slot_inner=((2, half, z.rows, z.mine), BF16), stage_inner=((z.rows, z.mine), BF16),
+        slot_qkv=((2, half, z.rows, 3 * c), BF16), stage_qkv=((z.rows, 3 * c), BF16),
+        slot_out=((2, half, z.row, w), BF16), stage_out=((z.row, w), BF16),
+        slot_vec=((2, half, SLAB, 128), F32), stage_vec=((SLAB, 128), F32),
+        fin_inner=((z.rows, z.mine), BF16), got_inner=((4, z.row, z.mine), BF16),
+        fin_qkv=((z.rows, 3 * c), BF16), got_qkv=((4, z.row, 3 * c), BF16),
+        fin_out=((z.row, w), BF16), got_out=((z.row, w), BF16),
+        fin_vec=((SLAB, 128), F32), got_vec=((4, SLAB, 128), F32),
+    )
+    z.sems = 192
+    sems = pltpu.SemaphoreType.DMA((z.sems,))
+    names = list(ins) + list(outs) + list(scratch) + list(dict(send_sem=0, recv_sem=0))
+    vmem = pl.BlockSpec(memory_space=pltpu.VMEM)
+    parts = pl.pallas_call(
+        functools.partial(layer_kernel, z, names),
+        out_shape=[jax.ShapeDtypeStruct(*v) for v in outs.values()],
+        in_specs=[
+            pl.BlockSpec(memory_space=pltpu.SMEM) if v is valid_len else vmem for v in ins.values()
+        ],
+        out_specs=[vmem] * len(outs),
+        scratch_shapes=[pltpu.VMEM(*v) for v in scratch.values()]
+        + [sems, sems],
+        compiler_params=pltpu.CompilerParams(
+            collective_id=0, has_side_effects=True, vmem_limit_bytes=67043328
+        ),
+        name="layer",
+    )(*ins.values())
+    row, big = z.row, jax.ShapeDtypeStruct((n, w), F32)
+    mat = jax.ShapeDtypeStruct((row, w), F32)
+    vec = jax.ShapeDtypeStruct((1, row), F32)
+    shapes = [
+        big, big, mat, vec, mat, mat, vec, mat, vec, vec, vec,
+        jax.ShapeDtypeStruct((row, z.units), F32), jax.ShapeDtypeStruct((1, z.unit), F32),
+        jax.ShapeDtypeStruct((z.unit, w), F32), vec, vec, vec,
+    ]
+    results = pl.pallas_call(
+        functools.partial(finish_kernel, z),
+        out_shape=shapes,
+        in_specs=[vmem] * 7,
+        out_specs=[vmem] * len(shapes),
+        name="finish",
+    )(*parts)
+    results = list(results)
+    for i in (0, 1):
+        results[i] = results[i].reshape(tokens.shape)
+    for i in range(2, 17):
+        if results[i].shape[0] == 1:
+            results[i] = results[i].reshape(results[i].shape[1])
+    return tuple(results)
+
+
 def body(
     tokens,
     valid_len,
@@ -348,4 +1231,20 @@
         P(("page", "seq")),
         P(("page", "seq")),
     )
-    return jax.shard_map(body, mesh=mesh, in_specs=in_specs, out_specs=out_specs, check_vma=False)
+
+    def layer(*arrays):
+        width, units = arrays[11].shape
+        if supported(mesh, arrays[0].shape, width, units):
+            z = Sizes(mesh, width, units, arrays[0].shape[1] // mesh.shape["seq"])
+
+            def run(tokens, valid_len, *rest):
+                return paged_layer(z, tokens, valid_len, rest[:-1], rest[-1])
+
+            chosen = run
+        else:
+            chosen = body
+        return jax.shard_map(
+            chosen, mesh=mesh, in_specs=in_specs, out_specs=out_specs, check_vma=False
+        )(*arrays)
+
+    return layer

time: 1470 us -> 206 us (0.14)
  waiting for transfers between devices: 1170 us -> 0 us
  Pallas kernels: 0 us -> 205 us
  blocking collectives: 122 us -> 0 us
  matrix products: 78.5 us -> 0 us
  local copies, waits for them, and re-layouts: 59.8 us -> 0 us
  other arithmetic: 16.7 us -> 0 us
    reduce_scatter x3 -> x0, waiting for transfers between devices: 508 us -> none  [the longest x1 187 us: sequence_layer(): lax.psum_scatter(grad_wouter, ('page', 'seq'), scatter_dimension=0, tiled...]
    unnamed x21 -> x0, waiting for transfers between devices: 349 us -> none
    all_gather x8 -> x0, waiting for transfers between devices: 317 us -> none  [the longest x1 77.4 us: sequence_layer(): lax.all_gather(lowered[9], ('page', 'seq'), axis=0, tiled=True)]
    pallas_call x0 -> x2, Pallas kernels: none -> 205 us  [the longest x1 202 us: paged_layer(): pl.pallas_call(functools.partial(layer_kernel, z, names), out_shape=[jax....]
    unnamed x2 -> x0, blocking collectives: 82.9 us -> none
    dot_general x24 -> x0, matrix products: 78.5 us -> none  [the longest x6 29.1 us: product_tn(): lax.dot_general(left, right, (((0,), (0,)), ((), ())), preferred_element_...]
    unnamed x94 -> x0, local copies, waits for them, and re-layouts: 54.7 us -> none
    all_gather x1 -> x0, blocking collectives: 39.5 us -> none  [sequence_layer(): lax.all_gather(lowered[10], ('page', 'seq'), axis=0, tiled=True)]
  transfers between devices with their start and end apart: 16 -> 0, of which waited for: 15 -> 0; matrix products, arithmetic and copies ran while one was open for 8% -> 0% of each run, Pallas kernels for 0% -> 0%
where the time goes in v1:
time: 206 us
  Pallas kernels  205 us (100%)
    pallas_call x1, Pallas kernels, paged_layer(): pl.pallas_call(functools.partial(layer_kernel, z, names), out_shape=[jax....  202 us

profile of v1, /device:TPU:0, one launch (start us, length us, event | category | flops | bytes accessed | tf_op | source)
XLA Modules:
  0.0 205.9 jit_solution(3559633753305905985)
XLA Ops:
  1.3 201.5 %layer.1 = (f32[128,1024]{1,0:T(8,128)}, f32[128,1024]{1,0:T(8,128)}, f32[128,1024]{1,0:T(8,128)}, bf16[4,32,1024]{2,1,0:T(8,128)(2,1)}, bf16[4,32,768]{2,1,0:T(...) custom-call(s32[1]{0:T(128)S(6)} %copy.35.refs_0_, f32[128,1024]{1,0:T(8,128)} %bitcast.22, ...), custom_call_target="tpu_custom_call" | custom-call | tf_op jit(solution)/shard_map/layer/pallas_call | solution.py:1112
  202.8 3.1 %finish.1 = (f32[128,1024]{1,0:T(8,128)}, f32[128,1024]{1,0:T(8,128)}, f32[32,1024]{1,0:T(8,128)}, f32[1,32]{1,0:T(1,128)}, f32[32,1024]{1,0:T(8,128)}, /*index=...) custom-call(f32[128,1024]{1,0:T(8,128)} %get-tuple-element.41.out, ...), custom_call_target="tpu_custom_call" | custom-call | tf_op jit(solution)/shard_map/finish/pallas_call | solution.py:1134

commit v2 on v1

--- a/solution.py
+++ b/solution.py
@@ -386,19 +386,62 @@
 
         def copy(self, j, owner):
             piece = block(self.ref, owner, self.size)
-            return copy(piece, piece, self.first + j, (page, peer(j)))
+            return copy(piece, piece, self.first + j, (page, peer(1 if j == 3 else j)))
 
         def start(self):
-            for j in (2, 3, 1):
-                self.copy(j, part).start()
-            sent.append(lambda: [self.copy(j, part).wait_send() for j in (1, 2, 3)])
+            self.copy(2, part).start()
+            self.copy(1, part).start()
+
+        def forward(self):
+            self.copy(2, peer(2)).wait_recv()
+            self.copy(3, peer(2)).start()
+
+            def leave():
+                self.copy(1, part).wait_send()
+                self.copy(2, part).wait_send()
+                self.copy(3, peer(2)).wait_send()
+
+            sent.append(leave)
 
         def wait(self, j):
             self.copy(j, peer(j)).wait_recv()
 
-        def wait_all(self):
-            for j in (1, 2, 3):
-                self.wait(j)
+    class Combine:
+        def __init__(self, phase, make):
+            self.phase, self.make, self.first = phase, make, slots(4)
+
+        def rows(self, j):
+            return pl.ds(pl.multiple_of(peer(j) * n, n), n)
+
+        def copy(self, j):
+            return copy(
+                r.part_out.at[self.phase, self.rows(j)],
+                r.part_in.at[self.phase, j],
+                self.first + j,
+                (page, peer(2 if j == 2 else 1)),
+            )
+
+        def term(self, j):
+            value = self.make(self.rows(j))
+            if j == 0:
+                r.part_own[...] = value
+                return
+            if j == 2:
+                self.copy(3).wait_recv()
+                value = value + r.part_in[self.phase, 3].astype(F32)
+            r.part_out[self.phase, self.rows(j), :] = value.astype(BF16)
+            self.copy(j).start()
+            sent.append(lambda: self.copy(j).wait_send())
+
+        def wait(self):
+            for j in (1, 2):
+                self.copy(j).wait_recv()
+
+        def total(self, rows):
+            total = r.part_own[rows, :]
+            for j in (1, 2):
+                total = total + r.part_in[self.phase, j, rows, :].astype(F32)
+            return total
 
     class Spread:
         def __init__(self, src, dst, size):
@@ -412,14 +455,9 @@
                 (page, peer(j)),
             )
 
-        def start(self, j):
-            self.copy(j).start()
-
-        def start_all(self):
+        def start(self):
             for j in (2, 3, 1):
-                self.start(j)
-
-        def finish(self):
+                self.copy(j).start()
             sent.append(lambda: [self.copy(j).wait_send() for j in (1, 2, 3)])
 
         def wait(self, j):
@@ -447,102 +485,127 @@
                 self.copy(j, peer(j)).wait_recv()
 
     class Gather:
-        def __init__(self, ref, size):
-            self.ref, self.size = ref, size
-            self.first = slots(2 * z.half)
-
-        def copy(self, t, d, index):
-            piece = block(self.ref, page_at(index), self.size)
+        def __init__(self, ref, size, pieces=1):
+            self.ref, self.size, self.pieces = ref, size, pieces
+            self.first = slots(2 * z.half * pieces)
+
+        def copy(self, t, d, k, index):
+            height = self.size // self.pieces
+            start = k * height
             if t == z.half - 1:
-                h = self.size // 2
-                piece = piece.at[pl.ds(d * h, h)]
+                height = height // 2
+                start = start + d * height
+            piece = block(self.ref, page_at(index), self.size).at[pl.ds(start, height)]
             return copy(
-                piece, piece, self.first + 2 * t + d, (page_at(place + 1 - 2 * d), part)
+                piece,
+                piece,
+                self.first + (t * self.pieces + k) * 2 + d,
+                (page_at(place + 1 - 2 * d), part),
             )
 
-        def wait(self, t):
-            for d in (0, 1):
-                self.copy(t, d, place - (1 - 2 * d) * (1 + t)).wait_recv()
+        def wait(self, t, k, d):
+            self.copy(t, d, k, place - (1 - 2 * d) * (1 + t)).wait_recv()
 
         def step(self, t):
-            if t > 0:
-                self.wait(t - 1)
-            for d in (0, 1):
-                self.copy(t, d, place - (1 - 2 * d) * t).start()
-                sent.append(
-                    functools.partial(
-                        lambda t, d: self.copy(t, d, place - (1 - 2 * d) * t).wait_send(), t, d
-                    )
-                )
+            for k in range(self.pieces):
+                for d in (0, 1):
+                    if t > 0:
+                        self.wait(t - 1, k, d)
+                    self.copy(t, d, k, place - (1 - 2 * d) * t).start()
+                    sent.append(functools.partial(self.leave, t, k, d))
+
+        def leave(self, t, k, d):
+            self.copy(t, d, k, place - (1 - 2 * d) * t).wait_send()
 
         def done(self):
-            self.wait(z.half - 1)
+            for k in range(self.pieces):
+                for d in (0, 1):
+                    self.wait(z.half - 1, k, d)
 
     class Reduce:
-        def __init__(self, slot, stage, local, shape, kind):
+        def __init__(self, slot, stage, local, shape, kind, pieces=1):
             self.slot, self.stage, self.local = slot, stage, local
-            self.size, self.kind = shape[0], kind
-            self.first = slots(2 * z.half)
-
-        def copy(self, t, d):
+            self.size, self.kind, self.pieces = shape[0], kind, pieces
+            self.wide = shape[1] // pieces
+            self.first = slots(2 * z.half * pieces)
+
+        def copy(self, t, d, k):
             h = self.size // 2
             if t == 0:
-                src = self.stage.at[pl.ds(d * h, h)]
-                dst = self.slot.at[d, 0, pl.ds(d * h, h)]
+                src = self.stage.at[k, pl.ds(d * h, h)]
+                dst = self.slot.at[k, d, 0, pl.ds(d * h, h)]
             else:
-                src = self.slot.at[d, t - 1]
-                dst = self.slot.at[d, t]
-            return copy(src, dst, self.first + 2 * t + d, (page_at(place + 1 - 2 * d), part))
+                src = self.slot.at[k, d, t - 1]
+                dst = self.slot.at[k, d, t]
+            return copy(
+                src,
+                dst,
+                self.first + (t * self.pieces + k) * 2 + d,
+                (page_at(place + 1 - 2 * d), part),
+            )
+
+        def leave(self, t, d, k):
+            self.copy(t, d, k).wait_send()
 
         def step(self, t):
             h = self.size // 2
+            wide = self.wide
             if t == 0:
-                self.stage[...] = self.local(page_at(place + z.half)).astype(self.kind)
+                term = self.local(page_at(place + z.half)).astype(self.kind)
+                for k in range(self.pieces):
+                    self.stage[k] = term[:, k * wide : (k + 1) * wide]
+            else:
+                terms = [
+                    self.local(page_at(place + (1 - 2 * d) * (z.half - t))) for d in (0, 1)
+                ]
+            for k in range(self.pieces):
                 for d in (0, 1):
-                    self.copy(0, d).start()
-            else:
+                    if t > 0:
+                        term = terms[d][:, k * wide : (k + 1) * wide]
+                        self.copy(t - 1, d, k).wait_recv()
+                        held = self.slot.at[k, d, t - 1]
+                        if t == 1:
+                            near, far = pl.ds(d * h, h), pl.ds((1 - d) * h, h)
+                            term_near = term[d * h : (d + 1) * h]
+                            term_far = term[(1 - d) * h : (2 - d) * h]
+                            held[near] = (held[near].astype(F32) + term_near).astype(self.kind)
+                            held[far] = term_far.astype(self.kind)
+                        else:
+                            held[...] = (held[...].astype(F32) + term).astype(self.kind)
+                    self.copy(t, d, k).start()
+                    sent.append(functools.partial(self.leave, t, d, k))
+
+        def total(self, out):
+            term = self.local(page)
+            last = z.half - 1
+            for k in range(self.pieces):
                 for d in (0, 1):
-                    term = self.local(page_at(place + (1 - 2 * d) * (z.half - t)))
-                    self.copy(t - 1, d).wait_recv()
-                    held = self.slot.at[d, t - 1]
-                    if t == 1:
-                        near, far = pl.ds(d * h, h), pl.ds((1 - d) * h, h)
-                        part_near = term[d * h : (d + 1) * h]
-                        part_far = term[(1 - d) * h : (2 - d) * h]
-                        held[near] = (held[near].astype(F32) + part_near).astype(self.kind)
-                        held[far] = part_far.astype(self.kind)
-                    else:
-                        held[...] = (held[...].astype(F32) + term).astype(self.kind)
-                    self.copy(t, d).start()
-            for d in (0, 1):
-                sent.append(functools.partial(lambda t, d: self.copy(t, d).wait_send(), t, d))
-
-        def total(self):
-            term = self.local(page)
-            for d in (0, 1):
-                self.copy(z.half - 1, d).wait_recv()
-            last = z.half - 1
-            return term + self.slot[0, last].astype(F32) + self.slot[1, last].astype(F32)
+                    self.copy(last, d, k).wait_recv()
+                at = slice(k * self.wide, (k + 1) * self.wide)
+                out[:, at] = (
+                    term[:, at] + self.slot[k, 0, last].astype(F32) + self.slot[k, 1, last].astype(F32)
+                ).astype(out.dtype)
 
     c, w, n = z.cols, z.width, z.span
     for q in range(z.parts):
         rows = pl.ds(q * z.row, z.row)
         for i, weight in enumerate((r.w_query, r.w_key, r.w_value)):
             r.cut_qkv[rows, i * c : (i + 1) * c] = weight[:, q * c : (q + 1) * c].astype(BF16)
-        for g in range(z.pages):
-            at = (z.parts * g + q) * z.unit
-            r.cut_inner[rows, g * z.unit : (g + 1) * z.unit] = r.w_inner[
-                :, at : at + z.unit
-            ].astype(BF16)
-    r.own_out[...] = r.w_out[...].astype(BF16)
-    r.tok_all[pl.ds(pl.multiple_of(part * n, n), n), :] = r.tokens[...].astype(BF16)
     base = pl.multiple_of(rank * SLAB, SLAB)
     for i, small in enumerate(
         (r.b_query, r.b_value, r.b_out, r.g_attn, r.s_attn, r.b_outer, r.g_final, r.s_final)
     ):
         r.vec_all[pl.ds(base + i, 1), 0 : z.row] = small[...]
     r.vec_all[pl.ds(base + VECTORS, 1), :] = r.b_inner[...]
-
+    r.outer_w[pl.ds(pl.multiple_of(page * z.unit, z.unit), z.unit), :] = r.w_outer[...].astype(
+        BF16
+    )
+
+    ring_qkv = Gather(r.qkv_w, z.rows, 2)
+    ring_vec = Gather(r.vec_all, z.parts * SLAB)
+    ring_inner = Gather(r.inner_w, z.rows, 2)
+    ring_out = Gather(r.out_w, z.row)
+    ring_outer = Gather(r.outer_w, z.unit, 2)
     cut_qkv = Place(r.cut_qkv, r.qkv_w, z.row, page * z.parts)
     cut_inner = Place(r.cut_inner, r.inner_w, z.row, page * z.parts)
     share_tok = Share(r.tok_all, n)
@@ -557,61 +620,59 @@
     vec_share = ShareVec()
     hold = slots(1)
 
-    def hold_copy():
-        return copy(
-            r.own_out, block(r.out_w, own_slot_page, z.row), hold, (hold_page, hold_part)
-        )
-
-    own_slot_page = hold_page
+    def hold_copy(slot):
+        return copy(r.own_out, block(r.out_w, slot, z.row), hold, (hold_page, hold_part))
+
     pl.semaphore_wait(barrier, 5 + 2 * moves)
     cut_qkv.start()
     for j in (2, 3, 1):
         vec_share.copy(j, part).start()
     sent.append(lambda: [vec_share.copy(j, part).wait_send() for j in (1, 2, 3)])
-    share_tok.start()
+    ring_outer.step(0)
+    r.own_out[...] = r.w_out[...].astype(BF16)
 
     @pl.when(moves == 1)
     def _():
-        hold_copy().start()
+        hold_copy(hold_page).start()
 
     @pl.when(moves == 0)
     def _():
         r.out_w[pl.ds(pl.multiple_of(page * z.row, z.row), z.row), :] = r.own_out[...]
 
+    r.tok_all[pl.ds(pl.multiple_of(part * n, n), n), :] = r.tokens[...].astype(BF16)
+    share_tok.start()
+    for q in range(z.parts):
+        rows = pl.ds(q * z.row, z.row)
+        for g in range(z.pages):
+            at = (z.parts * g + q) * z.unit
+            r.cut_inner[rows, g * z.unit : (g + 1) * z.unit] = r.w_inner[
+                :, at : at + z.unit
+            ].astype(BF16)
     cut_inner.start()
     own_rows = pl.ds(pl.multiple_of(rank * z.row, z.row), z.row)
     cut_rows = pl.ds(pl.multiple_of(part * z.row, z.row), z.row)
     r.qkv_w[own_rows, :] = r.cut_qkv[cut_rows, :]
     r.inner_w[own_rows, :] = r.cut_inner[cut_rows, :]
-    r.outer_w[pl.ds(pl.multiple_of(page * z.unit, z.unit), z.unit), :] = r.w_outer[
-        ...
-    ].astype(BF16)
-
-    ring_qkv = Gather(r.qkv_w, z.rows)
-    ring_vec = Gather(r.vec_all, z.parts * SLAB)
-    ring_inner = Gather(r.inner_w, z.rows)
-    ring_out = Gather(r.out_w, z.row)
-    ring_outer = Gather(r.outer_w, z.unit)
 
     cut_qkv.wait()
     ring_qkv.step(0)
     for j in (1, 2, 3):
         vec_share.copy(j, peer(j)).wait_recv()
     ring_vec.step(0)
+
+    @pl.when(moves == 1)
+    def _():
+        hold_copy(page).wait_recv()
+
+    ring_out.step(0)
     for t in range(1, z.half):
         ring_qkv.step(t)
         ring_vec.step(t)
-
-    @pl.when(moves == 1)
-    def _():
-        copy(
-            r.own_out, block(r.out_w, page, z.row), hold, (hold_page, hold_part)
-        ).wait_recv()
-
-    ring_out.step(0)
+        ring_out.step(t)
+        if t == 1:
+            share_tok.forward()
     cut_inner.wait()
     ring_inner.step(0)
-    ring_qkv.done()
     ring_vec.done()
 
     lane = lax.broadcasted_iota(jnp.int32, (VECTORS, 128), 1)
@@ -632,7 +693,9 @@
 
     my_cols = pl.ds(pl.multiple_of(part * c, c), c)
 
-    share_tok.wait_all()
+    share_tok.wait(1)
+    share_tok.wait(3)
+    ring_qkv.done()
 
     def make_qkv(b, carry):
         rows = pl.ds(pl.multiple_of(b * n, n), n)
@@ -643,7 +706,6 @@
         return carry
 
     lax.fori_loop(0, z.parts, make_qkv, 0)
-    ring_out.step(1)
     ring_inner.step(1)
 
     scale = HEAD_DIM ** (-0.5)
@@ -678,44 +740,18 @@
         lax.fori_loop(0, z.parts, body, 0)
 
     attend(0)
-    ring_out.step(2)
     ring_inner.step(2)
-    ring_outer.step(0)
+    ring_outer.step(1)
     attend(1)
-    ring_out.step(3)
+    ring_out.done()
+
+    combine = Combine(0, lambda rows: dot_nn(r.ctx[rows, :], r.out_w[...]))
+    combine.term(3)
+    combine.term(2)
     ring_inner.step(3)
-    ring_outer.step(1)
-    ring_out.done()
-
-    def partial_rows(phase, make):
-        spread = Spread(r.part_out.at[phase], r.part_in.at[phase], n)
-
-        def body(i, carry):
-            j = (i + 1) % 4
-            b = peer(j)
-            rows = pl.ds(pl.multiple_of(b * n, n), n)
-            term = make(rows, j)
-
-            @pl.when(j > 0)
-            def _():
-                r.part_out[phase, rows, :] = term.astype(BF16)
-                spread.start(j)
-
-            @pl.when(j == 0)
-            def _():
-                r.part_own[...] = term
-
-            return carry
-
-        lax.fori_loop(0, z.parts, body, 0)
-        spread.finish()
-        return spread
-
-    def row_sum(phase, rows):
-        total = r.part_own[rows, :]
-        for j in (1, 2, 3):
-            total = total + r.part_in[phase, j, rows, :].astype(F32)
-        return total
+    ring_outer.step(2)
+    combine.term(1)
+    combine.term(0)
 
     def by_rows(fn):
         size = 32
@@ -731,15 +767,12 @@
 
     r.sums[...] = jnp.zeros_like(r.sums)
 
-    spread = partial_rows(0, lambda rows, j: dot_nn(r.ctx[rows, :], r.out_w[...]))
-    ring_outer.step(2)
-    for j in (1, 2, 3):
-        spread.wait(j)
+    combine.wait()
 
     share_hid = Share(r.hid_all, n)
 
     def first_norm(rows, at):
-        mixed = r.tokens[rows, :] + (row_sum(0, rows) + vector(2))
+        mixed = r.tokens[rows, :] + (combine.total(rows) + vector(2))
         normed, inverse = norm_parts(mixed)
         hidden = normed * vector(3) + vector(4)
         r.norm_one[rows, :] = normed
@@ -752,13 +785,10 @@
     ring_outer.step(3)
     ring_inner.done()
 
-    def make_inner(j, carry):
-        @pl.when(j > 0)
-        def _():
-            share_hid.copy(j, peer(j)).wait_recv()
-
+    tile = 256
+
+    def make_inner(j):
         rows = pl.ds(pl.multiple_of(peer(j) * n, n), n)
-        tile = 256
 
         def columns(i, carry):
             cols = pl.ds(pl.multiple_of(i * tile, tile), tile)
@@ -768,18 +798,25 @@
             r.slope[rows, cols] = slope
             return carry
 
-        return lax.fori_loop(0, z.mine // tile, columns, carry)
-
-    lax.fori_loop(0, z.parts, make_inner, 0)
+        lax.fori_loop(0, z.mine // tile, columns, 0)
+
+    make_inner(0)
+    share_hid.wait(1)
+    make_inner(1)
+    share_hid.forward()
+    make_inner(2)
+    share_hid.wait(3)
+    make_inner(3)
     ring_outer.done()
-    spread = partial_rows(1, lambda rows, j: dot_nn(r.active[rows, :], r.outer_w[...]))
-    for j in (1, 2, 3):
-        spread.wait(j)
+    combine_two = Combine(1, lambda rows: dot_nn(r.active[rows, :], r.outer_w[...]))
+    for j in (3, 2, 1, 0):
+        combine_two.term(j)
+    combine_two.wait()
 
     share_gf = Share(r.gf_all, n)
 
     def second_norm(rows, at):
-        outer = row_sum(1, rows) + vector(5)
+        outer = combine_two.total(rows) + vector(5)
         normed, inverse = norm_parts(r.hidden[rows, :] + outer)
         r.o_out[rows, :] = normed * vector(6) + vector(7)
         grad = r.out_grad[rows, :]
@@ -802,15 +839,15 @@
         return local
 
     reduce_outer = Reduce(
-        r.slot_outer, r.stage_outer, chunk_term(r.active, r.gf_all, z.unit), (z.unit, w), BF16
+        r.slot_outer, r.stage_outer, chunk_term(r.active, r.gf_all, z.unit), (z.unit, w), BF16, 2
     )
     reduce_inner = Reduce(
         r.slot_inner, r.stage_inner, chunk_term(r.hid_all, r.grad_inner, z.rows),
-        (z.rows, z.mine), BF16,
+        (z.rows, z.mine), BF16, 2
     )
     reduce_qkv = Reduce(
         r.slot_qkv, r.stage_qkv, chunk_term(r.tok_all, r.grad_qkv, z.rows),
-        (z.rows, 3 * c), BF16,
+        (z.rows, 3 * c), BF16, 2
     )
     reduce_out = Reduce(
         r.slot_out, r.stage_out,
@@ -823,12 +860,8 @@
 
     r.b_sum[...] = jnp.zeros_like(r.b_sum)
 
-    def make_grad_inner(rows, j):
-        @pl.when(j > 0)
-        def _():
-            share_gf.copy(j, peer(j)).wait_recv()
-
-        tile = 256
+    def make_grad_inner(j):
+        rows = pl.ds(pl.multiple_of(peer(j) * n, n), n)
 
         def columns(i, carry):
             cols = pl.ds(pl.multiple_of(i * tile, tile), tile)
@@ -839,18 +872,30 @@
             return carry
 
         lax.fori_loop(0, z.mine // tile, columns, 0)
-        return dot_nt(r.grad_inner[rows, :], r.inner_w[...])
-
-    spread = partial_rows(2, make_grad_inner)
+
+    make_grad_inner(0)
+    share_gf.wait(1)
+    make_grad_inner(1)
+    share_gf.forward()
+    share_gf.wait(3)
     reduce_outer.step(0)
+    make_grad_inner(2)
+    make_grad_inner(3)
+    combine_three = Combine(2, lambda rows: dot_nt(r.grad_inner[rows, :], r.inner_w[...]))
+    combine_three.term(3)
+    combine_three.term(2)
+    reduce_outer.step(1)
     reduce_inner.step(0)
-    for j in (1, 2, 3):
-        spread.wait(j)
+    combine_three.term(1)
+    combine_three.term(0)
+    reduce_outer.step(2)
+    reduce_inner.step(1)
+    combine_three.wait()
 
     share_ga = Share(r.ga_all, n)
 
     def first_norm_back(rows, at):
-        grad = r.grad_sum[rows, :] + row_sum(2, rows)
+        grad = r.grad_sum[rows, :] + combine_three.total(rows)
         normed = r.norm_one[rows, :]
         add_column_sum(3, grad * normed)
         add_column_sum(4, grad)
@@ -862,19 +907,20 @@
 
     by_rows(first_norm_back)
     share_ga.start()
-    reduce_outer.step(1)
-    reduce_inner.step(1)
-
-    def make_grad_ctx(j, carry):
-        @pl.when(j > 0)
-        def _():
-            share_ga.copy(j, peer(j)).wait_recv()
-
+
+    def make_grad_ctx(j):
         rows = pl.ds(pl.multiple_of(peer(j) * n, n), n)
         r.grad_ctx[rows, :] = dot_nt(r.ga_all[rows, :], r.out_w[...]).astype(BF16)
-        return carry
-
-    lax.fori_loop(0, z.parts, make_grad_ctx, 0)
+
+    make_grad_ctx(0)
+    share_ga.wait(1)
+    make_grad_ctx(1)
+    reduce_outer.step(3)
+    reduce_inner.step(2)
+    share_ga.forward()
+    make_grad_ctx(2)
+    share_ga.wait(3)
+    make_grad_ctx(3)
     r.term_out[...] = dot_tn(r.ctx[...], r.ga_all[...])
     reduce_out.step(0)
 
@@ -909,14 +955,11 @@
         r.grad_qkv[:, pair_cols(2, pair)] = r.grad_kv[1].astype(BF16)
 
     attend_back(0)
-    reduce_outer.step(2)
-    reduce_inner.step(2)
+    reduce_inner.step(3)
     reduce_out.step(1)
     attend_back(1)
-    reduce_outer.step(3)
-    reduce_inner.step(3)
+    reduce_qkv.step(0)
     reduce_out.step(2)
-    reduce_qkv.step(0)
 
     r.sums[0:1, my_cols] = jnp.sum(r.grad_qkv[:, 0:c].astype(F32), axis=0, keepdims=True)
     r.sums[1:2, my_cols] = jnp.sum(r.grad_qkv[:, 2 * c :].astype(F32), axis=0, keepdims=True)
@@ -928,26 +971,28 @@
         ]
     reduce_vec.step(0)
 
-    spread = partial_rows(3, lambda rows, j: dot_nt(r.grad_qkv[rows, :], r.qkv_w[...]))
-    reduce_out.step(3)
+    combine_four = Combine(3, lambda rows: dot_nt(r.grad_qkv[rows, :], r.qkv_w[...]))
+    combine_four.term(3)
+    combine_four.term(2)
     reduce_qkv.step(1)
     reduce_vec.step(1)
-
-    r.o_outer[...] = reduce_outer.total()
-    r.fin_inner[...] = reduce_inner.total().astype(BF16)
+    reduce_out.step(3)
+    combine_four.term(1)
+    combine_four.term(0)
+
+    reduce_outer.total(r.o_outer)
+    reduce_inner.total(r.fin_inner)
     fin_inner = Spread(r.fin_inner, r.got_inner, z.row)
-    fin_inner.start_all()
-    fin_inner.finish()
+    fin_inner.start()
     reduce_qkv.step(2)
     reduce_vec.step(2)
-    for j in (1, 2, 3):
-        spread.wait(j)
+    combine_four.wait()
 
     def input_rows(rows, at):
-        r.o_grad[rows, :] = r.grad_mixed[rows, :] + row_sum(3, rows)
+        r.o_grad[rows, :] = r.grad_mixed[rows, :] + combine_four.total(rows)
 
     by_rows(input_rows)
-    r.fin_out[...] = reduce_out.total().astype(BF16)
+    reduce_out.total(r.fin_out)
     home = slots(1)
 
     def home_copy():
@@ -963,7 +1008,7 @@
 
     reduce_qkv.step(3)
     reduce_vec.step(3)
-    r.fin_vec[...] = reduce_vec.total()
+    reduce_vec.total(r.fin_vec)
 
     class VecAll:
         first = slots(4)
@@ -975,10 +1020,9 @@
     for j in (2, 3, 1):
         fin_vec.copy(j).start()
     sent.append(lambda: [fin_vec.copy(j).wait_send() for j in (1, 2, 3)])
-    r.fin_qkv[...] = reduce_qkv.total().astype(BF16)
+    reduce_qkv.total(r.fin_qkv)
     fin_qkv = Spread(r.fin_qkv, r.got_qkv, z.row)
-    fin_qkv.start_all()
-    fin_qkv.finish()
+    fin_qkv.start()
 
     my_rows = pl.ds(pl.multiple_of(part * z.row, z.row), z.row)
 
@@ -1009,7 +1053,7 @@
 
     @pl.when(moves == 1)
     def _():
-        hold_copy().wait_send()
+        hold_copy(hold_page).wait_send()
         home_copy().wait_send()
 
     assert counter[0] <= z.sems, counter[0]
@@ -1095,11 +1139,11 @@
         b_sum=((1, z.mine), F32),
         term_out=((c, w), F32),
         term_vec=((z.pages * SLAB, 128), F32),
-        slot_outer=((2, half, z.unit, w), BF16), stage_outer=((z.unit, w), BF16),
-        slot_inner=((2, half, z.rows, z.mine), BF16), stage_inner=((z.rows, z.mine), BF16),
-        slot_qkv=((2, half, z.rows, 3 * c), BF16), stage_qkv=((z.rows, 3 * c), BF16),
-        slot_out=((2, half, z.row, w), BF16), stage_out=((z.row, w), BF16),
-        slot_vec=((2, half, SLAB, 128), F32), stage_vec=((SLAB, 128), F32),
+        slot_outer=((2, 2, half, z.unit, w // 2), BF16), stage_outer=((2, z.unit, w // 2), BF16),
+        slot_inner=((2, 2, half, z.rows, z.mine // 2), BF16), stage_inner=((2, z.rows, z.mine // 2), BF16),
+        slot_qkv=((2, 2, half, z.rows, 3 * c // 2), BF16), stage_qkv=((2, z.rows, 3 * c // 2), BF16),
+        slot_out=((1, 2, half, z.row, w // 1), BF16), stage_out=((1, z.row, w // 1), BF16),
+        slot_vec=((1, 2, half, SLAB, 128 // 1), F32), stage_vec=((1, SLAB, 128 // 1), F32),
         fin_inner=((z.rows, z.mine), BF16), got_inner=((4, z.row, z.mine), BF16),
         fin_qkv=((z.rows, 3 * c), BF16), got_qkv=((4, z.row, 3 * c), BF16),
         fin_out=((z.row, w), BF16), got_out=((z.row, w), BF16),

time: 206 us -> 178 us (0.86)
  Pallas kernels: 205 us -> 176 us
    pallas_call x1, Pallas kernels: 202 us -> 173 us  [paged_layer(): pl.pallas_call(functools.partial(layer_kernel, z, names), out_shape=[jax....]
where the time goes in v2:
time: 178 us; the launch traced here: 177 us
  Pallas kernels  176 us (99%)
    pallas_call x1, Pallas kernels, paged_layer(): pl.pallas_call(functools.partial(layer_kernel, z, names), out_shape=[jax....  173 us

profile of v2, /device:TPU:0, one launch (start us, length us, event | category | flops | bytes accessed | tf_op | source)
XLA Modules:
  0.0 177.3 jit_solution(18354248185035751640)
XLA Ops:
  1.3 172.8 %layer.1 = (f32[128,1024]{1,0:T(8,128)}, f32[128,1024]{1,0:T(8,128)}, f32[128,1024]{1,0:T(8,128)}, bf16[4,32,1024]{2,1,0:T(8,128)(2,1)}, bf16[4,32,768]{2,1,0:T(...) custom-call(s32[1]{0:T(128)S(6)} %copy.35.refs_0_, f32[128,1024]{1,0:T(8,128)} %bitcast.22, ...), custom_call_target="tpu_custom_call" | custom-call | tf_op jit(solution)/shard_map/layer/pallas_call | solution.py:1156
  174.1 3.1 %finish.1 = (f32[128,1024]{1,0:T(8,128)}, f32[128,1024]{1,0:T(8,128)}, f32[32,1024]{1,0:T(8,128)}, f32[1,32]{1,0:T(1,128)}, f32[32,1024]{1,0:T(8,128)}, /*index=...) custom-call(f32[128,1024]{1,0:T(8,128)} %get-tuple-element.41.out, ...), custom_call_target="tpu_custom_call" | custom-call | tf_op jit(solution)/shard_map/finish/pallas_call | solution.py:1178

commit v3 on v2

--- a/solution.py
+++ b/solution.py
@@ -322,11 +322,10 @@
 
 def layer_kernel(z, names, *refs):
     r = types.SimpleNamespace(**dict(zip(names, refs)))
-    send_sem, recv_sem = r.send_sem, r.recv_sem
+    send_sem, recv_sem, load_sem = r.send_sem, r.recv_sem, r.load_sem
     page = lax.axis_index("page")
     part = lax.axis_index("seq")
     counter = [0]
-    sent = []
 
     def slots(count):
         first = counter[0]
@@ -337,12 +336,20 @@
     place = odd * (z.pages - 1 - page // 2) + (1 - odd) * (page // 2)
 
     def page_at(index):
-        index = (index + 2 * z.pages) % z.pages
+        index = (index + z.pages) % z.pages
         late = index // z.half
         return (1 - late) * (2 * index) + late * (2 * z.pages - 1 - 2 * index)
 
+    ring = [page] + [page_at(place + step) for step in range(1, z.pages)]
+    peers = [part] + [
+        ((part // 2 + j // 2) % 2) * 2 + (part % 2 + j % 2) % 2 for j in range(1, 4)
+    ]
+
+    def around(step):
+        return ring[step % z.pages]
+
     def peer(j):
-        return ((part // 2 + j // 2) % 2) * 2 + (part % 2 + j % 2) % 2
+        return peers[j]
 
     rank = page * z.parts + part
     hold_page, hold_part = rank % z.pages, rank // z.pages
@@ -352,15 +359,41 @@
         1 - jnp.minimum(1, (hold_part - part) * (hold_part - part))
     )
 
-    def copy(src, dst, index, device):
-        return pltpu.make_async_remote_copy(
-            src_ref=src,
-            dst_ref=dst,
-            send_sem=send_sem.at[index],
-            recv_sem=recv_sem.at[index],
-            device_id=device,
-            device_id_type=MESH,
-        )
+    class Copy:
+        def __init__(self, src, dst, index, device, group=None):
+            self.args = src, dst, index, device
+            self.group = group
+
+        def made(self, group):
+            src, dst, index, device = self.args
+            return pltpu.make_async_remote_copy(
+                src_ref=src,
+                dst_ref=dst,
+                send_sem=send_sem.at[group],
+                recv_sem=recv_sem.at[index],
+                device_id=device,
+                device_id_type=MESH,
+            )
+
+        def start(self):
+            group = self.group
+            if group is None:
+                src = self.args[0]
+                size = math.prod(src.shape) * jnp.dtype(src.dtype).itemsize
+                if groups[-1] + size > z.group_bytes:
+                    groups.append(0)
+                groups[-1] += size
+                group = 2 + len(groups) - 1
+            self.made(group).start()
+
+        def wait_recv(self):
+            self.made(0).wait_recv()
+
+        def wait_send(self):
+            self.made(self.group).wait_send()
+
+    groups = [0]
+    copy = Copy
 
     def block(ref, index, size):
         return ref.at[pl.ds(pl.multiple_of(index * size, size), size)]
@@ -372,8 +405,8 @@
 
     for j in (1, 2, 3):
         greet((page, peer(j)))
-    greet((page_at(place + 1), part))
-    greet((page_at(place - 1), part))
+    greet((around(1), part))
+    greet((around(-1), part))
 
     @pl.when(moves == 1)
     def _():
@@ -381,71 +414,83 @@
         greet((own_page, own_part))
 
     class Share:
-        def __init__(self, ref, size):
-            self.ref, self.size, self.first = ref, size, slots(4)
-
-        def copy(self, j, owner):
-            piece = block(self.ref, owner, self.size)
-            return copy(piece, piece, self.first + j, (page, peer(1 if j == 3 else j)))
-
-        def start(self):
-            self.copy(2, part).start()
-            self.copy(1, part).start()
+        def __init__(self, ref, size, pieces=2):
+            self.ref, self.size, self.pieces = ref, size, pieces
+            self.first = slots(3 * pieces) - 1
+
+        def copy(self, j, owner, k):
+            height = self.size // self.pieces
+            piece = block(self.ref, owner, self.size).at[pl.ds(k * height, height)]
+            return copy(piece, piece, self.first + 3 * k + j, (page, peer(1 if j == 3 else j)))
+
+        def start(self, k):
+            self.copy(2, part, k).start()
+            self.copy(1, part, k).start()
 
         def forward(self):
-            self.copy(2, peer(2)).wait_recv()
-            self.copy(3, peer(2)).start()
-
-            def leave():
-                self.copy(1, part).wait_send()
-                self.copy(2, part).wait_send()
-                self.copy(3, peer(2)).wait_send()
-
-            sent.append(leave)
+            for k in range(self.pieces):
+                self.copy(2, peer(2), k).wait_recv()
+                self.copy(3, peer(2), k).start()
+
 
         def wait(self, j):
-            self.copy(j, peer(j)).wait_recv()
+            for k in range(self.pieces):
+                self.copy(j, peer(j), k).wait_recv()
 
     class Combine:
-        def __init__(self, phase, make):
-            self.phase, self.make, self.first = phase, make, slots(4)
-
-        def rows(self, j):
-            return pl.ds(pl.multiple_of(peer(j) * n, n), n)
-
-        def copy(self, j):
+        def __init__(self, phase, make, pieces=2):
+            self.phase, self.make, self.pieces = phase, make, pieces
+            self.first = slots(3 * pieces) - 1
+
+        def copy(self, j, k):
+            height = n // self.pieces
+            at = pl.multiple_of(peer(j) * n + k * height, height)
             return copy(
-                r.part_out.at[self.phase, self.rows(j)],
-                r.part_in.at[self.phase, j],
-                self.first + j,
+                r.part_out.at[self.phase, pl.ds(at, height)],
+                r.part_in.at[self.phase, j, pl.ds(k * height, height)],
+                self.first + 3 * k + j,
                 (page, peer(2 if j == 2 else 1)),
             )
 
         def term(self, j):
-            value = self.make(self.rows(j))
+            value = self.make(pl.ds(pl.multiple_of(peer(j) * n, n), n))
             if j == 0:
                 r.part_own[...] = value
                 return
-            if j == 2:
-                self.copy(3).wait_recv()
-                value = value + r.part_in[self.phase, 3].astype(F32)
-            r.part_out[self.phase, self.rows(j), :] = value.astype(BF16)
-            self.copy(j).start()
-            sent.append(lambda: self.copy(j).wait_send())
-
-        def wait(self):
-            for j in (1, 2):
-                self.copy(j).wait_recv()
-
-        def total(self, rows):
-            total = r.part_own[rows, :]
-            for j in (1, 2):
-                total = total + r.part_in[self.phase, j, rows, :].astype(F32)
-            return total
+            height = n // self.pieces
+            for k in range(self.pieces):
+                rows = slice(k * height, (k + 1) * height)
+                mine = value[rows]
+                if j == 2:
+                    self.copy(3, k).wait_recv()
+                    mine = mine + r.part_in[self.phase, 3, rows, :].astype(F32)
+                at = pl.multiple_of(peer(j) * n + k * height, height)
+                r.part_out[self.phase, pl.ds(at, height), :] = mine.astype(BF16)
+                self.copy(j, k).start()
+
+
+        def finish(self, fn, after=None):
+            height, size = n // self.pieces, 32
+            for k in range(self.pieces):
+                for j in (1, 2):
+                    self.copy(j, k).wait_recv()
+
+                def body(i, carry):
+                    at = pl.multiple_of(k * height + i * size, size)
+                    rows = pl.ds(at, size)
+                    total = r.part_own[rows, :]
+                    for j in (1, 2):
+                        total = total + r.part_in[self.phase, j, rows, :].astype(F32)
+                    fn(rows, at, total)
+                    return carry
+
+                lax.fori_loop(0, height // size, body, 0)
+                if after is not None:
+                    after(k)
 
     class Spread:
         def __init__(self, src, dst, size):
-            self.src, self.dst, self.size, self.first = src, dst, size, slots(4)
+            self.src, self.dst, self.size, self.first = src, dst, size, slots(3) - 1
 
         def copy(self, j):
             return copy(
@@ -458,14 +503,13 @@
         def start(self):
             for j in (2, 3, 1):
                 self.copy(j).start()
-            sent.append(lambda: [self.copy(j).wait_send() for j in (1, 2, 3)])
 
         def wait(self, j):
             self.copy(j).wait_recv()
 
     class Place:
         def __init__(self, src, dst, size, base):
-            self.src, self.dst, self.size, self.base, self.first = src, dst, size, base, slots(4)
+            self.src, self.dst, self.size, self.base, self.first = src, dst, size, base, slots(3) - 1
 
         def copy(self, j, owner):
             return copy(
@@ -478,7 +522,6 @@
         def start(self):
             for j in (2, 3, 1):
                 self.copy(j, part).start()
-            sent.append(lambda: [self.copy(j, part).wait_send() for j in (1, 2, 3)])
 
         def wait(self):
             for j in (1, 2, 3):
@@ -489,33 +532,30 @@
             self.ref, self.size, self.pieces = ref, size, pieces
             self.first = slots(2 * z.half * pieces)
 
-        def copy(self, t, d, k, index):
+        def copy(self, t, d, k, step):
             height = self.size // self.pieces
             start = k * height
             if t == z.half - 1:
                 height = height // 2
                 start = start + d * height
-            piece = block(self.ref, page_at(index), self.size).at[pl.ds(start, height)]
+            piece = block(self.ref, around(step), self.size).at[pl.ds(start, height)]
             return copy(
                 piece,
                 piece,
                 self.first + (t * self.pieces + k) * 2 + d,
-                (page_at(place + 1 - 2 * d), part),
+                (around(1 - 2 * d), part),
             )
 
         def wait(self, t, k, d):
-            self.copy(t, d, k, place - (1 - 2 * d) * (1 + t)).wait_recv()
+            self.copy(t, d, k, -(1 - 2 * d) * (1 + t)).wait_recv()
 
         def step(self, t):
             for k in range(self.pieces):
                 for d in (0, 1):
                     if t > 0:
                         self.wait(t - 1, k, d)
-                    self.copy(t, d, k, place - (1 - 2 * d) * t).start()
-                    sent.append(functools.partial(self.leave, t, k, d))
-
-        def leave(self, t, k, d):
-            self.copy(t, d, k, place - (1 - 2 * d) * t).wait_send()
+                    self.copy(t, d, k, -(1 - 2 * d) * t).start()
+
 
         def done(self):
             for k in range(self.pieces):
@@ -541,22 +581,20 @@
                 src,
                 dst,
                 self.first + (t * self.pieces + k) * 2 + d,
-                (page_at(place + 1 - 2 * d), part),
+                (around(1 - 2 * d), part),
             )
 
-        def leave(self, t, d, k):
-            self.copy(t, d, k).wait_send()
 
         def step(self, t):
             h = self.size // 2
             wide = self.wide
             if t == 0:
-                term = self.local(page_at(place + z.half)).astype(self.kind)
+                term = self.local(around(z.half)).astype(self.kind)
                 for k in range(self.pieces):
                     self.stage[k] = term[:, k * wide : (k + 1) * wide]
             else:
                 terms = [
-                    self.local(page_at(place + (1 - 2 * d) * (z.half - t))) for d in (0, 1)
+                    self.local(around((1 - 2 * d) * (z.half - t))) for d in (0, 1)
                 ]
             for k in range(self.pieces):
                 for d in (0, 1):
@@ -573,7 +611,6 @@
                         else:
                             held[...] = (held[...].astype(F32) + term).astype(self.kind)
                     self.copy(t, d, k).start()
-                    sent.append(functools.partial(self.leave, t, d, k))
 
         def total(self, out):
             term = self.local(page)
@@ -587,22 +624,44 @@
                 ).astype(out.dtype)
 
     c, w, n = z.cols, z.width, z.span
+
+    def fetch(i, name):
+        return pltpu.make_async_copy(getattr(r, name), getattr(r, z.held + name), load_sem.at[i])
+
+    for i, name in enumerate(z.fetched):
+        fetch(i, name).start()
+    hbm = r
+    r = types.SimpleNamespace(**vars(hbm))
+    for name in z.fetched:
+        setattr(r, name, getattr(hbm, z.held + name))
+    fetches = iter(range(len(z.fetched)))
+
+    def arrive(count):
+        for _ in range(count):
+            i = next(fetches)
+            pltpu.make_async_copy(
+                getattr(hbm, z.fetched[i]), getattr(r, z.fetched[i]), load_sem.at[i]
+            ).wait()
+
+    arrive(3)
     for q in range(z.parts):
         rows = pl.ds(q * z.row, z.row)
         for i, weight in enumerate((r.w_query, r.w_key, r.w_value)):
             r.cut_qkv[rows, i * c : (i + 1) * c] = weight[:, q * c : (q + 1) * c].astype(BF16)
-    base = pl.multiple_of(rank * SLAB, SLAB)
+    mine = pl.multiple_of(part * SLAB, SLAB)
     for i, small in enumerate(
         (r.b_query, r.b_value, r.b_out, r.g_attn, r.s_attn, r.b_outer, r.g_final, r.s_final)
     ):
-        r.vec_all[pl.ds(base + i, 1), 0 : z.row] = small[...]
-    r.vec_all[pl.ds(base + VECTORS, 1), :] = r.b_inner[...]
+        r.vec_raw[pl.ds(mine + i, 1), 0 : z.row] = small[...]
+    at_page = pl.multiple_of(page * SLAB, SLAB)
+    r.vec_all[pl.ds(at_page + VECTORS, 1), :] = r.b_inner[...]
+    arrive(1)
     r.outer_w[pl.ds(pl.multiple_of(page * z.unit, z.unit), z.unit), :] = r.w_outer[...].astype(
         BF16
     )
 
     ring_qkv = Gather(r.qkv_w, z.rows, 2)
-    ring_vec = Gather(r.vec_all, z.parts * SLAB)
+    ring_vec = Gather(r.vec_all, SLAB)
     ring_inner = Gather(r.inner_w, z.rows, 2)
     ring_out = Gather(r.out_w, z.row)
     ring_outer = Gather(r.outer_w, z.unit, 2)
@@ -611,25 +670,26 @@
     share_tok = Share(r.tok_all, n)
 
     class ShareVec:
-        first = slots(4)
+        first = slots(3) - 1
 
         def copy(self, j, owner):
-            piece = block(r.vec_all, page * z.parts + owner, SLAB)
+            piece = block(r.vec_raw, owner, SLAB).at[pl.ds(0, VECTORS)]
             return copy(piece, piece, self.first + j, (page, peer(j)))
 
     vec_share = ShareVec()
     hold = slots(1)
 
     def hold_copy(slot):
-        return copy(r.own_out, block(r.out_w, slot, z.row), hold, (hold_page, hold_part))
+        return copy(r.own_out, block(r.out_w, slot, z.row), hold, (hold_page, hold_part), 0)
 
     pl.semaphore_wait(barrier, 5 + 2 * moves)
     cut_qkv.start()
     for j in (2, 3, 1):
         vec_share.copy(j, part).start()
-    sent.append(lambda: [vec_share.copy(j, part).wait_send() for j in (1, 2, 3)])
     ring_outer.step(0)
+    arrive(1)
     r.own_out[...] = r.w_out[...].astype(BF16)
+    arrive(1)
 
     @pl.when(moves == 1)
     def _():
@@ -640,7 +700,9 @@
         r.out_w[pl.ds(pl.multiple_of(page * z.row, z.row), z.row), :] = r.own_out[...]
 
     r.tok_all[pl.ds(pl.multiple_of(part * n, n), n), :] = r.tokens[...].astype(BF16)
-    share_tok.start()
+    share_tok.start(0)
+    share_tok.start(1)
+    arrive(1)
     for q in range(z.parts):
         rows = pl.ds(q * z.row, z.row)
         for g in range(z.pages):
@@ -658,35 +720,38 @@
     ring_qkv.step(0)
     for j in (1, 2, 3):
         vec_share.copy(j, peer(j)).wait_recv()
+    lane = lax.broadcasted_iota(jnp.int32, (VECTORS, 128), 1)
+    total = jnp.zeros((VECTORS, 128), F32)
+    for q in range(z.parts):
+        tile = r.vec_raw[q * SLAB : q * SLAB + VECTORS, :]
+        if q:
+            tile = pltpu.roll(tile, q * z.row, 1)
+        total = total + jnp.where(lane // z.row == q, tile, 0.0)
+    r.vec_all[pl.ds(at_page, VECTORS), :] = total
     ring_vec.step(0)
+    ring_qkv.step(1)
+    ring_vec.step(1)
 
     @pl.when(moves == 1)
     def _():
         hold_copy(page).wait_recv()
 
     ring_out.step(0)
-    for t in range(1, z.half):
-        ring_qkv.step(t)
-        ring_vec.step(t)
-        ring_out.step(t)
-        if t == 1:
-            share_tok.forward()
+    ring_qkv.step(2)
+    ring_vec.step(2)
+    ring_out.step(1)
+    share_tok.forward()
+    ring_qkv.step(3)
+    ring_vec.step(3)
+    ring_out.step(2)
     cut_inner.wait()
     ring_inner.step(0)
     ring_vec.done()
 
-    lane = lax.broadcasted_iota(jnp.int32, (VECTORS, 128), 1)
     for g in range(z.pages):
-        total = jnp.zeros((VECTORS, 128), F32)
-        for q in range(z.parts):
-            tile = r.vec_all[pl.ds((g * z.parts + q) * SLAB, VECTORS), :]
-            if q:
-                tile = pltpu.roll(tile, q * z.row, 1)
-            total = total + jnp.where(lane // z.row == q, tile, 0.0)
-        r.vecs[:, g * 128 : (g + 1) * 128] = total.astype(BF16).astype(F32)
-        at = pl.multiple_of((g * z.parts + part) * SLAB + VECTORS, VECTORS)
-        tile = r.vec_all[pl.ds(at, 8), :]
-        r.b_mine[:, g * z.unit : (g + 1) * z.unit] = tile[0:1].astype(BF16).astype(F32)
+        tile = r.vec_all[g * SLAB : (g + 1) * SLAB, :].astype(BF16).astype(F32)
+        r.vecs[:, g * 128 : (g + 1) * 128] = tile[0:VECTORS]
+        r.b_mine[:, g * z.unit : (g + 1) * z.unit] = tile[VECTORS : VECTORS + 1]
 
     def vector(i):
         return r.vecs[i : i + 1, :]
@@ -707,6 +772,8 @@
 
     lax.fori_loop(0, z.parts, make_qkv, 0)
     ring_inner.step(1)
+    ring_out.step(3)
+    ring_outer.step(1)
 
     scale = HEAD_DIM ** (-0.5)
     first_head = lax.broadcasted_iota(jnp.int32, (n, 128), 1) < HEAD_DIM
@@ -740,39 +807,26 @@
         lax.fori_loop(0, z.parts, body, 0)
 
     attend(0)
-    ring_inner.step(2)
-    ring_outer.step(1)
     attend(1)
     ring_out.done()
 
     combine = Combine(0, lambda rows: dot_nn(r.ctx[rows, :], r.out_w[...]))
     combine.term(3)
     combine.term(2)
-    ring_inner.step(3)
-    ring_outer.step(2)
+    ring_inner.step(2)
     combine.term(1)
     combine.term(0)
-
-    def by_rows(fn):
-        size = 32
-
-        def body(i, carry):
-            fn(pl.ds(pl.multiple_of(i * size, size), size), pl.multiple_of(i * size, size))
-            return carry
-
-        lax.fori_loop(0, n // size, body, 0)
+    ring_outer.step(2)
 
     def add_column_sum(i, values):
         r.sums[i : i + 1, :] += jnp.sum(values, axis=0, keepdims=True)
 
     r.sums[...] = jnp.zeros_like(r.sums)
 
-    combine.wait()
-
     share_hid = Share(r.hid_all, n)
 
-    def first_norm(rows, at):
-        mixed = r.tokens[rows, :] + (combine.total(rows) + vector(2))
+    def first_norm(rows, at, total):
+        mixed = r.tokens[rows, :] + (total + vector(2))
         normed, inverse = norm_parts(mixed)
         hidden = normed * vector(3) + vector(4)
         r.norm_one[rows, :] = normed
@@ -780,8 +834,8 @@
         r.hidden[rows, :] = hidden
         r.hid_all[pl.ds(pl.multiple_of(part * n + at, 32), 32), :] = hidden.astype(BF16)
 
-    by_rows(first_norm)
-    share_hid.start()
+    combine.finish(first_norm, share_hid.start)
+    ring_inner.step(3)
     ring_outer.step(3)
     ring_inner.done()
 
@@ -811,12 +865,12 @@
     combine_two = Combine(1, lambda rows: dot_nn(r.active[rows, :], r.outer_w[...]))
     for j in (3, 2, 1, 0):
         combine_two.term(j)
-    combine_two.wait()
-
     share_gf = Share(r.gf_all, n)
 
-    def second_norm(rows, at):
-        outer = combine_two.total(rows) + vector(5)
+    arrive(1)
+
+    def second_norm(rows, at, total):
+        outer = total + vector(5)
         normed, inverse = norm_parts(r.hidden[rows, :] + outer)
         r.o_out[rows, :] = normed * vector(6) + vector(7)
         grad = r.out_grad[rows, :]
@@ -828,8 +882,7 @@
         r.grad_sum[rows, :] = grad_sum
         r.gf_all[pl.ds(pl.multiple_of(part * n + at, 32), 32), :] = low
 
-    by_rows(second_norm)
-    share_gf.start()
+    combine_two.finish(second_norm, share_gf.start)
 
     def chunk_term(left, right, size):
         def local(g):
@@ -838,8 +891,13 @@
 
         return local
 
-    reduce_outer = Reduce(
-        r.slot_outer, r.stage_outer, chunk_term(r.active, r.gf_all, z.unit), (z.unit, w), BF16, 2
+    reduce_outer_a = Reduce(
+        r.slot_outer_a, r.stage_outer_a,
+        chunk_term(r.active, r.gf_all.at[:, 0 : w // 2], z.unit), (z.unit, w // 2), BF16,
+    )
+    reduce_outer_b = Reduce(
+        r.slot_outer_b, r.stage_outer_b,
+        chunk_term(r.active, r.gf_all.at[:, w // 2 :], z.unit), (z.unit, w // 2), BF16,
     )
     reduce_inner = Reduce(
         r.slot_inner, r.stage_inner, chunk_term(r.hid_all, r.grad_inner, z.rows),
@@ -877,25 +935,23 @@
     share_gf.wait(1)
     make_grad_inner(1)
     share_gf.forward()
+    make_grad_inner(2)
     share_gf.wait(3)
-    reduce_outer.step(0)
-    make_grad_inner(2)
+    reduce_outer_a.step(0)
     make_grad_inner(3)
     combine_three = Combine(2, lambda rows: dot_nt(r.grad_inner[rows, :], r.inner_w[...]))
     combine_three.term(3)
     combine_three.term(2)
-    reduce_outer.step(1)
     reduce_inner.step(0)
+    reduce_outer_a.step(1)
     combine_three.term(1)
     combine_three.term(0)
-    reduce_outer.step(2)
     reduce_inner.step(1)
-    combine_three.wait()
 
     share_ga = Share(r.ga_all, n)
 
-    def first_norm_back(rows, at):
-        grad = r.grad_sum[rows, :] + combine_three.total(rows)
+    def first_norm_back(rows, at, total):
+        grad = r.grad_sum[rows, :] + total
         normed = r.norm_one[rows, :]
         add_column_sum(3, grad * normed)
         add_column_sum(4, grad)
@@ -905,8 +961,7 @@
         r.grad_mixed[rows, :] = mixed
         r.ga_all[pl.ds(pl.multiple_of(part * n + at, 32), 32), :] = low
 
-    by_rows(first_norm_back)
-    share_ga.start()
+    combine_three.finish(first_norm_back, share_ga.start)
 
     def make_grad_ctx(j):
         rows = pl.ds(pl.multiple_of(peer(j) * n, n), n)
@@ -915,7 +970,7 @@
     make_grad_ctx(0)
     share_ga.wait(1)
     make_grad_ctx(1)
-    reduce_outer.step(3)
+    reduce_outer_a.step(2)
     reduce_inner.step(2)
     share_ga.forward()
     make_grad_ctx(2)
@@ -923,6 +978,7 @@
     make_grad_ctx(3)
     r.term_out[...] = dot_tn(r.ctx[...], r.ga_all[...])
     reduce_out.step(0)
+    reduce_outer_a.step(3)
 
     def attend_back(pair):
         r.grad_kv[...] = jnp.zeros_like(r.grad_kv)
@@ -959,6 +1015,7 @@
     reduce_out.step(1)
     attend_back(1)
     reduce_qkv.step(0)
+    reduce_outer_b.step(0)
     reduce_out.step(2)
 
     r.sums[0:1, my_cols] = jnp.sum(r.grad_qkv[:, 0:c].astype(F32), axis=0, keepdims=True)
@@ -975,28 +1032,29 @@
     combine_four.term(3)
     combine_four.term(2)
     reduce_qkv.step(1)
+    reduce_outer_b.step(1)
     reduce_vec.step(1)
     reduce_out.step(3)
     combine_four.term(1)
     combine_four.term(0)
 
-    reduce_outer.total(r.o_outer)
     reduce_inner.total(r.fin_inner)
     fin_inner = Spread(r.fin_inner, r.got_inner, z.row)
     fin_inner.start()
     reduce_qkv.step(2)
+    reduce_outer_b.step(2)
     reduce_vec.step(2)
-    combine_four.wait()
-
-    def input_rows(rows, at):
-        r.o_grad[rows, :] = r.grad_mixed[rows, :] + combine_four.total(rows)
-
-    by_rows(input_rows)
+
+    def input_rows(rows, at, total):
+        r.o_grad[rows, :] = r.grad_mixed[rows, :] + total
+
+    combine_four.finish(input_rows)
+    reduce_outer_a.total(r.o_outer.at[:, 0 : w // 2])
     reduce_out.total(r.fin_out)
     home = slots(1)
 
     def home_copy():
-        return copy(r.fin_out, r.got_out, home, (own_page, own_part))
+        return copy(r.fin_out, r.got_out, home, (own_page, own_part), 1)
 
     @pl.when(moves == 1)
     def _():
@@ -1008,10 +1066,11 @@
 
     reduce_qkv.step(3)
     reduce_vec.step(3)
+    reduce_outer_b.step(3)
     reduce_vec.total(r.fin_vec)
 
     class VecAll:
-        first = slots(4)
+        first = slots(3) - 1
 
         def copy(self, j):
             return copy(r.fin_vec, r.got_vec.at[j], self.first + j, (page, peer(j)))
@@ -1019,7 +1078,6 @@
     fin_vec = VecAll()
     for j in (2, 3, 1):
         fin_vec.copy(j).start()
-    sent.append(lambda: [fin_vec.copy(j).wait_send() for j in (1, 2, 3)])
     reduce_qkv.total(r.fin_qkv)
     fin_qkv = Spread(r.fin_qkv, r.got_qkv, z.row)
     fin_qkv.start()
@@ -1046,17 +1104,19 @@
         summed = summed + r.got_vec[j, 0:VECTORS, :]
     r.o_vec[0:VECTORS, :] = pltpu.roll(summed, (128 - part * z.row) % 128, 1)
     r.o_vec[VECTORS:, :] = r.fin_vec[VECTORS:, :]
+    reduce_outer_b.total(r.o_outer.at[:, w // 2 :])
     deliver(fin_qkv, r.fin_qkv, r.got_qkv, r.o_qkv)
 
-    for wait in sent:
-        wait()
+    for group, size in enumerate(groups):
+        rows = r.measure.at[pl.ds(0, size // 512)]
+        copy(rows, rows, 0, (page, part), 2 + group).wait_send()
 
     @pl.when(moves == 1)
     def _():
         hold_copy(hold_page).wait_send()
         home_copy().wait_send()
 
-    assert counter[0] <= z.sems, counter[0]
+    assert counter[0] == z.sems and 2 + len(groups) <= z.groups, (counter, groups)
 
 
 def finish_kernel(z, out, grad, outer, inner, qkv, wout, vec, *outs):
@@ -1108,7 +1168,8 @@
         inner_w=((w, z.mine), BF16),
         out_w=((c, w), BF16),
         outer_w=((z.mine, w), BF16),
-        vec_all=((z.pages * z.parts * SLAB, 128), F32),
+        vec_all=((z.pages * SLAB, 128), F32),
+        vec_raw=((z.parts * SLAB, 128), F32),
         cut_qkv=((z.rows, 3 * c), BF16),
         cut_inner=((z.rows, z.mine), BF16),
         own_out=((z.row, w), BF16),
@@ -1121,6 +1182,7 @@
         qkv=((ln, 3 * c), BF16),
         grad_qkv=((ln, 3 * c), BF16),
         probs=((z.heads, ln, ln), F32),
+        measure=((8192, 128), F32),
         ctx=((ln, c), BF16),
         grad_ctx=((ln, c), BF16),
         grad_kv=((2, ln, 128), F32),
@@ -1139,7 +1201,8 @@
         b_sum=((1, z.mine), F32),
         term_out=((c, w), F32),
         term_vec=((z.pages * SLAB, 128), F32),
-        slot_outer=((2, 2, half, z.unit, w // 2), BF16), stage_outer=((2, z.unit, w // 2), BF16),
+        slot_outer_a=((1, 2, half, z.unit, w // 2), BF16), stage_outer_a=((1, z.unit, w // 2), BF16),
+        slot_outer_b=((1, 2, half, z.unit, w // 2), BF16), stage_outer_b=((1, z.unit, w // 2), BF16),
         slot_inner=((2, 2, half, z.rows, z.mine // 2), BF16), stage_inner=((2, z.rows, z.mine // 2), BF16),
         slot_qkv=((2, 2, half, z.rows, 3 * c // 2), BF16), stage_qkv=((2, z.rows, 3 * c // 2), BF16),
         slot_out=((1, 2, half, z.row, w // 1), BF16), stage_out=((1, z.row, w // 1), BF16),
@@ -1149,19 +1212,29 @@
         fin_out=((z.row, w), BF16), got_out=((z.row, w), BF16),
         fin_vec=((SLAB, 128), F32), got_vec=((4, SLAB, 128), F32),
     )
-    z.sems = 192
-    sems = pltpu.SemaphoreType.DMA((z.sems,))
-    names = list(ins) + list(outs) + list(scratch) + list(dict(send_sem=0, recv_sem=0))
+    z.sems = 196
+    z.groups, z.group_bytes = 7, 4 << 20
+    fetched = dict(w_query=0, w_key=0, w_value=0, w_outer=0, w_out=0, tokens=0, w_inner=0, out_grad=0)
+    z.fetched, z.held = tuple(fetched), "f_"
+    for name in z.fetched:
+        scratch[z.held + name] = (ins[name].shape, F32)
+    sems = [pltpu.SemaphoreType.DMA((z.groups,)), pltpu.SemaphoreType.DMA((z.sems,)), pltpu.SemaphoreType.DMA((len(fetched),))]
+    names = list(ins) + list(outs) + list(scratch) + list(dict(send_sem=0, recv_sem=0, load_sem=0))
     vmem = pl.BlockSpec(memory_space=pltpu.VMEM)
     parts = pl.pallas_call(
         functools.partial(layer_kernel, z, names),
         out_shape=[jax.ShapeDtypeStruct(*v) for v in outs.values()],
         in_specs=[
-            pl.BlockSpec(memory_space=pltpu.SMEM) if v is valid_len else vmem for v in ins.values()
+            pl.BlockSpec(memory_space=pltpu.SMEM)
+            if v is valid_len
+            else pl.BlockSpec(memory_space=pl.ANY)
+            if k in fetched
+            else vmem
+            for k, v in ins.items()
         ],
         out_specs=[vmem] * len(outs),
         scratch_shapes=[pltpu.VMEM(*v) for v in scratch.values()]
-        + [sems, sems],
+        + sems,
         compiler_params=pltpu.CompilerParams(
             collective_id=0, has_side_effects=True, vmem_limit_bytes=67043328
         ),

time: 178 us -> 165 us (0.927)
  Pallas kernels: 176 us -> 162 us
    pallas_call x1, Pallas kernels: 173 us -> 159 us  [paged_layer(): pl.pallas_call(functools.partial(layer_kernel, z, names), out_shape=[jax....]
where the time goes in v3:
time: 165 us; the launch traced here: 164 us
  Pallas kernels  162 us (98%)
    pallas_call x1, Pallas kernels, paged_layer(): pl.pallas_call(functools.partial(layer_kernel, z, names), out_shape=[jax....  159 us

profile of v3, /device:TPU:0, one launch (start us, length us, event | category | flops | bytes accessed | tf_op | source)
XLA Modules:
  0.0 163.5 jit_solution(7964683372687197455)
XLA Ops:
  1.3 159.0 %layer.1 = (f32[128,1024]{1,0:T(8,128)}, f32[128,1024]{1,0:T(8,128)}, f32[128,1024]{1,0:T(8,128)}, bf16[4,32,1024]{2,1,0:T(8,128)(2,1)}, bf16[4,32,768]{2,1,0:T(...) custom-call(s32[1]{0:T(128)S(6)} %copy.35.refs_0_, f32[128,1024]{1,0:T(8,128)} %bitcast.22, ...), custom_call_target="tpu_custom_call" | custom-call | tf_op jit(solution)/shard_map/layer/pallas_call | solution.py:1224
  160.3 3.1 %finish.1 = (f32[128,1024]{1,0:T(8,128)}, f32[128,1024]{1,0:T(8,128)}, f32[32,1024]{1,0:T(8,128)}, f32[1,32]{1,0:T(1,128)}, f32[32,1024]{1,0:T(8,128)}, /*index=...) custom-call(f32[128,1024]{1,0:T(8,128)} %get-tuple-element.41.out, ...), custom_call_target="tpu_custom_call" | custom-call | tf_op jit(solution)/shard_map/finish/pallas_call | solution.py:1251

commit v4 on v3

--- a/solution.py
+++ b/solution.py
@@ -303,6 +303,7 @@
         self.mine = self.unit * self.pages
         self.cols = width // self.parts
         self.heads = self.cols // HEAD_DIM
+        self.pairs = self.cols // 128
 
 
 def supported(mesh, token_shape, width, units):
@@ -352,12 +353,6 @@
         return peers[j]
 
     rank = page * z.parts + part
-    hold_page, hold_part = rank % z.pages, rank // z.pages
-    flat = part * z.pages + page
-    own_page, own_part = flat // z.parts, flat % z.parts
-    moves = 1 - (1 - jnp.minimum(1, (hold_page - page) * (hold_page - page))) * (
-        1 - jnp.minimum(1, (hold_part - part) * (hold_part - part))
-    )
 
     class Copy:
         def __init__(self, src, dst, index, device, group=None):
@@ -383,7 +378,7 @@
                 if groups[-1] + size > z.group_bytes:
                     groups.append(0)
                 groups[-1] += size
-                group = 2 + len(groups) - 1
+                group = len(groups) - 1
             self.made(group).start()
 
         def wait_recv(self):
@@ -408,11 +403,6 @@
     greet((around(1), part))
     greet((around(-1), part))
 
-    @pl.when(moves == 1)
-    def _():
-        greet((hold_page, hold_part))
-        greet((own_page, own_part))
-
     class Share:
         def __init__(self, ref, size, pieces=2):
             self.ref, self.size, self.pieces = ref, size, pieces
@@ -438,55 +428,58 @@
                 self.copy(j, peer(j), k).wait_recv()
 
     class Combine:
-        def __init__(self, phase, make, pieces=2):
-            self.phase, self.make, self.pieces = phase, make, pieces
+        def __init__(self, refs, size, make, pieces=2):
+            self.out, self.got, self.own = refs
+            self.size, self.make, self.pieces = size, make, pieces
+            self.height = size // pieces
             self.first = slots(3 * pieces) - 1
 
+        def rows(self, j, k):
+            at = pl.multiple_of(peer(j) * self.size + k * self.height, self.height)
+            return pl.ds(at, self.height)
+
         def copy(self, j, k):
-            height = n // self.pieces
-            at = pl.multiple_of(peer(j) * n + k * height, height)
             return copy(
-                r.part_out.at[self.phase, pl.ds(at, height)],
-                r.part_in.at[self.phase, j, pl.ds(k * height, height)],
+                self.out.at[self.rows(j, k)],
+                self.got.at[j, pl.ds(k * self.height, self.height)],
                 self.first + 3 * k + j,
                 (page, peer(2 if j == 2 else 1)),
             )
 
         def term(self, j):
-            value = self.make(pl.ds(pl.multiple_of(peer(j) * n, n), n))
+            value = self.make(pl.ds(pl.multiple_of(peer(j) * self.size, self.size), self.size), j)
             if j == 0:
-                r.part_own[...] = value
+                self.own[...] = value
                 return
-            height = n // self.pieces
             for k in range(self.pieces):
-                rows = slice(k * height, (k + 1) * height)
+                rows = slice(k * self.height, (k + 1) * self.height)
                 mine = value[rows]
                 if j == 2:
                     self.copy(3, k).wait_recv()
-                    mine = mine + r.part_in[self.phase, 3, rows, :].astype(F32)
-                at = pl.multiple_of(peer(j) * n + k * height, height)
-                r.part_out[self.phase, pl.ds(at, height), :] = mine.astype(BF16)
+                    mine = mine + self.got[3, rows, :].astype(F32)
+                self.out[self.rows(j, k), :] = mine.astype(BF16)
                 self.copy(j, k).start()
 
-
-        def finish(self, fn, after=None):
-            height, size = n // self.pieces, 32
+        def finish(self, fn, after=None, step=32):
             for k in range(self.pieces):
                 for j in (1, 2):
                     self.copy(j, k).wait_recv()
 
                 def body(i, carry):
-                    at = pl.multiple_of(k * height + i * size, size)
-                    rows = pl.ds(at, size)
-                    total = r.part_own[rows, :]
+                    at = pl.multiple_of(k * self.height + i * step, step)
+                    rows = pl.ds(at, step)
+                    total = self.own[rows, :]
                     for j in (1, 2):
-                        total = total + r.part_in[self.phase, j, rows, :].astype(F32)
+                        total = total + self.got[j, rows, :].astype(F32)
                     fn(rows, at, total)
                     return carry
 
-                lax.fori_loop(0, height // size, body, 0)
+                lax.fori_loop(0, self.height // step, body, 0)
                 if after is not None:
                     after(k)
+
+    def token_refs(phase):
+        return r.part_out.at[phase], r.part_in.at[phase], r.part_own
 
     class Spread:
         def __init__(self, src, dst, size):
@@ -647,7 +640,10 @@
     for q in range(z.parts):
         rows = pl.ds(q * z.row, z.row)
         for i, weight in enumerate((r.w_query, r.w_key, r.w_value)):
-            r.cut_qkv[rows, i * c : (i + 1) * c] = weight[:, q * c : (q + 1) * c].astype(BF16)
+            for k in range(z.pairs):
+                r.cut_qkv[rows, (3 * k + i) * 128 : (3 * k + i + 1) * 128] = weight[
+                    :, q * c + k * 128 : q * c + (k + 1) * 128
+                ].astype(BF16)
     mine = pl.multiple_of(part * SLAB, SLAB)
     for i, small in enumerate(
         (r.b_query, r.b_value, r.b_out, r.g_attn, r.s_attn, r.b_outer, r.g_final, r.s_final)
@@ -663,9 +659,10 @@
     ring_qkv = Gather(r.qkv_w, z.rows, 2)
     ring_vec = Gather(r.vec_all, SLAB)
     ring_inner = Gather(r.inner_w, z.rows, 2)
-    ring_out = Gather(r.out_w, z.row)
+    ring_out = Gather(r.out_w, z.rows)
     ring_outer = Gather(r.outer_w, z.unit, 2)
     cut_qkv = Place(r.cut_qkv, r.qkv_w, z.row, page * z.parts)
+    cut_out = Place(r.cut_out, r.out_w, z.row, page * z.parts)
     cut_inner = Place(r.cut_inner, r.inner_w, z.row, page * z.parts)
     share_tok = Share(r.tok_all, n)
 
@@ -677,31 +674,18 @@
             return copy(piece, piece, self.first + j, (page, peer(j)))
 
     vec_share = ShareVec()
-    hold = slots(1)
-
-    def hold_copy(slot):
-        return copy(r.own_out, block(r.out_w, slot, z.row), hold, (hold_page, hold_part), 0)
-
-    pl.semaphore_wait(barrier, 5 + 2 * moves)
+    pl.semaphore_wait(barrier, 5)
     cut_qkv.start()
     for j in (2, 3, 1):
         vec_share.copy(j, part).start()
     ring_outer.step(0)
-    arrive(1)
-    r.own_out[...] = r.w_out[...].astype(BF16)
-    arrive(1)
-
-    @pl.when(moves == 1)
-    def _():
-        hold_copy(hold_page).start()
-
-    @pl.when(moves == 0)
-    def _():
-        r.out_w[pl.ds(pl.multiple_of(page * z.row, z.row), z.row), :] = r.own_out[...]
-
+    arrive(2)
     r.tok_all[pl.ds(pl.multiple_of(part * n, n), n), :] = r.tokens[...].astype(BF16)
     share_tok.start(0)
     share_tok.start(1)
+    for q in range(z.parts):
+        r.cut_out[pl.ds(q * z.row, z.row), :] = r.w_out[:, q * c : (q + 1) * c].astype(BF16)
+    cut_out.start()
     arrive(1)
     for q in range(z.parts):
         rows = pl.ds(q * z.row, z.row)
@@ -714,6 +698,7 @@
     own_rows = pl.ds(pl.multiple_of(rank * z.row, z.row), z.row)
     cut_rows = pl.ds(pl.multiple_of(part * z.row, z.row), z.row)
     r.qkv_w[own_rows, :] = r.cut_qkv[cut_rows, :]
+    r.out_w[own_rows, :] = r.cut_out[cut_rows, :]
     r.inner_w[own_rows, :] = r.cut_inner[cut_rows, :]
 
     cut_qkv.wait()
@@ -731,11 +716,7 @@
     ring_vec.step(0)
     ring_qkv.step(1)
     ring_vec.step(1)
-
-    @pl.when(moves == 1)
-    def _():
-        hold_copy(page).wait_recv()
-
+    cut_out.wait()
     ring_out.step(0)
     ring_qkv.step(2)
     ring_vec.step(2)
@@ -756,7 +737,6 @@
     def vector(i):
         return r.vecs[i : i + 1, :]
 
-    my_cols = pl.ds(pl.multiple_of(part * c, c), c)
 
     share_tok.wait(1)
     share_tok.wait(3)
@@ -765,9 +745,14 @@
     def make_qkv(b, carry):
         rows = pl.ds(pl.multiple_of(b * n, n), n)
         out = dot_nn(r.tok_all[rows, :], r.qkv_w[...])
-        r.qkv[rows, 0:c] = (out[:, 0:c] + r.vecs[0:1, my_cols]).astype(BF16)
-        r.qkv[rows, c : 2 * c] = out[:, c : 2 * c].astype(BF16)
-        r.qkv[rows, 2 * c :] = (out[:, 2 * c :] + r.vecs[1:2, my_cols]).astype(BF16)
+        for k in range(z.pairs):
+            mine = pl.ds(pl.multiple_of(part * c + k * 128, 128), 128)
+            for i, bias in enumerate((0, None, 1)):
+                cols = slice((3 * k + i) * 128, (3 * k + i + 1) * 128)
+                value = out[:, cols]
+                if bias is not None:
+                    value = value + r.vecs[bias : bias + 1, mine]
+                r.qkv[rows, cols] = value.astype(BF16)
         return carry
 
     lax.fori_loop(0, z.parts, make_qkv, 0)
@@ -781,7 +766,7 @@
     valid = r.valid[0]
 
     def pair_cols(kind, pair):
-        return pl.ds(kind * c + pair * 128, 128)
+        return pl.ds((3 * pair + kind) * 128, 128)
 
     def attend(pair):
         def body(b, carry):
@@ -799,24 +784,44 @@
                 probs = weight * (1.0 / jnp.sum(weight, axis=-1, keepdims=True))
                 r.probs[2 * pair + h, rows, :] = probs
                 outs.append(dot_nn(probs.astype(BF16), values))
-            r.ctx[rows, pl.ds(pair * 128, 128)] = jnp.where(first_head, outs[0], outs[1]).astype(
+            place_rows = pl.ds(
+                pl.multiple_of((part * z.pairs + pair) * z.length + b * n, n), n
+            )
+            r.ctx_all[place_rows, :] = jnp.where(first_head, outs[0], outs[1]).astype(
                 BF16
             )
             return carry
 
         lax.fori_loop(0, z.parts, body, 0)
 
-    attend(0)
-    attend(1)
+    share_ctx = Share(r.ctx_all, z.pairs * z.length, z.pairs)
+    for pair in range(z.pairs):
+        attend(pair)
+        share_ctx.start(pair)
+    ring_inner.step(2)
+
+    def project(j):
+        term = None
+        for k in range(z.pairs):
+            rows = pl.ds(pl.multiple_of((peer(j) * z.pairs + k) * z.length, z.length), z.length)
+            features = pl.ds(pl.multiple_of(peer(j) * c + k * 128, 128), 128)
+            more = dot_nn(r.ctx_all[rows, :], r.out_w[features, :])
+            term = more if term is None else term + more
+        r.att_sum[...] = term if j == 0 else r.att_sum[...] + term
+
     ring_out.done()
-
-    combine = Combine(0, lambda rows: dot_nn(r.ctx[rows, :], r.out_w[...]))
-    combine.term(3)
-    combine.term(2)
-    ring_inner.step(2)
-    combine.term(1)
-    combine.term(0)
-    ring_outer.step(2)
+    project(0)
+    share_ctx.wait(1)
+    project(1)
+    share_ctx.forward()
+    project(2)
+    share_ctx.wait(3)
+    project(3)
+    r.att_cut[...] = r.att_sum[...].astype(BF16)
+    move_att = Place(r.att_cut, r.att_got, n, 0)
+    move_att.start()
+    own_block = pl.ds(pl.multiple_of(part * n, n), n)
+    r.att_got[own_block, :] = r.att_cut[own_block, :]
 
     def add_column_sum(i, values):
         r.sums[i : i + 1, :] += jnp.sum(values, axis=0, keepdims=True)
@@ -834,9 +839,25 @@
         r.hidden[rows, :] = hidden
         r.hid_all[pl.ds(pl.multiple_of(part * n + at, 32), 32), :] = hidden.astype(BF16)
 
-    combine.finish(first_norm, share_hid.start)
     ring_inner.step(3)
-    ring_outer.step(3)
+    move_att.wait()
+    for k in range(2):
+
+        def norm_rows(i, carry):
+            at = pl.multiple_of(k * (n // 2) + i * 32, 32)
+            total = jnp.concatenate(
+                [
+                    r.att_got[pl.ds(pl.multiple_of(q * n + at, 32), 32), :].astype(F32)
+                    for q in range(z.parts)
+                ],
+                axis=1,
+            )
+            first_norm(pl.ds(at, 32), at, total)
+            return carry
+
+        lax.fori_loop(0, n // 64, norm_rows, 0)
+        share_hid.start(k)
+    ring_outer.step(2)
     ring_inner.done()
 
     tile = 256
@@ -857,12 +878,13 @@
     make_inner(0)
     share_hid.wait(1)
     make_inner(1)
+    ring_outer.step(3)
     share_hid.forward()
     make_inner(2)
     share_hid.wait(3)
     make_inner(3)
     ring_outer.done()
-    combine_two = Combine(1, lambda rows: dot_nn(r.active[rows, :], r.outer_w[...]))
+    combine_two = Combine(token_refs(0), n, lambda rows, j: dot_nn(r.active[rows, :], r.outer_w[...]))
     for j in (3, 2, 1, 0):
         combine_two.term(j)
     share_gf = Share(r.gf_all, n)
@@ -903,14 +925,22 @@
         r.slot_inner, r.stage_inner, chunk_term(r.hid_all, r.grad_inner, z.rows),
         (z.rows, z.mine), BF16, 2
     )
-    reduce_qkv = Reduce(
-        r.slot_qkv, r.stage_qkv, chunk_term(r.tok_all, r.grad_qkv, z.rows),
-        (z.rows, 3 * c), BF16, 2
-    )
-    reduce_out = Reduce(
-        r.slot_out, r.stage_out,
-        lambda g: r.term_out[pl.ds(pl.multiple_of(g * z.row, z.row), z.row), :], (z.row, w), BF16,
-    )
+    def pair_term(k):
+        def local(g):
+            cols = pl.ds(pl.multiple_of(g * z.rows, z.rows), z.rows)
+            return dot_tn(r.tok_all[:, cols], r.grad_qkv[:, 384 * k : 384 * (k + 1)])
+
+        return local
+
+    def out_term(g):
+        rows = pl.ds(pl.multiple_of(g * z.length, z.length), z.length)
+        return dot_tn(r.ctx_all[rows, :], r.ga_cols[...])
+
+    reduce_pair = [
+        Reduce(r.slot_pair.at[k], r.stage_pair.at[k], pair_term(k), (z.rows, 384), BF16)
+        for k in range(z.pairs)
+    ]
+    reduce_out = Reduce(r.slot_out, r.stage_out, out_term, (z.rows, c), BF16)
     reduce_vec = Reduce(
         r.slot_vec, r.stage_vec,
         lambda g: r.term_vec[pl.ds(pl.multiple_of(g * SLAB, SLAB), SLAB), :], (SLAB, 128), F32,
@@ -938,17 +968,19 @@
     make_grad_inner(2)
     share_gf.wait(3)
     reduce_outer_a.step(0)
+    reduce_outer_b.step(0)
     make_grad_inner(3)
-    combine_three = Combine(2, lambda rows: dot_nt(r.grad_inner[rows, :], r.inner_w[...]))
+    combine_three = Combine(token_refs(1), n, lambda rows, j: dot_nt(r.grad_inner[rows, :], r.inner_w[...]))
     combine_three.term(3)
     combine_three.term(2)
     reduce_inner.step(0)
     reduce_outer_a.step(1)
     combine_three.term(1)
     combine_three.term(0)
+    reduce_outer_b.step(1)
     reduce_inner.step(1)
 
-    share_ga = Share(r.ga_all, n)
+    move_ga = Place(r.ga_cut, r.ga_cols, n, 0)
 
     def first_norm_back(rows, at, total):
         grad = r.grad_sum[rows, :] + total
@@ -959,26 +991,39 @@
         low = mixed.astype(BF16)
         add_column_sum(2, low.astype(F32))
         r.grad_mixed[rows, :] = mixed
-        r.ga_all[pl.ds(pl.multiple_of(part * n + at, 32), 32), :] = low
-
-    combine_three.finish(first_norm_back, share_ga.start)
-
-    def make_grad_ctx(j):
-        rows = pl.ds(pl.multiple_of(peer(j) * n, n), n)
-        r.grad_ctx[rows, :] = dot_nt(r.ga_all[rows, :], r.out_w[...]).astype(BF16)
-
-    make_grad_ctx(0)
-    share_ga.wait(1)
-    make_grad_ctx(1)
+        for q in range(z.parts):
+            r.ga_cut[pl.ds(pl.multiple_of(q * n + at, 32), 32), :] = low[:, q * c : (q + 1) * c]
+
+    combine_three.finish(first_norm_back)
+    move_ga.start()
+    r.ga_cols[own_block, :] = r.ga_cut[own_block, :]
     reduce_outer_a.step(2)
+
+    def grad_ctx_term(rows, j):
+        return jnp.concatenate(
+            [
+                dot_nt(
+                    r.ga_cols[...],
+                    r.out_w[pl.ds(pl.multiple_of(peer(j) * c + k * 128, 128), 128), :],
+                )
+                for k in range(z.pairs)
+            ],
+            axis=0,
+        )
+
+    combine_ctx = Combine(
+        (r.ctx_out, r.ctx_in, r.ctx_own), z.pairs * z.length, grad_ctx_term, z.pairs
+    )
+    move_ga.wait()
+    combine_ctx.term(3)
+    combine_ctx.term(2)
+    combine_ctx.term(1)
+    combine_ctx.term(0)
+    reduce_out.step(0)
     reduce_inner.step(2)
-    share_ga.forward()
-    make_grad_ctx(2)
-    share_ga.wait(3)
-    make_grad_ctx(3)
-    r.term_out[...] = dot_tn(r.ctx[...], r.ga_all[...])
-    reduce_out.step(0)
-    reduce_outer_a.step(3)
+
+    def keep_grad_ctx(rows, at, total):
+        r.grad_ctx[rows, :] = total.astype(BF16)
 
     def attend_back(pair):
         r.grad_kv[...] = jnp.zeros_like(r.grad_kv)
@@ -988,7 +1033,7 @@
             queries = r.qkv[rows, pair_cols(0, pair)]
             keys = r.qkv[:, pair_cols(1, pair)]
             values = r.qkv[:, pair_cols(2, pair)]
-            grad = r.grad_ctx[rows, pl.ds(pair * 128, 128)]
+            grad = r.grad_ctx[pl.ds(pl.multiple_of(pair * z.length + b * n, n), n), :]
             outs = []
             for h in range(2):
                 mine = first_head if h == 0 else ~first_head
@@ -1010,16 +1055,24 @@
         r.grad_qkv[:, pair_cols(1, pair)] = (r.grad_kv[0] * scale).astype(BF16)
         r.grad_qkv[:, pair_cols(2, pair)] = r.grad_kv[1].astype(BF16)
 
-    attend_back(0)
+    def after_pair(pair):
+        attend_back(pair)
+        reduce_pair[pair].step(0)
+        if pair == 0:
+            reduce_outer_a.step(3)
+            reduce_outer_b.step(2)
+            reduce_out.step(1)
+
+    combine_ctx.finish(keep_grad_ctx, after_pair, step=128)
     reduce_inner.step(3)
-    reduce_out.step(1)
-    attend_back(1)
-    reduce_qkv.step(0)
-    reduce_outer_b.step(0)
     reduce_out.step(2)
 
-    r.sums[0:1, my_cols] = jnp.sum(r.grad_qkv[:, 0:c].astype(F32), axis=0, keepdims=True)
-    r.sums[1:2, my_cols] = jnp.sum(r.grad_qkv[:, 2 * c :].astype(F32), axis=0, keepdims=True)
+    for k in range(z.pairs):
+        mine = pl.ds(pl.multiple_of(part * c + k * 128, 128), 128)
+        for row, kind in ((0, 0), (1, 2)):
+            r.sums[row : row + 1, mine] = jnp.sum(
+                r.grad_qkv[:, pair_cols(kind, k)].astype(F32), axis=0, keepdims=True
+            )
     r.term_vec[...] = jnp.zeros_like(r.term_vec)
     for g in range(z.pages):
         r.term_vec[g * SLAB : g * SLAB + VECTORS, :] = r.sums[:, g * 128 : (g + 1) * 128]
@@ -1028,12 +1081,12 @@
         ]
     reduce_vec.step(0)
 
-    combine_four = Combine(3, lambda rows: dot_nt(r.grad_qkv[rows, :], r.qkv_w[...]))
+    combine_four = Combine(token_refs(2), n, lambda rows, j: dot_nt(r.grad_qkv[rows, :], r.qkv_w[...]))
     combine_four.term(3)
     combine_four.term(2)
-    reduce_qkv.step(1)
-    reduce_outer_b.step(1)
     reduce_vec.step(1)
+    for pair in range(z.pairs):
+        reduce_pair[pair].step(1)
     reduce_out.step(3)
     combine_four.term(1)
     combine_four.term(0)
@@ -1041,32 +1094,22 @@
     reduce_inner.total(r.fin_inner)
     fin_inner = Spread(r.fin_inner, r.got_inner, z.row)
     fin_inner.start()
-    reduce_qkv.step(2)
-    reduce_outer_b.step(2)
     reduce_vec.step(2)
+    for pair in range(z.pairs):
+        reduce_pair[pair].step(2)
 
     def input_rows(rows, at, total):
         r.o_grad[rows, :] = r.grad_mixed[rows, :] + total
 
     combine_four.finish(input_rows)
     reduce_outer_a.total(r.o_outer.at[:, 0 : w // 2])
+    reduce_vec.step(3)
+    for pair in range(z.pairs):
+        reduce_pair[pair].step(3)
+    reduce_outer_b.step(3)
     reduce_out.total(r.fin_out)
-    home = slots(1)
-
-    def home_copy():
-        return copy(r.fin_out, r.got_out, home, (own_page, own_part), 1)
-
-    @pl.when(moves == 1)
-    def _():
-        home_copy().start()
-
-    @pl.when(moves == 0)
-    def _():
-        r.got_out[...] = r.fin_out[...]
-
-    reduce_qkv.step(3)
-    reduce_vec.step(3)
-    reduce_outer_b.step(3)
+    fin_out = Spread(r.fin_out, r.got_out, z.row)
+    fin_out.start()
     reduce_vec.total(r.fin_vec)
 
     class VecAll:
@@ -1078,9 +1121,11 @@
     fin_vec = VecAll()
     for j in (2, 3, 1):
         fin_vec.copy(j).start()
-    reduce_qkv.total(r.fin_qkv)
-    fin_qkv = Spread(r.fin_qkv, r.got_qkv, z.row)
-    fin_qkv.start()
+    fin_pair = []
+    for k in range(z.pairs):
+        reduce_pair[k].total(r.fin_pair.at[k])
+        fin_pair.append(Spread(r.fin_pair.at[k], r.got_pair.at[k], z.row))
+        fin_pair[k].start()
 
     my_rows = pl.ds(pl.multiple_of(part * z.row, z.row), z.row)
 
@@ -1092,12 +1137,7 @@
             out[peer(j)] = value
 
     deliver(fin_inner, r.fin_inner, r.got_inner, r.o_inner)
-
-    @pl.when(moves == 1)
-    def _():
-        home_copy().wait_recv()
-
-    r.o_wout[...] = r.got_out[...]
+    deliver(fin_out, r.fin_out, r.got_out, r.o_wout)
     summed = r.fin_vec[0:VECTORS, :]
     for j in (1, 2, 3):
         fin_vec.copy(j).wait_recv()
@@ -1105,30 +1145,29 @@
     r.o_vec[0:VECTORS, :] = pltpu.roll(summed, (128 - part * z.row) % 128, 1)
     r.o_vec[VECTORS:, :] = r.fin_vec[VECTORS:, :]
     reduce_outer_b.total(r.o_outer.at[:, w // 2 :])
-    deliver(fin_qkv, r.fin_qkv, r.got_qkv, r.o_qkv)
+    for k in range(z.pairs):
+        deliver(fin_pair[k], r.fin_pair.at[k], r.got_pair.at[k], r.o_pair.at[k])
 
     for group, size in enumerate(groups):
         rows = r.measure.at[pl.ds(0, size // 512)]
-        copy(rows, rows, 0, (page, part), 2 + group).wait_send()
-
-    @pl.when(moves == 1)
-    def _():
-        hold_copy(hold_page).wait_send()
-        home_copy().wait_send()
-
-    assert counter[0] == z.sems and 2 + len(groups) <= z.groups, (counter, groups)
-
-
-def finish_kernel(z, out, grad, outer, inner, qkv, wout, vec, *outs):
+        copy(rows, rows, 0, (page, part), group).wait_send()
+
+    assert counter[0] == z.sems and len(groups) == z.groups, (counter, groups)
+
+
+def finish_kernel(z, out, grad, outer, inner, pair, wout, vec, *outs):
     (o_out, o_grad, o_wq, o_bq, o_wk, o_wv, o_bv, o_wo, o_bo, o_ga, o_sa, o_wi, o_bi, o_wu, o_bu, o_gf, o_sf) = outs
     o_out[...] = out[...]
     o_grad[...] = grad[...]
     o_wu[...] = outer[...]
-    o_wo[...] = wout[...].astype(F32)
     c = z.cols
     for q in range(z.parts):
+        o_wo[:, q * c : (q + 1) * c] = wout[q].astype(F32)
         for i, ref in enumerate((o_wq, o_wk, o_wv)):
-            ref[:, q * c : (q + 1) * c] = qkv[q, :, i * c : (i + 1) * c].astype(F32)
+            for k in range(z.pairs):
+                ref[:, q * c + k * 128 : q * c + (k + 1) * 128] = pair[
+                    k, q, :, i * 128 : (i + 1) * 128
+                ].astype(F32)
         for g in range(z.pages):
             at = (z.parts * g + q) * z.unit
             o_wi[:, at : at + z.unit] = inner[q, :, g * z.unit : (g + 1) * z.unit].astype(F32)
@@ -1159,35 +1198,42 @@
         o_grad=((n, w), F32),
         o_outer=((z.unit, w), F32),
         o_inner=((z.parts, z.row, z.mine), BF16),
-        o_qkv=((z.parts, z.row, 3 * c), BF16),
-        o_wout=((z.row, w), BF16),
+        o_pair=((z.pairs, z.parts, z.row, 384), BF16),
+        o_wout=((z.parts, z.row, c), BF16),
         o_vec=((SLAB, 128), F32),
     )
     scratch = dict(
         qkv_w=((w, 3 * c), BF16),
+        out_w=((w, c), BF16),
+        cut_out=((z.rows, c), BF16),
         inner_w=((w, z.mine), BF16),
-        out_w=((c, w), BF16),
         outer_w=((z.mine, w), BF16),
         vec_all=((z.pages * SLAB, 128), F32),
         vec_raw=((z.parts * SLAB, 128), F32),
         cut_qkv=((z.rows, 3 * c), BF16),
         cut_inner=((z.rows, z.mine), BF16),
-        own_out=((z.row, w), BF16),
         vecs=((VECTORS, w), F32),
         b_mine=((1, z.mine), F32),
         tok_all=((ln, w), BF16),
         hid_all=((ln, w), BF16),
         gf_all=((ln, w), BF16),
-        ga_all=((ln, w), BF16),
+        ga_cut=((ln, c), BF16),
+        ga_cols=((ln, c), BF16),
+        att_sum=((ln, c), F32),
+        att_cut=((ln, c), BF16),
+        att_got=((ln, c), BF16),
+        ctx_out=((w // 128 * ln, 128), BF16),
+        ctx_in=((4, z.pairs * ln, 128), BF16),
+        ctx_own=((z.pairs * ln, 128), F32),
         qkv=((ln, 3 * c), BF16),
         grad_qkv=((ln, 3 * c), BF16),
         probs=((z.heads, ln, ln), F32),
         measure=((8192, 128), F32),
-        ctx=((ln, c), BF16),
-        grad_ctx=((ln, c), BF16),
+        ctx_all=((w // 128 * ln, 128), BF16),
+        grad_ctx=((z.pairs * ln, 128), BF16),
         grad_kv=((2, ln, 128), F32),
-        part_out=((4, ln, w), BF16),
-        part_in=((4, 4, n, w), BF16),
+        part_out=((3, ln, w), BF16),
+        part_in=((3, 4, n, w), BF16),
         part_own=((n, w), F32),
         norm_one=((n, w), F32),
         inv_one=((n, 1), F32),
@@ -1199,21 +1245,20 @@
         grad_inner=((ln, z.mine), BF16),
         sums=((VECTORS, w), F32),
         b_sum=((1, z.mine), F32),
-        term_out=((c, w), F32),
         term_vec=((z.pages * SLAB, 128), F32),
         slot_outer_a=((1, 2, half, z.unit, w // 2), BF16), stage_outer_a=((1, z.unit, w // 2), BF16),
         slot_outer_b=((1, 2, half, z.unit, w // 2), BF16), stage_outer_b=((1, z.unit, w // 2), BF16),
         slot_inner=((2, 2, half, z.rows, z.mine // 2), BF16), stage_inner=((2, z.rows, z.mine // 2), BF16),
-        slot_qkv=((2, 2, half, z.rows, 3 * c // 2), BF16), stage_qkv=((2, z.rows, 3 * c // 2), BF16),
-        slot_out=((1, 2, half, z.row, w // 1), BF16), stage_out=((1, z.row, w // 1), BF16),
+        slot_pair=((z.pairs, 1, 2, half, z.rows, 384), BF16), stage_pair=((z.pairs, 1, z.rows, 384), BF16),
+        slot_out=((1, 2, half, z.rows, c), BF16), stage_out=((1, z.rows, c), BF16),
         slot_vec=((1, 2, half, SLAB, 128 // 1), F32), stage_vec=((1, SLAB, 128 // 1), F32),
         fin_inner=((z.rows, z.mine), BF16), got_inner=((4, z.row, z.mine), BF16),
-        fin_qkv=((z.rows, 3 * c), BF16), got_qkv=((4, z.row, 3 * c), BF16),
-        fin_out=((z.row, w), BF16), got_out=((z.row, w), BF16),
+        fin_pair=((z.pairs, z.rows, 384), BF16), got_pair=((z.pairs, 4, z.row, 384), BF16),
+        fin_out=((z.rows, c), BF16), got_out=((4, z.row, c), BF16),
         fin_vec=((SLAB, 128), F32), got_vec=((4, SLAB, 128), F32),
     )
-    z.sems = 196
-    z.groups, z.group_bytes = 7, 4 << 20
+    z.sems = 209
+    z.groups, z.group_bytes = 5, 4 << 20
     fetched = dict(w_query=0, w_key=0, w_value=0, w_outer=0, w_out=0, tokens=0, w_inner=0, out_grad=0)
     z.fetched, z.held = tuple(fetched), "f_"
     for name in z.fetched:

time: 165 us -> 160 us (0.970); the launches traced: 164 us -> 160 us
  Pallas kernels: 162 us -> 159 us
    pallas_call x1, Pallas kernels: 159 us -> 156 us  [paged_layer(): pl.pallas_call(functools.partial(layer_kernel, z, names), out_shape=[jax....]
where the time goes in v4:
time: 160 us
  Pallas kernels  159 us (99%)
    pallas_call x1, Pallas kernels, paged_layer(): pl.pallas_call(functools.partial(layer_kernel, z, names), out_shape=[jax....  156 us

profile of v4, /device:TPU:0, one launch (start us, length us, event | category | flops | bytes accessed | tf_op | source)
XLA Modules:
  0.0 160.2 jit_solution(11967415530057705716)
XLA Ops:
  1.3 155.7 %layer.1 = (f32[128,1024]{1,0:T(8,128)}, f32[128,1024]{1,0:T(8,128)}, f32[128,1024]{1,0:T(8,128)}, bf16[4,32,1024]{2,1,0:T(8,128)(2,1)}, bf16[2,4,32,384]{3,2,1,...) custom-call(s32[1]{0:T(128)S(6)} %copy.35.refs_0_, f32[128,1024]{1,0:T(8,128)} %bitcast.22, ...), custom_call_target="tpu_custom_call" | custom-call | tf_op jit(solution)/shard_map/layer/pallas_call | solution.py:1269
  157.0 3.1 %finish.1 = (f32[128,1024]{1,0:T(8,128)}, f32[128,1024]{1,0:T(8,128)}, f32[32,1024]{1,0:T(8,128)}, f32[1,32]{1,0:T(1,128)}, f32[32,1024]{1,0:T(8,128)}, /*index=...) custom-call(f32[128,1024]{1,0:T(8,128)} %get-tuple-element.41.out, ...), custom_call_target="tpu_custom_call" | custom-call | tf_op jit(solution)/shard_map/finish/pallas_call | solution.py:1296

commit v5 on v4

--- a/solution.py
+++ b/solution.py
@@ -373,8 +373,7 @@
         def start(self):
             group = self.group
             if group is None:
-                src = self.args[0]
-                size = math.prod(src.shape) * jnp.dtype(src.dtype).itemsize
+                size = self.size()
                 if groups[-1] + size > z.group_bytes:
                     groups.append(0)
                 groups[-1] += size
@@ -384,6 +383,14 @@
         def wait_recv(self):
             self.made(0).wait_recv()
 
+        def size(self):
+            src = self.args[0]
+            return math.prod(src.shape) * jnp.dtype(src.dtype).itemsize
+
+        def wait_bytes(self, size):
+            rows = r.measure.at[pl.ds(0, size // 512)]
+            Copy(rows, rows, *self.args[2:]).wait_recv()
+
         def wait_send(self):
             self.made(self.group).wait_send()
 
@@ -406,12 +413,13 @@
     class Share:
         def __init__(self, ref, size, pieces=2):
             self.ref, self.size, self.pieces = ref, size, pieces
-            self.first = slots(3 * pieces) - 1
+            self.first = slots(2 + pieces)
 
         def copy(self, j, owner, k):
             height = self.size // self.pieces
             piece = block(self.ref, owner, self.size).at[pl.ds(k * height, height)]
-            return copy(piece, piece, self.first + 3 * k + j, (page, peer(1 if j == 3 else j)))
+            index = self.first + (2 + k if j == 2 else j // 2)
+            return copy(piece, piece, index, (page, peer(1 if j == 3 else j)))
 
         def start(self, k):
             self.copy(2, part, k).start()
@@ -424,15 +432,15 @@
 
 
         def wait(self, j):
-            for k in range(self.pieces):
-                self.copy(j, peer(j), k).wait_recv()
+            arrival = self.copy(j, peer(j), 0)
+            arrival.wait_bytes(self.pieces * arrival.size())
 
     class Combine:
         def __init__(self, refs, size, make, pieces=2):
             self.out, self.got, self.own = refs
             self.size, self.make, self.pieces = size, make, pieces
             self.height = size // pieces
-            self.first = slots(3 * pieces) - 1
+            self.first = slots(2 * pieces)
 
         def rows(self, j, k):
             at = pl.multiple_of(peer(j) * self.size + k * self.height, self.height)
@@ -442,7 +450,7 @@
             return copy(
                 self.out.at[self.rows(j, k)],
                 self.got.at[j, pl.ds(k * self.height, self.height)],
-                self.first + 3 * k + j,
+                self.first + 2 * k + j // 3,
                 (page, peer(2 if j == 2 else 1)),
             )
 
@@ -462,8 +470,8 @@
 
         def finish(self, fn, after=None, step=32):
             for k in range(self.pieces):
-                for j in (1, 2):
-                    self.copy(j, k).wait_recv()
+                arrival = self.copy(1, k)
+                arrival.wait_bytes(2 * arrival.size())
 
                 def body(i, carry):
                     at = pl.multiple_of(k * self.height + i * step, step)
@@ -483,13 +491,13 @@
 
     class Spread:
         def __init__(self, src, dst, size):
-            self.src, self.dst, self.size, self.first = src, dst, size, slots(3) - 1
+            self.src, self.dst, self.size, self.first = src, dst, size, slots(1)
 
         def copy(self, j):
             return copy(
                 block(self.src, peer(j), self.size),
                 self.dst.at[j],
-                self.first + j,
+                self.first,
                 (page, peer(j)),
             )
 
@@ -497,18 +505,19 @@
             for j in (2, 3, 1):
                 self.copy(j).start()
 
-        def wait(self, j):
-            self.copy(j).wait_recv()
+        def wait(self):
+            arrival = self.copy(1)
+            arrival.wait_bytes(3 * arrival.size())
 
     class Place:
         def __init__(self, src, dst, size, base):
-            self.src, self.dst, self.size, self.base, self.first = src, dst, size, base, slots(3) - 1
+            self.src, self.dst, self.size, self.base, self.first = src, dst, size, base, slots(1)
 
         def copy(self, j, owner):
             return copy(
                 block(self.src, peer(j), self.size),
                 block(self.dst, self.base + owner, self.size),
-                self.first + j,
+                self.first,
                 (page, peer(j)),
             )
 
@@ -517,13 +526,13 @@
                 self.copy(j, part).start()
 
         def wait(self):
-            for j in (1, 2, 3):
-                self.copy(j, peer(j)).wait_recv()
+            arrival = self.copy(1, peer(1))
+            arrival.wait_bytes(3 * arrival.size())
 
     class Gather:
         def __init__(self, ref, size, pieces=1):
             self.ref, self.size, self.pieces = ref, size, pieces
-            self.first = slots(2 * z.half * pieces)
+            self.first = slots(z.half * pieces)
 
         def copy(self, t, d, k, step):
             height = self.size // self.pieces
@@ -535,32 +544,32 @@
             return copy(
                 piece,
                 piece,
-                self.first + (t * self.pieces + k) * 2 + d,
+                self.first + t * self.pieces + k,
                 (around(1 - 2 * d), part),
             )
 
-        def wait(self, t, k, d):
-            self.copy(t, d, k, -(1 - 2 * d) * (1 + t)).wait_recv()
-
-        def step(self, t):
-            for k in range(self.pieces):
+        def wait(self, t, k):
+            both = 2 * self.copy(t, 0, k, 0).size()
+            self.copy(t, 0, k, 0).wait_bytes(both)
+
+        def step(self, t, pieces=None):
+            for k in pieces or range(self.pieces):
+                if t > 0:
+                    self.wait(t - 1, k)
                 for d in (0, 1):
-                    if t > 0:
-                        self.wait(t - 1, k, d)
                     self.copy(t, d, k, -(1 - 2 * d) * t).start()
 
 
         def done(self):
             for k in range(self.pieces):
-                for d in (0, 1):
-                    self.wait(z.half - 1, k, d)
+                self.wait(z.half - 1, k)
 
     class Reduce:
         def __init__(self, slot, stage, local, shape, kind, pieces=1):
             self.slot, self.stage, self.local = slot, stage, local
             self.size, self.kind, self.pieces = shape[0], kind, pieces
             self.wide = shape[1] // pieces
-            self.first = slots(2 * z.half * pieces)
+            self.first = slots(z.half * pieces)
 
         def copy(self, t, d, k):
             h = self.size // 2
@@ -573,7 +582,7 @@
             return copy(
                 src,
                 dst,
-                self.first + (t * self.pieces + k) * 2 + d,
+                self.first + t * self.pieces + k,
                 (around(1 - 2 * d), part),
             )
 
@@ -590,10 +599,11 @@
                     self.local(around((1 - 2 * d) * (z.half - t))) for d in (0, 1)
                 ]
             for k in range(self.pieces):
+                if t > 0:
+                    self.wait(t - 1, k)
                 for d in (0, 1):
                     if t > 0:
                         term = terms[d][:, k * wide : (k + 1) * wide]
-                        self.copy(t - 1, d, k).wait_recv()
                         held = self.slot.at[k, d, t - 1]
                         if t == 1:
                             near, far = pl.ds(d * h, h), pl.ds((1 - d) * h, h)
@@ -605,12 +615,15 @@
                             held[...] = (held[...].astype(F32) + term).astype(self.kind)
                     self.copy(t, d, k).start()
 
+        def wait(self, t, k):
+            arrival = self.copy(t, 0, k)
+            arrival.wait_bytes(2 * arrival.size())
+
         def total(self, out):
             term = self.local(page)
             last = z.half - 1
             for k in range(self.pieces):
-                for d in (0, 1):
-                    self.copy(last, d, k).wait_recv()
+                self.wait(last, k)
                 at = slice(k * self.wide, (k + 1) * self.wide)
                 out[:, at] = (
                     term[:, at] + self.slot[k, 0, last].astype(F32) + self.slot[k, 1, last].astype(F32)
@@ -667,11 +680,11 @@
     share_tok = Share(r.tok_all, n)
 
     class ShareVec:
-        first = slots(3) - 1
+        first = slots(1)
 
         def copy(self, j, owner):
             piece = block(r.vec_raw, owner, SLAB).at[pl.ds(0, VECTORS)]
-            return copy(piece, piece, self.first + j, (page, peer(j)))
+            return copy(piece, piece, self.first, (page, peer(j)))
 
     vec_share = ShareVec()
     pl.semaphore_wait(barrier, 5)
@@ -703,8 +716,8 @@
 
     cut_qkv.wait()
     ring_qkv.step(0)
-    for j in (1, 2, 3):
-        vec_share.copy(j, peer(j)).wait_recv()
+    arrival = vec_share.copy(1, peer(1))
+    arrival.wait_bytes(3 * arrival.size())
     lane = lax.broadcasted_iota(jnp.int32, (VECTORS, 128), 1)
     total = jnp.zeros((VECTORS, 128), F32)
     for q in range(z.parts):
@@ -799,6 +812,7 @@
         attend(pair)
         share_ctx.start(pair)
     ring_inner.step(2)
+    ring_outer.step(2, (0,))
 
     def project(j):
         term = None
@@ -840,6 +854,7 @@
         r.hid_all[pl.ds(pl.multiple_of(part * n + at, 32), 32), :] = hidden.astype(BF16)
 
     ring_inner.step(3)
+    ring_outer.step(2, (1,))
     move_att.wait()
     for k in range(2):
 
@@ -857,7 +872,6 @@
 
         lax.fori_loop(0, n // 64, norm_rows, 0)
         share_hid.start(k)
-    ring_outer.step(2)
     ring_inner.done()
 
     tile = 256
@@ -894,7 +908,7 @@
     def second_norm(rows, at, total):
         outer = total + vector(5)
         normed, inverse = norm_parts(r.hidden[rows, :] + outer)
-        r.o_out[rows, :] = normed * vector(6) + vector(7)
+        r.v_out[rows, :] = normed * vector(6) + vector(7)
         grad = r.out_grad[rows, :]
         add_column_sum(6, grad * normed)
         add_column_sum(7, grad)
@@ -905,6 +919,11 @@
         r.gf_all[pl.ds(pl.multiple_of(part * n + at, 32), 32), :] = low
 
     combine_two.finish(second_norm, share_gf.start)
+
+    def leave_early(i, src, dst):
+        return pltpu.make_async_copy(src, dst, load_sem.at[len(z.fetched) + i])
+
+    leave_early(0, r.v_out, r.o_out).start()
 
     def chunk_term(left, right, size):
         def local(g):
@@ -1084,9 +1103,9 @@
     combine_four = Combine(token_refs(2), n, lambda rows, j: dot_nt(r.grad_qkv[rows, :], r.qkv_w[...]))
     combine_four.term(3)
     combine_four.term(2)
-    reduce_vec.step(1)
     for pair in range(z.pairs):
         reduce_pair[pair].step(1)
+    reduce_vec.step(1)
     reduce_out.step(3)
     combine_four.term(1)
     combine_four.term(0)
@@ -1094,53 +1113,54 @@
     reduce_inner.total(r.fin_inner)
     fin_inner = Spread(r.fin_inner, r.got_inner, z.row)
     fin_inner.start()
-    reduce_vec.step(2)
     for pair in range(z.pairs):
         reduce_pair[pair].step(2)
+    reduce_vec.step(2)
 
     def input_rows(rows, at, total):
-        r.o_grad[rows, :] = r.grad_mixed[rows, :] + total
+        r.v_grad[rows, :] = r.grad_mixed[rows, :] + total
 
     combine_four.finish(input_rows)
+    leave_early(1, r.v_grad, r.o_grad).start()
     reduce_outer_a.total(r.o_outer.at[:, 0 : w // 2])
-    reduce_vec.step(3)
     for pair in range(z.pairs):
         reduce_pair[pair].step(3)
+    reduce_vec.step(3)
     reduce_outer_b.step(3)
     reduce_out.total(r.fin_out)
     fin_out = Spread(r.fin_out, r.got_out, z.row)
     fin_out.start()
-    reduce_vec.total(r.fin_vec)
-
-    class VecAll:
-        first = slots(3) - 1
-
-        def copy(self, j):
-            return copy(r.fin_vec, r.got_vec.at[j], self.first + j, (page, peer(j)))
-
-    fin_vec = VecAll()
-    for j in (2, 3, 1):
-        fin_vec.copy(j).start()
     fin_pair = []
     for k in range(z.pairs):
         reduce_pair[k].total(r.fin_pair.at[k])
         fin_pair.append(Spread(r.fin_pair.at[k], r.got_pair.at[k], z.row))
         fin_pair[k].start()
+    reduce_vec.total(r.fin_vec)
+
+    class VecAll:
+        first = slots(1)
+
+        def copy(self, j):
+            return copy(r.fin_vec, r.got_vec.at[j], self.first, (page, peer(j)))
+
+    fin_vec = VecAll()
+    for j in (2, 3, 1):
+        fin_vec.copy(j).start()
 
     my_rows = pl.ds(pl.multiple_of(part * z.row, z.row), z.row)
 
     def deliver(spread, mine, got, out):
+        spread.wait()
         for j in range(4):
-            if j:
-                spread.wait(j)
             value = got[j] if j else mine[my_rows, :]
             out[peer(j)] = value
 
     deliver(fin_inner, r.fin_inner, r.got_inner, r.o_inner)
     deliver(fin_out, r.fin_out, r.got_out, r.o_wout)
+    arrival = fin_vec.copy(1)
+    arrival.wait_bytes(3 * arrival.size())
     summed = r.fin_vec[0:VECTORS, :]
     for j in (1, 2, 3):
-        fin_vec.copy(j).wait_recv()
         summed = summed + r.got_vec[j, 0:VECTORS, :]
     r.o_vec[0:VECTORS, :] = pltpu.roll(summed, (128 - part * z.row) % 128, 1)
     r.o_vec[VECTORS:, :] = r.fin_vec[VECTORS:, :]
@@ -1148,6 +1168,8 @@
     for k in range(z.pairs):
         deliver(fin_pair[k], r.fin_pair.at[k], r.got_pair.at[k], r.o_pair.at[k])
 
+    leave_early(0, r.v_out, r.o_out).wait()
+    leave_early(1, r.v_grad, r.o_grad).wait()
     for group, size in enumerate(groups):
         rows = r.measure.at[pl.ds(0, size // 512)]
         copy(rows, rows, 0, (page, part), group).wait_send()
@@ -1236,6 +1258,8 @@
         part_in=((3, 4, n, w), BF16),
         part_own=((n, w), F32),
         norm_one=((n, w), F32),
+        v_out=((n, w), F32),
+        v_grad=((n, w), F32),
         inv_one=((n, 1), F32),
         hidden=((n, w), F32),
         grad_sum=((n, w), F32),
@@ -1257,13 +1281,13 @@
         fin_out=((z.rows, c), BF16), got_out=((4, z.row, c), BF16),
         fin_vec=((SLAB, 128), F32), got_vec=((4, SLAB, 128), F32),
     )
-    z.sems = 209
+    z.sems = 107
     z.groups, z.group_bytes = 5, 4 << 20
     fetched = dict(w_query=0, w_key=0, w_value=0, w_outer=0, w_out=0, tokens=0, w_inner=0, out_grad=0)
     z.fetched, z.held = tuple(fetched), "f_"
     for name in z.fetched:
         scratch[z.held + name] = (ins[name].shape, F32)
-    sems = [pltpu.SemaphoreType.DMA((z.groups,)), pltpu.SemaphoreType.DMA((z.sems,)), pltpu.SemaphoreType.DMA((len(fetched),))]
+    sems = [pltpu.SemaphoreType.DMA((z.groups,)), pltpu.SemaphoreType.DMA((z.sems,)), pltpu.SemaphoreType.DMA((len(fetched) + 2,))]
     names = list(ins) + list(outs) + list(scratch) + list(dict(send_sem=0, recv_sem=0, load_sem=0))
     vmem = pl.BlockSpec(memory_space=pltpu.VMEM)
     parts = pl.pallas_call(
@@ -1277,7 +1301,7 @@
             else vmem
             for k, v in ins.items()
         ],
-        out_specs=[vmem] * len(outs),
+        out_specs=[pl.BlockSpec(memory_space=pl.ANY)] * 2 + [vmem] * (len(outs) - 2),
         scratch_shapes=[pltpu.VMEM(*v) for v in scratch.values()]
         + sems,
         compiler_params=pltpu.CompilerParams(

time: 160 us -> 157 us (0.981)
  Pallas kernels: 159 us -> 155 us
    pallas_call x1, Pallas kernels: 156 us -> 152 us  [paged_layer(): pl.pallas_call(functools.partial(layer_kernel, z, names), out_shape=[jax....]
where the time goes in v5:
time: 157 us
  Pallas kernels  155 us (99%)
    pallas_call x1, Pallas kernels, paged_layer(): pl.pallas_call(functools.partial(layer_kernel, z, names), out_shape=[jax....  152 us

profile of v5, /device:TPU:0, one launch (start us, length us, event | category | flops | bytes accessed | tf_op | source)
XLA Modules:
  0.0 156.9 jit_solution(8516894238203832513)
XLA Ops:
  1.3 152.3 %layer.1 = (f32[128,1024]{1,0:T(8,128)}, f32[128,1024]{1,0:T(8,128)}, f32[128,1024]{1,0:T(8,128)}, bf16[4,32,1024]{2,1,0:T(8,128)(2,1)}, bf16[2,4,32,384]{3,2,1,...) custom-call(s32[1]{0:T(128)S(6)} %copy.35.refs_0_, f32[128,1024]{1,0:T(8,128)} %bitcast.22, ...), custom_call_target="tpu_custom_call" | custom-call | tf_op jit(solution)/shard_map/layer/pallas_call | solution.py:1293
  153.6 3.1 %finish.1 = (f32[128,1024]{1,0:T(8,128)}, f32[128,1024]{1,0:T(8,128)}, f32[32,1024]{1,0:T(8,128)}, f32[1,32]{1,0:T(1,128)}, f32[32,1024]{1,0:T(8,128)}, /*index=...) custom-call(f32[128,1024]{1,0:T(8,128)} %get-tuple-element.41.out, ...), custom_call_target="tpu_custom_call" | custom-call | tf_op jit(solution)/shard_map/finish/pallas_call | solution.py:1320

commit v6 on v5

--- a/solution.py
+++ b/solution.py
@@ -657,6 +657,7 @@
                 r.cut_qkv[rows, (3 * k + i) * 128 : (3 * k + i + 1) * 128] = weight[
                     :, q * c + k * 128 : q * c + (k + 1) * 128
                 ].astype(BF16)
+    arrive(9)
     mine = pl.multiple_of(part * SLAB, SLAB)
     for i, small in enumerate(
         (r.b_query, r.b_value, r.b_out, r.g_attn, r.s_attn, r.b_outer, r.g_final, r.s_final)
@@ -776,6 +777,7 @@
     scale = HEAD_DIM ** (-0.5)
     first_head = lax.broadcasted_iota(jnp.int32, (n, 128), 1) < HEAD_DIM
     key_place = lax.broadcasted_iota(jnp.int32, (n, z.length), 1)
+    pltpu.make_async_copy(hbm.valid, r.valid, load_sem.at[len(z.fetched) - 1]).wait()
     valid = r.valid[0]
 
     def pair_cols(kind, pair):
@@ -996,8 +998,8 @@
     reduce_outer_a.step(1)
     combine_three.term(1)
     combine_three.term(0)
+    reduce_inner.step(1)
     reduce_outer_b.step(1)
-    reduce_inner.step(1)
 
     move_ga = Place(r.ga_cut, r.ga_cols, n, 0)
 
@@ -1084,7 +1086,6 @@
 
     combine_ctx.finish(keep_grad_ctx, after_pair, step=128)
     reduce_inner.step(3)
-    reduce_out.step(2)
 
     for k in range(z.pairs):
         mine = pl.ds(pl.multiple_of(part * c + k * 128, 128), 128)
@@ -1106,7 +1107,7 @@
     for pair in range(z.pairs):
         reduce_pair[pair].step(1)
     reduce_vec.step(1)
-    reduce_out.step(3)
+    reduce_out.step(2)
     combine_four.term(1)
     combine_four.term(0)
 
@@ -1116,17 +1117,18 @@
     for pair in range(z.pairs):
         reduce_pair[pair].step(2)
     reduce_vec.step(2)
+    reduce_out.step(3)
 
     def input_rows(rows, at, total):
         r.v_grad[rows, :] = r.grad_mixed[rows, :] + total
 
-    combine_four.finish(input_rows)
-    leave_early(1, r.v_grad, r.o_grad).start()
     reduce_outer_a.total(r.o_outer.at[:, 0 : w // 2])
     for pair in range(z.pairs):
         reduce_pair[pair].step(3)
     reduce_vec.step(3)
     reduce_outer_b.step(3)
+    combine_four.finish(input_rows)
+    leave_early(1, r.v_grad, r.o_grad).start()
     reduce_out.total(r.fin_out)
     fin_out = Spread(r.fin_out, r.got_out, z.row)
     fin_out.start()
@@ -1283,26 +1285,28 @@
     )
     z.sems = 107
     z.groups, z.group_bytes = 5, 4 << 20
-    fetched = dict(w_query=0, w_key=0, w_value=0, w_outer=0, w_out=0, tokens=0, w_inner=0, out_grad=0)
+    fetched = dict(
+        w_query=0, w_key=0, w_value=0, b_query=0, b_value=0, b_out=0, g_attn=0, s_attn=0, b_outer=0,
+        g_final=0, s_final=0, b_inner=0, w_outer=0, w_out=0, tokens=0, w_inner=0, out_grad=0, valid=0)
     z.fetched, z.held = tuple(fetched), "f_"
     for name in z.fetched:
-        scratch[z.held + name] = (ins[name].shape, F32)
-    sems = [pltpu.SemaphoreType.DMA((z.groups,)), pltpu.SemaphoreType.DMA((z.sems,)), pltpu.SemaphoreType.DMA((len(fetched) + 2,))]
+        scratch[z.held + name] = (ins[name].shape, ins[name].dtype)
+    sems = [pltpu.SemaphoreType.DMA((v,)) for v in (z.groups, z.sems, len(fetched) + 2)]
     names = list(ins) + list(outs) + list(scratch) + list(dict(send_sem=0, recv_sem=0, load_sem=0))
     vmem = pl.BlockSpec(memory_space=pltpu.VMEM)
     parts = pl.pallas_call(
         functools.partial(layer_kernel, z, names),
         out_shape=[jax.ShapeDtypeStruct(*v) for v in outs.values()],
         in_specs=[
-            pl.BlockSpec(memory_space=pltpu.SMEM)
-            if v is valid_len
-            else pl.BlockSpec(memory_space=pl.ANY)
+            pl.BlockSpec(memory_space=pl.ANY)
             if k in fetched
             else vmem
             for k, v in ins.items()
         ],
         out_specs=[pl.BlockSpec(memory_space=pl.ANY)] * 2 + [vmem] * (len(outs) - 2),
-        scratch_shapes=[pltpu.VMEM(*v) for v in scratch.values()]
+        scratch_shapes=[
+            (pltpu.SMEM if v[1] == jnp.int32 else pltpu.VMEM)(*v) for v in scratch.values()
+        ]
         + sems,
         compiler_params=pltpu.CompilerParams(
             collective_id=0, has_side_effects=True, vmem_limit_bytes=67043328
@@ -1317,11 +1321,28 @@
         jax.ShapeDtypeStruct((row, z.units), F32), jax.ShapeDtypeStruct((1, z.unit), F32),
         jax.ShapeDtypeStruct((z.unit, w), F32), vec, vec, vec,
     ]
+    steps = 2
+
+    def rows_of(rows, width):
+        return pl.BlockSpec((rows // steps, width), lambda i: (i, 0))
+
     results = pl.pallas_call(
         functools.partial(finish_kernel, z),
         out_shape=shapes,
-        in_specs=[vmem] * 7,
-        out_specs=[vmem] * len(shapes),
+        grid=(steps,),
+        in_specs=[
+            rows_of(n, w), rows_of(n, w), rows_of(z.unit, w),
+            pl.BlockSpec((z.parts, row // steps, z.mine), lambda i: (0, i, 0)),
+            pl.BlockSpec((z.pairs, z.parts, row // steps, 384), lambda i: (0, 0, i, 0)),
+            pl.BlockSpec((z.parts, row // steps, c), lambda i: (0, i, 0)),
+            pl.BlockSpec((SLAB, 128), lambda i: (0, 0)),
+        ],
+        out_specs=[
+            rows_of(v.shape[0], v.shape[1])
+            if v.shape[0] > 1
+            else pl.BlockSpec(v.shape, lambda i: (0, 0))
+            for v in shapes
+        ],
         name="finish",
     )(*parts)
     results = list(results)

time: 157 us -> 156 us (level)
  no operation moved by 1% of the time
where the time goes in v6:
time: 156 us
  Pallas kernels  154 us (99%)
    pallas_call x1, Pallas kernels, paged_layer(): pl.pallas_call(functools.partial(layer_kernel, z, names), out_shape=[jax....  151 us

profile of v6, /device:TPU:0, one launch (start us, length us, event | category | flops | bytes accessed | tf_op | source)
XLA Modules:
  0.0 155.7 jit_solution(18109155700752354453)
XLA Ops:
  1.3 151.4 %layer.1 = (f32[128,1024]{1,0:T(8,128)}, f32[128,1024]{1,0:T(8,128)}, f32[128,1024]{1,0:T(8,128)}, bf16[4,32,1024]{2,1,0:T(8,128)(2,1)}, bf16[2,4,32,384]{3,2,1,...) custom-call(s32[1]{0:T(128)S(6)} %copy.35.refs_0_, f32[128,1024]{1,0:T(8,128)} %bitcast.22, ...), custom_call_target="tpu_custom_call" | custom-call | tf_op jit(solution)/shard_map/layer/pallas_call | solution.py:1297
  152.7 2.8 %finish.1 = (f32[128,1024]{1,0:T(8,128)}, f32[128,1024]{1,0:T(8,128)}, f32[32,1024]{1,0:T(8,128)}, f32[1,32]{1,0:T(1,128)}, f32[32,1024]{1,0:T(8,128)}, /*index=...) custom-call(f32[128,1024]{1,0:T(8,128)} %get-tuple-element.41.out, ...), custom_call_target="tpu_custom_call" | custom-call | tf_op jit(solution)/shard_map/finish/pallas_call | solution.py:1329

commit v7 on v6

--- a/solution.py
+++ b/solution.py
@@ -876,10 +876,11 @@
         share_hid.start(k)
     ring_inner.done()
 
-    tile = 256
+    tile = 512
 
     def make_inner(j):
-        rows = pl.ds(pl.multiple_of(peer(j) * n, n), n)
+        chip = (part // 2 + j) % 2
+        rows = pl.ds(pl.multiple_of(chip * 2 * n, 2 * n), 2 * n)
 
         def columns(i, carry):
             cols = pl.ds(pl.multiple_of(i * tile, tile), tile)
@@ -891,19 +892,17 @@
 
         lax.fori_loop(0, z.mine // tile, columns, 0)
 
+    share_hid.wait(1)
     make_inner(0)
-    share_hid.wait(1)
-    make_inner(1)
     ring_outer.step(3)
     share_hid.forward()
-    make_inner(2)
     share_hid.wait(3)
-    make_inner(3)
+    make_inner(1)
     ring_outer.done()
-    combine_two = Combine(token_refs(0), n, lambda rows, j: dot_nn(r.active[rows, :], r.outer_w[...]))
+    combine_two = Combine(token_refs(0), n, lambda rows, j: dot_nn(r.active[rows, :], r.outer_w[...]), 4)
     for j in (3, 2, 1, 0):
         combine_two.term(j)
-    share_gf = Share(r.gf_all, n)
+    share_gf = Share(r.gf_all, n, 4)
 
     arrive(1)
 
@@ -958,7 +957,7 @@
         return dot_tn(r.ctx_all[rows, :], r.ga_cols[...])
 
     reduce_pair = [
-        Reduce(r.slot_pair.at[k], r.stage_pair.at[k], pair_term(k), (z.rows, 384), BF16)
+        Reduce(r.slot_pair.at[k], r.stage_pair.at[k], pair_term(k), (z.rows, 384), BF16, 3)
         for k in range(z.pairs)
     ]
     reduce_out = Reduce(r.slot_out, r.stage_out, out_term, (z.rows, c), BF16)
@@ -970,7 +969,8 @@
     r.b_sum[...] = jnp.zeros_like(r.b_sum)
 
     def make_grad_inner(j):
-        rows = pl.ds(pl.multiple_of(peer(j) * n, n), n)
+        chip = (part // 2 + j) % 2
+        rows = pl.ds(pl.multiple_of(chip * 2 * n, 2 * n), 2 * n)
 
         def columns(i, carry):
             cols = pl.ds(pl.multiple_of(i * tile, tile), tile)
@@ -982,15 +982,13 @@
 
         lax.fori_loop(0, z.mine // tile, columns, 0)
 
+    share_gf.wait(1)
     make_grad_inner(0)
-    share_gf.wait(1)
-    make_grad_inner(1)
     share_gf.forward()
-    make_grad_inner(2)
     share_gf.wait(3)
     reduce_outer_a.step(0)
     reduce_outer_b.step(0)
-    make_grad_inner(3)
+    make_grad_inner(1)
     combine_three = Combine(token_refs(1), n, lambda rows, j: dot_nt(r.grad_inner[rows, :], r.inner_w[...]))
     combine_three.term(3)
     combine_three.term(2)
@@ -1275,7 +1273,7 @@
         slot_outer_a=((1, 2, half, z.unit, w // 2), BF16), stage_outer_a=((1, z.unit, w // 2), BF16),
         slot_outer_b=((1, 2, half, z.unit, w // 2), BF16), stage_outer_b=((1, z.unit, w // 2), BF16),
         slot_inner=((2, 2, half, z.rows, z.mine // 2), BF16), stage_inner=((2, z.rows, z.mine // 2), BF16),
-        slot_pair=((z.pairs, 1, 2, half, z.rows, 384), BF16), stage_pair=((z.pairs, 1, z.rows, 384), BF16),
+        slot_pair=((z.pairs, 3, 2, half, z.rows, 128), BF16), stage_pair=((z.pairs, 3, z.rows, 128), BF16),
         slot_out=((1, 2, half, z.rows, c), BF16), stage_out=((1, z.rows, c), BF16),
         slot_vec=((1, 2, half, SLAB, 128 // 1), F32), stage_vec=((1, SLAB, 128 // 1), F32),
         fin_inner=((z.rows, z.mine), BF16), got_inner=((4, z.row, z.mine), BF16),
@@ -1283,7 +1281,7 @@
         fin_out=((z.rows, c), BF16), got_out=((4, z.row, c), BF16),
         fin_vec=((SLAB, 128), F32), got_vec=((4, SLAB, 128), F32),
     )
-    z.sems = 107
+    z.sems = 129
     z.groups, z.group_bytes = 5, 4 << 20
     fetched = dict(
         w_query=0, w_key=0, w_value=0, b_query=0, b_value=0, b_out=0, g_attn=0, s_attn=0, b_outer=0,

time: 156 us -> 154 us (0.987)
  Pallas kernels: 154 us -> 152 us
    pallas_call x1, Pallas kernels: 151 us -> 149 us  [paged_layer(): pl.pallas_call(functools.partial(layer_kernel, z, names), out_shape=[jax....]
where the time goes in v7:
time: 154 us; the launch traced here: 153 us
  Pallas kernels  152 us (99%)
    pallas_call x1, Pallas kernels, paged_layer(): pl.pallas_call(functools.partial(layer_kernel, z, names), out_shape=[jax....  149 us

profile of v7, /device:TPU:0, one launch (start us, length us, event | category | flops | bytes accessed | tf_op | source)
XLA Modules:
  0.0 153.5 jit_solution(14919325806904184983)
XLA Ops:
  1.3 149.2 %layer.1 = (f32[128,1024]{1,0:T(8,128)}, f32[128,1024]{1,0:T(8,128)}, f32[128,1024]{1,0:T(8,128)}, bf16[4,32,1024]{2,1,0:T(8,128)(2,1)}, bf16[2,4,32,384]{3,2,1,...) custom-call(s32[1]{0:T(128)S(6)} %copy.35.refs_0_, f32[128,1024]{1,0:T(8,128)} %bitcast.22, ...), custom_call_target="tpu_custom_call" | custom-call | tf_op jit(solution)/shard_map/layer/pallas_call | solution.py:1295
  150.5 2.8 %finish.1 = (f32[128,1024]{1,0:T(8,128)}, f32[128,1024]{1,0:T(8,128)}, f32[32,1024]{1,0:T(8,128)}, f32[1,32]{1,0:T(1,128)}, f32[32,1024]{1,0:T(8,128)}, /*index=...) custom-call(f32[128,1024]{1,0:T(8,128)} %get-tuple-element.41.out, ...), custom_call_target="tpu_custom_call" | custom-call | tf_op jit(solution)/shard_map/finish/pallas_call | solution.py:1327

commit v8 on v7

--- a/solution.py
+++ b/solution.py
@@ -436,7 +436,8 @@
             arrival.wait_bytes(self.pieces * arrival.size())
 
     class Combine:
-        def __init__(self, refs, size, make, pieces=2):
+        def __init__(self, refs, size, make, pieces=2, wide=None):
+            self.wide = wide
             self.out, self.got, self.own = refs
             self.size, self.make, self.pieces = size, make, pieces
             self.height = size // pieces
@@ -455,7 +456,16 @@
             )
 
         def term(self, j):
-            value = self.make(pl.ds(pl.multiple_of(peer(j) * self.size, self.size), self.size), j)
+            if self.wide is None:
+                at = pl.multiple_of(peer(j) * self.size, self.size)
+                value = self.make(pl.ds(at, self.size), j)
+            else:
+                if j in (1, 3):
+                    chip = (part // 2 + j // 2) % 2
+                    at = pl.multiple_of(chip * 2 * self.size, 2 * self.size)
+                    self.wide[...] = self.make(pl.ds(at, 2 * self.size), j)
+                at = pl.multiple_of((peer(j) % 2) * self.size, self.size)
+                value = self.wide[pl.ds(at, self.size), :]
             if j == 0:
                 self.own[...] = value
                 return
@@ -899,7 +909,7 @@
     share_hid.wait(3)
     make_inner(1)
     ring_outer.done()
-    combine_two = Combine(token_refs(0), n, lambda rows, j: dot_nn(r.active[rows, :], r.outer_w[...]), 4)
+    combine_two = Combine(token_refs(0), n, lambda rows, j: dot_nn(r.active[rows, :], r.outer_w[...]), 4, r.wide)
     for j in (3, 2, 1, 0):
         combine_two.term(j)
     share_gf = Share(r.gf_all, n, 4)
@@ -989,7 +999,9 @@
     reduce_outer_a.step(0)
     reduce_outer_b.step(0)
     make_grad_inner(1)
-    combine_three = Combine(token_refs(1), n, lambda rows, j: dot_nt(r.grad_inner[rows, :], r.inner_w[...]))
+    combine_three = Combine(
+        token_refs(1), n, lambda rows, j: dot_nt(r.grad_inner[rows, :], r.inner_w[...]), wide=r.wide
+    )
     combine_three.term(3)
     combine_three.term(2)
     reduce_inner.step(0)
@@ -1257,6 +1269,7 @@
         part_out=((3, ln, w), BF16),
         part_in=((3, 4, n, w), BF16),
         part_own=((n, w), F32),
+        wide=((2 * n, w), F32),
         norm_one=((n, w), F32),
         v_out=((n, w), F32),
         v_grad=((n, w), F32),

time: 154 us -> 153 us (level)
  no operation moved by 1% of the time
where the time goes in v8:
time: 153 us
  Pallas kernels  152 us (99%)
    pallas_call x1, Pallas kernels, paged_layer(): pl.pallas_call(functools.partial(layer_kernel, z, names), out_shape=[jax....  149 us

profile of v8, /device:TPU:0, one launch (start us, length us, event | category | flops | bytes accessed | tf_op | source)
XLA Modules:
  0.0 153.1 jit_solution(11653360796685622249)
XLA Ops:
  1.3 148.8 %layer.1 = (f32[128,1024]{1,0:T(8,128)}, f32[128,1024]{1,0:T(8,128)}, f32[128,1024]{1,0:T(8,128)}, bf16[4,32,1024]{2,1,0:T(8,128)(2,1)}, bf16[2,4,32,384]{3,2,1,...) custom-call(s32[1]{0:T(128)S(6)} %copy.35.refs_0_, f32[128,1024]{1,0:T(8,128)} %bitcast.22, ...), custom_call_target="tpu_custom_call" | custom-call | tf_op jit(solution)/shard_map/layer/pallas_call | solution.py:1308
  150.1 2.8 %finish.1 = (f32[128,1024]{1,0:T(8,128)}, f32[128,1024]{1,0:T(8,128)}, f32[32,1024]{1,0:T(8,128)}, f32[1,32]{1,0:T(1,128)}, f32[32,1024]{1,0:T(8,128)}, /*index=...) custom-call(f32[128,1024]{1,0:T(8,128)} %get-tuple-element.41.out, ...), custom_call_target="tpu_custom_call" | custom-call | tf_op jit(solution)/shard_map/finish/pallas_call | solution.py:1340
